TPU v7x, 32 devices: a whole 2x2x4 slice. The times are simulated.
32 devices in a mesh: dp: 8 (over z, x), seq: 4 (over y, core).
Axes of the slice: x: 2, y: 2, z: 4, core: 2. Of those that a mesh axis runs over, the one named last changes fastest.
Arguments:
- tokens: bfloat16 [8, 1024, 768], P('dp', 'seq'), may hold values from -6 to 6
- segment_ids: int32 [8, 1024], P('dp'), may hold values from 0 to 5, never falling along the last dimension, each value on 1 to 512 neighbouring positions
- pad_lengths: int32 [8], P('dp'), may hold values from 0 to 511
- threshold: float32 [1], replicated, may hold values from 0.05 to 2
- gains: float32 [2, 768], replicated, may hold values from 0.5 to 1.5
- gain_first: float32 [2, 768], replicated, may hold values from -256 to 256
- gain_second: float32 [2, 768], replicated, may hold values from 2048 to 8192
- slot_tiles: int32 [448], replicated, may hold values from 0 to 447, as said below
- weight_slots: float32 [448, 128, 128], P(('dp', 'seq')), may hold values from -2 to 2
- first_moment: float32 [448, 128, 128], P(('dp', 'seq')), may hold values from -160 to 160
- second_moment: float32 [448, 128, 128], P(('dp', 'seq')), may hold values from 819.2 to 3276.8
- basis_left: float32 [448, 128, 128], P(('dp', 'seq')), may hold values from -1 to 1, as said below
- basis_right: float32 [448, 128, 128], P(('dp', 'seq')), may hold values from -1 to 1, as said below
- out_grad: bfloat16 [8, 1024, 768], P('dp', 'seq'), may hold values from -6 to 6
Outputs:
- output: bfloat16 [8, 1024, 768], P('dp', 'seq')
- input_grad: float32 [8, 1024, 768], P('dp', 'seq')
- fraction: float32 [8], P('dp')
- moment_first: float32 [448, 128, 128], P(('dp', 'seq'))
- moment_second: float32 [448, 128, 128], P(('dp', 'seq'))
- new_weights: float32 [448, 128, 128], P(('dp', 'seq'))
- gain_update: float32 [2, 768], replicated
- gain_moment: float32 [2, 768], replicated
- gain_square: float32 [2, 768], replicated
Inputs may be any that keep to these rules, and one draw needn't show every extreme that they name: `segment_ids`: segment numbers never fall along a row; each segment has 1 to 512 positions, one exactly that many. `slot_tiles`: a permutation of the slot numbers; a slot whose entry is 432 or more holds no tile. `basis_left`: each slot's matrix is orthogonal. `basis_right`: each slot's matrix is orthogonal.
All inputs are finite; a program needn't handle non-finite values.
Results may differ from a plain program's by a relative error of at most 0.011.
Values may be sent and summed in bfloat16 or wider, within the bound.
No kernel may reach another device: no remote copies, remote signals or barrier semaphores. Data moves between devices by JAX's collectives and lax.ppermute only.
A program may use at most 192 MiB of HBM per device.

v0:
```python
import jax
import jax.numpy as jnp
from jax import lax
from jax.sharding import PartitionSpec as P

H = 12
HD = 64
FF = 3072
STEP = 3


select_scale = 0.2
fraction_slope = 2.0
first_decay = 0.5
second_decay = 0.5
adam_epsilon = 1e-08
weight_rate = 0.05
gain_rate = 0.2
decay_rate = 0.1
norm_epsilon = 1e-05
precise = lax.Precision.HIGHEST


def carried_in(value, axis, join, neutral, backward):
    count, mine = (lax.axis_size(axis), lax.axis_index(axis))
    pieces = lax.all_gather(value, axis)
    if backward:
        pieces = pieces[::-1]
        mine = count - 1 - mine
    total = jnp.full_like(value, 0) + jnp.asarray(neutral, value.dtype)

    def step(position, total):
        longer = join(total, pieces[position])
        return jnp.where(position < mine, longer, total)

    return lax.fori_loop(0, count - 1, step, total)


def layer_norm(values, gain):
    centred = values - jnp.mean(values, axis=-1, keepdims=True)
    spread = jnp.mean(centred * centred, axis=-1, keepdims=True)
    return centred * lax.rsqrt(spread + norm_epsilon) * gain


def gelu_local(values):
    return jax.nn.gelu(values, approximate=True)


def tiles_of(matrix, tile_side):
    height, across = matrix.shape
    shaped = matrix.reshape(height // tile_side, tile_side, across // tile_side, tile_side)
    return shaped.transpose(0, 2, 1, 3).reshape(-1, tile_side, tile_side)


def matrix_of(tile_stack, height, across):
    tile_side = tile_stack.shape[-1]
    shaped = tile_stack.reshape(height // tile_side, across // tile_side, tile_side, tile_side)
    return shaped.transpose(0, 2, 1, 3).reshape(height, across)


def split_tiles(tile_stack, width, hidden_width):
    tile_side = tile_stack.shape[-1]
    shapes = [(width, 3 * width), (width, width), (width, hidden_width), (hidden_width, width)]
    result = []
    offset = 0
    for height, across in shapes:
        count_here = height * across // (tile_side * tile_side)
        result.append(matrix_of(tile_stack[offset : offset + count_here], height, across))
        offset = offset + count_here
    return result


def slot_buffer(grads, slot_tiles, tile_side, tile_count):
    stacked = jnp.concatenate(
        [tiles_of(grad, tile_side) for grad in grads]
        + [jnp.zeros((1, tile_side, tile_side), jnp.float32)],
        axis=0,
    )
    return stacked[jnp.minimum(slot_tiles, tile_count)]


def add_single(earlier, later):
    return earlier + later


def rotated_adam(grad_slots, first, second, left, right, weight, correction):
    turned = jnp.einsum("sji,sjk->sik", left, grad_slots, precision=precise)
    turned = jnp.einsum("sik,skl->sil", turned, right, precision=precise)
    first_new = first_decay * first + (1.0 - first_decay) * turned
    second_new = second_decay * second + (1.0 - second_decay) * turned * turned
    norm_step = first_new / correction / (jnp.sqrt(second_new / correction) + adam_epsilon)
    back = jnp.einsum("sik,skl->sil", left, norm_step, precision=precise)
    back = jnp.einsum("sil,sjl->sij", back, right, precision=precise)
    return (first_new, second_new, weight - weight_rate * back - weight_rate * decay_rate * weight)


def local(
    tokens,
    segment_ids,
    pad_lengths,
    threshold,
    gains,
    gain_first,
    gain_second,
    slot_tiles,
    weight_slots,
    first_moment,
    second_moment,
    basis_left,
    basis_right,
    out_grad,
):
    rows_here, tok_local, width = tokens.shape
    length = segment_ids.shape[1]
    hidden_width = FF
    heads = H
    head_dim = HD
    tile_side = weight_slots.shape[-1]
    slot_total = slot_tiles.shape[0]
    tile_count = (4 * width * width + 2 * width * hidden_width) // (tile_side * tile_side)
    query_start = lax.axis_index("seq") * tok_local
    query_pos = query_start + jnp.arange(tok_local, dtype=jnp.int32)
    key_pos = jnp.arange(length, dtype=jnp.int32)
    shared = lax.all_gather(weight_slots.astype(jnp.bfloat16), ("dp", "seq"), axis=0, tiled=True)
    tile_ids = jnp.arange(tile_count, dtype=jnp.int32)
    slot_ids = jnp.arange(slot_total, dtype=jnp.int32)
    position = jnp.sum(
        jnp.where(slot_tiles[None, :] == tile_ids[:, None], slot_ids[None, :], 0), axis=1
    )
    w_qkv, w_out, w_up, w_down = split_tiles(shared[position], width, hidden_width)
    local_ids = jnp.arange(tok_local, dtype=jnp.int32)
    lower_ones = (local_ids[None, :] < local_ids[:, None]).astype(jnp.float32)
    empty_columns = jnp.zeros((length,), jnp.float32)
    grad_sums = (
        jnp.zeros(w_qkv.shape, jnp.float32),
        jnp.zeros(w_out.shape, jnp.float32),
        jnp.zeros(w_up.shape, jnp.float32),
        jnp.zeros(w_down.shape, jnp.float32),
    )
    seg_row = segment_ids[0]
    valid_len = length - pad_lengths[0]
    seg_query = lax.dynamic_slice_in_dim(seg_row, query_start, tok_local)
    valid_keys = key_pos < valid_len
    row_input = tokens[0].astype(jnp.float32)
    normed_pre_f, pull_pre = jax.vjp(layer_norm, row_input, gains[0])
    normed_pre = normed_pre_f.astype(jnp.bfloat16)
    projected = jnp.dot(normed_pre, w_qkv, preferred_element_type=jnp.float32)
    query_heads = projected[:, :width].astype(jnp.bfloat16).reshape(tok_local, heads, head_dim)
    key_local = projected[:, width : 2 * width].astype(jnp.bfloat16)
    value_local = projected[:, 2 * width :].astype(jnp.bfloat16)
    key_all = lax.all_gather(key_local, "seq", axis=0, tiled=True)
    value_all = lax.all_gather(value_local, "seq", axis=0, tiled=True)
    key_heads = key_all.reshape(length, heads, head_dim)
    value_heads = value_all.reshape(length, heads, head_dim)
    value_float = value_heads.astype(jnp.float32)
    allowed = (seg_query[:, None] == seg_row[None, :]) & (key_pos[None, :] <= query_pos[:, None])
    allowed = allowed & (valid_keys[None, :] | (key_pos[None, :] == query_pos[:, None]))
    strict = allowed & (key_pos[None, :] < query_pos[:, None])
    strict_float = strict.astype(jnp.float32)
    allowed_float = allowed.astype(jnp.float32)
    scores = (
        jnp.einsum("qhd,khd->hqk", query_heads, key_heads, preferred_element_type=jnp.float32)
        * 0.125
    )
    select = select_scale * jax.nn.relu(scores[0]) * strict_float
    column_part = jnp.sum(select, axis=0)
    prefix = carried_in(column_part, "seq", add_single, empty_columns, False)
    shadow = prefix[None, :] + jnp.dot(lower_ones, select, precision=precise)
    logits = jnp.where(allowed[None], scores - shadow[None], -1e30)
    row_max = jnp.max(logits, axis=2)
    exps = jnp.exp(logits - row_max[:, :, None]) * allowed_float[None]
    totals = jnp.sum(exps, axis=2)
    probs = exps / totals[:, :, None]
    mixed_out = jnp.einsum("hqk,khd->qhd", probs, value_float, precision=precise).reshape(
        tok_local, width
    )
    column_total = lax.psum(column_part, "seq")
    counted = jnp.sum(
        valid_keys.astype(jnp.float32)
        * jax.nn.sigmoid((column_total - threshold[0]) * fraction_slope)
    )
    fraction_rows = [counted / valid_len.astype(jnp.float32)]
    mixed_b = mixed_out.astype(jnp.bfloat16)
    hidden_one = row_input + jnp.dot(mixed_b, w_out, preferred_element_type=jnp.float32)
    normed_mid_f, pull_mid = jax.vjp(layer_norm, hidden_one, gains[1])
    normed_mid = normed_mid_f.astype(jnp.bfloat16)
    upper = jnp.dot(normed_mid, w_up, preferred_element_type=jnp.float32)
    active_f, pull_gelu = jax.vjp(gelu_local, upper)
    active = active_f.astype(jnp.bfloat16)
    result = hidden_one + jnp.dot(active, w_down, preferred_element_type=jnp.float32)
    output_rows = [result.astype(jnp.bfloat16)]
    row_grad = out_grad[0]
    grad_down = jnp.einsum("tf,td->fd", active, row_grad, preferred_element_type=jnp.float32)
    grad_active = jnp.einsum("td,fd->tf", row_grad, w_down, preferred_element_type=jnp.float32)
    grad_upper = pull_gelu(grad_active)[0].astype(jnp.bfloat16)
    grad_up = jnp.einsum("td,tf->df", normed_mid, grad_upper, preferred_element_type=jnp.float32)
    grad_mid = jnp.einsum("tf,df->td", grad_upper, w_up, preferred_element_type=jnp.float32)
    grad_hidden_ln, grad_gain_mid = pull_mid(grad_mid)
    grad_hidden = row_grad.astype(jnp.float32) + grad_hidden_ln
    grad_branch = grad_hidden.astype(jnp.bfloat16)
    grad_out = jnp.einsum("td,te->de", mixed_b, grad_branch, preferred_element_type=jnp.float32)
    grad_mixed = jnp.einsum(
        "te,de->td", grad_branch, w_out, preferred_element_type=jnp.float32
    ).astype(jnp.bfloat16)
    delta_rows = jnp.sum(
        (grad_mixed.astype(jnp.float32) * mixed_out).reshape(tok_local, heads, head_dim), axis=2
    )
    grad_heads = grad_mixed.reshape(tok_local, heads, head_dim)
    dprob = jnp.einsum("qhd,khd->hqk", grad_heads, value_heads, preferred_element_type=jnp.float32)
    grad_values_part = jnp.einsum(
        "hqk,qhd->khd", probs, grad_heads.astype(jnp.float32), precision=precise
    )
    dlogit = probs * (dprob - delta_rows.T[:, :, None])
    grad_shadow = -jnp.sum(dlogit, axis=0)
    shadow_columns = jnp.sum(grad_shadow, axis=0)
    suffix = carried_in(shadow_columns, "seq", add_single, empty_columns, True)
    grad_select = jnp.dot(lower_ones.T, grad_shadow, precision=precise) + suffix[None, :]
    head_zero = (
        dlogit[0]
        + grad_select * select_scale * (scores[0] > 0.0).astype(jnp.float32) * strict_float
    )
    grad_scores = jnp.concatenate([head_zero[None], dlogit[1:]], axis=0).astype(jnp.bfloat16)
    grad_query = (
        jnp.einsum("hqk,khd->qhd", grad_scores, key_heads, preferred_element_type=jnp.float32)
        * 0.125
    ).reshape(tok_local, width)
    grad_keys_part = (
        jnp.einsum("hqk,qhd->khd", grad_scores, query_heads, preferred_element_type=jnp.float32)
        * 0.125
    )
    grad_keys = lax.psum_scatter(
        grad_keys_part.reshape(length, width).astype(jnp.bfloat16),
        "seq",
        scatter_dimension=0,
        tiled=True,
    )
    grad_values = lax.psum_scatter(
        grad_values_part.reshape(length, width).astype(jnp.bfloat16),
        "seq",
        scatter_dimension=0,
        tiled=True,
    )
    grad_qkv = jnp.concatenate([grad_query.astype(jnp.bfloat16), grad_keys, grad_values], axis=1)
    grad_qkv_w = jnp.einsum("td,te->de", normed_pre, grad_qkv, preferred_element_type=jnp.float32)
    grad_pre = jnp.einsum("te,de->td", grad_qkv, w_qkv, preferred_element_type=jnp.float32)
    grad_input_ln, grad_gain_pre = pull_pre(grad_pre)
    input_rows = [grad_hidden + grad_input_ln]
    gain_grad = jnp.stack([grad_gain_pre, grad_gain_mid])
    grad_sums = (grad_qkv_w, grad_out, grad_up, grad_down)
    owned_grad = lax.psum_scatter(
        slot_buffer(grad_sums, slot_tiles, tile_side, tile_count),
        ("dp", "seq"),
        scatter_dimension=0,
        tiled=True,
    )
    gain_total = lax.psum(gain_grad, ("dp", "seq"))
    correction = 1.0 - first_decay**STEP
    moment_first, moment_second, new_weights = rotated_adam(
        owned_grad, first_moment, second_moment, basis_left, basis_right, weight_slots, correction
    )
    gain_moment = first_decay * gain_first + (1.0 - first_decay) * gain_total
    gain_square = second_decay * gain_second + (1.0 - second_decay) * gain_total * gain_total
    gain_update = gains - gain_rate * (gain_moment / correction) / (
        jnp.sqrt(gain_square / correction) + adam_epsilon
    )
    return (
        jnp.stack(output_rows),
        jnp.stack(input_rows),
        jnp.stack(fraction_rows),
        moment_first,
        moment_second,
        new_weights,
        gain_update,
        gain_moment,
        gain_square,
    )


def solution(mesh):
    in_specs = (
        P("dp", "seq", None),
        P("dp", None),
        P("dp"),
        P(),
        P(),
        P(),
        P(),
        P(),
        P(("dp", "seq"), None, None),
        P(("dp", "seq"), None, None),
        P(("dp", "seq"), None, None),
        P(("dp", "seq"), None, None),
        P(("dp", "seq"), None, None),
        P("dp", "seq", None),
    )
    out_specs = (
        P("dp", "seq", None),
        P("dp", "seq", None),
        P("dp"),
        P(("dp", "seq"), None, None),
        P(("dp", "seq"), None, None),
        P(("dp", "seq"), None, None),
        P(),
        P(),
        P(),
    )
    return jax.shard_map(local, mesh=mesh, in_specs=in_specs, out_specs=out_specs, check_vma=False)
```

profile of v0, /device:TPU:0, one launch (start us, length us, event | category | flops | bytes accessed | tf_op | source)
XLA Modules:
  0.0 710.3 jit_solution(11046674508676594106)
XLA Ops:
  14.0 105.5 %all-gather.6.cloned.1.call-done = bf16[448,128,128]{2,1,0:T(8,128)(2,1)} async-done(((bf16[14,128,128]{2,1,0:T(8,128)(2,1)}), bf16[448,128,128]{2,1,0:T(8,128)(2,1)}) %all-gather.6.cloned.1.call-update) | async-done | bytes 14680080 | tf_op jit(solution)/shard_map/all_gather | solution.py:124
  119.5 18.3 %gather_fusion = bf16[432,128,128]{2,1,0:T(8,128)(2,1)} fusion(bf16[448,128,128]{2,1,0:T(8,128)(2,1)} %all-gather.6.cloned.1.call-done, s32[1024]{0:T(1024)S(1)} %pad_clamp_fusion.1), kind=kCustom, calls=%fused_computation | custom fusion | bytes 28313280 | tf_op jit(solution)/shard_map/gather | solution.py:130
  150.0 12.0 %fusion.132 = (bf16[144,128,128]{2,1,0:T(8,128)(2,1)}, bf16[144,128,128]{2,1,0:T(8,128)(2,1)}) fusion(bf16[432,128,128]{2,1,0:T(8,128)(2,1)} %gather_fusion), kind=kLoop, calls=%fused_computation.197 | loop fusion | bytes 18874368 | tf_op jit(solution)/shard_map/slice | solution.py:68
  162.0 6.9 copy.79
  168.9 7.5 %copy.78 = bf16[6,24,128,128]{3,1,2,0:T(8,128)(2,1)} copy(bf16[6,24,128,128]{3,2,1,0:T(8,128)(2,1)} %bitcast.240) | data formatting | bytes 9437184 | tf_op jit(solution)/shard_map/reshape | solution.py:57
  180.2 4.6 copy-done.1
  186.1 5.6 all-gather
  194.5 17.9 %fusion.134 = (f32[12,256]{1,0:T(8,128)S(1)}, f32[12,256,1024]{2,1,0:T(8,128)}) fusion(f32[256,1024]{1,0:T(8,128)S(1)} %copy-done.31, f32[12,256,1024]{2,1,0:T(8,128)} %copy-done.1, f32[256,1024]{1,0:T(8,128)S(1)} %convolution_add_fusion.1, pred[256,1024]{1,0:T(8,128)(4,1)S(1)} %get-tuple-element.238), kind=kOutput, calls=%fused_computation.199 | output fusion | flops 22021120 | bytes 27537408 | tf_op jit(solution)/shard_map/sub | solution.py:171
  214.2 10.6 %fusion.128 = f32[12,64,256]{2,1,0:T(8,128)S(1)} fusion(bf16[1024,12,64]{0,2,1:T(8,128)(2,1)S(1)} %bitcast.266, f32[12,256,1024]{2,1,0:T(8,128)} %get-tuple-element.241, f32[12,256]{1,0:T(8,128)S(1)} %get-tuple-element.240), kind=kOutput, calls=%fused_computation.194 | convolution fusion | flops 2419064832 | bytes 14954496 | tf_op jit(solution)/shard_map/hqk,khd->qhd/dot_general | solution.py:174
  245.1 11.4 %convolution_convert_fusion.1 = bf16[12,64,1024]{2,1,0:T(8,128)(2,1)} fusion(bf16[256,12,64]{0,2,1:T(8,128)(2,1)S(1)} %bitcast.277, f32[12,256,1024]{2,1,0:T(8,128)} %get-tuple-element.241, f32[12,256]{1,0:T(8,128)S(1)} %copy-done.64), kind=kOutput, calls=%fused_computation.60 | convolution fusion | flops 2419851264 | bytes 14561280 | tf_op jit(solution)/shard_map/hqk,qhd->khd/dot_general | solution.py:210
  256.9 11.2 %fusion.129 = (f32[1024]{0:T(1024)S(1)}, f32[256,1024]{1,0:T(8,128)}, f32[12,256,1024]{2,1,0:T(8,128)}) fusion(f32[12,256]{1,0:T(8,128)S(1)} %bitcast.284, bf16[256,12,64]{0,2,1:T(8,128)(2,1)} %bitcast.278, bf16[1024,12,64]{0,2,1:T(8,128)(2,1)} %bitcast.267, f32[12,256,1024]{2,1,0:T(8,128)} %get-tuple-element.241, f32[12,256]{1,0:T(8,128)S(1)} %copy-done.64), kind=kOutput, calls=%fused_computation.195 | convolution fusion | flops 418118656 | bytes 28209152 | tf_op jit(solution)/shard_map/qhd,khd->hqk/dot_general | solution.py:209
  268.2 8.0 %slice.78 = bf16[11,256,1024]{2,1,0:T(8,128)(2,1)} slice(f32[12,256,1024]{2,1,0:T(8,128)} %get-tuple-element.247), slice={[1:12], [0:256], [0:1024]} | slice | bytes 11534336 | tf_op jit(solution)/shard_map/slice | solution.py:222
  276.2 5.4 all-gather.1
  285.3 5.2 multiply_convert_fusion
  295.4 5.8 copy.106
  301.2 9.1 %copy.86 = f32[6,128,24,128]{3,1,2,0:T(8,128)} copy(f32[6,128,24,128]{3,2,1,0:T(8,128)} %bitcast.238) | data formatting | bytes 18874368 | tf_op jit(solution)/shard_map/reshape | solution.py:51
  313.9 5.6 fusion.62
  319.5 4.7 fusion.138
  346.2 8.6 %constant_dynamic-update-slice_fusion = f32[433,128,128]{2,1,0:T(8,128)} fusion(f32[433,128,128]{2,1,0:T(8,128)} %constant_dynamic-update-slice_fusion.1, f32[144,128,128]{2,1,0:T(8,128)} %bitcast.237), kind=kLoop, calls=%fused_computation.152 | loop fusion | bytes 18874368
  355.3 26.1 %gather_fusion.1 = f32[448,128,128]{2,1,0:T(8,128)} fusion(f32[433,128,128]{2,1,0:T(8,128)} %broadcast_dynamic-update-slice_fusion, s32[1024]{0:T(1024)S(1)} %pad_clamp_fusion), kind=kCustom, calls=%fused_computation.1 | custom fusion | bytes 58722048 | tf_op jit(solution)/shard_map/gather | solution.py:79
  382.2 7.6 %psum.14 = f32[1024]{0:T(1024)S(1)} all-reduce(f32[1024]{0:T(1024)S(1)} %copy-done.37), channel_id=1, replica_groups=mesh['dp'=8,'seq'=4] {'seq'}, use_global_device_ids=true, to_apply=%region_21.22 | all-reduce | flops 1024 | bytes 8192 | tf_op jit(solution)/shard_map/psum | solution.py:177
  391.1 6.3 fusion.64
  397.4 56.6 %psum.15 = f32[2,768]{1,0:T(2,128)S(1)} all-reduce(f32[2,768]{1,0:T(2,128)S(1)} %pad_maximum_fusion.10), channel_id=1, replica_groups=mesh['dp'=8,'seq'=4] {'dp','seq'}, use_global_device_ids=true, to_apply=%region_26.27 | all-reduce | flops 1536 | bytes 12288 | tf_op jit(solution)/shard_map/psum | solution.py:256
  457.0 234.1 %reduce-scatter.8.cloned.1.call-done = f32[14,128,128]{2,1,0:T(8,128)} async-done(((f32[448,128,128]{2,1,0:T(8,128)}), f32[14,128,128]{2,1,0:T(8,128)}) %reduce-scatter.8.cloned.1.call-update) | async-done | bytes 917520 | tf_op jit(solution)/shard_map/reduce_scatter | solution.py:250
  (255 shorter events, 97.2 us)
Async XLA Ops:
  7.2 687.0 %copy-start = (f32[14,128,128]{2,1,0:T(8,128)S(1)}, f32[14,128,128]{2,1,0:T(8,128)}, u32[]{:S(2)}) copy-start(f32[14,128,128]{2,1,0:T(8,128)} %param.30) | copy-start | bytes 2752516
  7.2 112.3 %all-gather.6.cloned.1.call-start = ((), (), s32[]{:S(2)}) async-start(), calls=%async_computation.3 | async-start | bytes 15138816 | tf_op jit(solution)/shard_map/all_gather | solution.py:124
  9.4 167.2 %all-gather.10.cloned.1.call-start = ((), (), s32[]{:S(2)}) async-start(), calls=%async_computation.5 | async-start | bytes 1966080 | tf_op jit(solution)/shard_map/all_gather | solution.py:151
  12.2 130.0 %copy-start.42 = (f32[256]{0:T(256)}, f32[256]{0:T(256)S(1)}, u32[]{:S(2)}) copy-start(f32[256]{0:T(256)S(1)} %broadcast_multiply_fusion.2) | copy-start | bytes 3076
  14.0 128.2 %copy-start.44 = (f32[256]{0:T(256)}, f32[256]{0:T(256)S(1)}, u32[]{:S(2)}) copy-start(f32[256]{0:T(256)S(1)} %fusion.112) | copy-start | bytes 3076
  145.4 67.1 %all-gather.8.cloned.1.call-start = ((), (), s32[]{:S(2)}) async-start(), calls=%async_computation.4 | async-start | bytes 1966080 | tf_op jit(solution)/shard_map/all_gather | solution.py:152
  148.0 30.3 %copy-start.29 = (bf16[256,768]{0,1:T(8,128)(2,1)}, bf16[256,768]{0,1:T(8,128)(2,1)S(1)}, u32[]{:S(2)}) copy-start(bf16[256,768]{0,1:T(8,128)(2,1)S(1)} %copy.75) | copy-start | bytes 1179652
  176.5 147.7 %reduce-scatter.6.cloned.1.call-start = ((), (), s32[]{:S(2)}) async-start(), calls=%async_computation.7 | async-start | bytes 1966080 | tf_op jit(solution)/shard_map/reduce_scatter | solution.py:237
  212.4 12.4 %copy-start.63 = (f32[12,256]{1,0:T(8,128)}, f32[12,256]{1,0:T(8,128)S(1)}, u32[]{:S(2)}) copy-start(f32[12,256]{1,0:T(8,128)S(1)} %get-tuple-element.240) | copy-start | bytes 36868
  214.1 12.4 %slice-start.7 = ((s8[4718592]{0:T(1024)(128)(4,1)}), s8[4194304]{0:T(1024)(128)(4,1)S(1)}, s32[]{:S(2)}) async-start(s8[4718592]{0:T(1024)(128)(4,1)} %bitcast.252), calls=%async_computation.16 | async-start | bytes 8388608
  214.2 12.4 %slice-start.8 = ((s8[4718592]{0:T(1024)(128)(4,1)}), s8[524288]{0:T(1024)(128)(4,1)S(1)}, s32[]{:S(2)}) async-start(s8[4718592]{0:T(1024)(128)(4,1)} %bitcast.252), calls=%async_computation.17 | async-start | bytes 1048576
  226.3 66.1 %copy-start.4 = (f32[256,768]{1,0:T(8,128)}, f32[256,768]{1,0:T(8,128)S(1)}, u32[]{:S(2)}) copy-start(f32[256,768]{1,0:T(8,128)S(1)} %get-tuple-element.243) | copy-start | bytes 2359300
  256.5 67.6 %reduce-scatter.4.cloned.1.call-start = ((), (), s32[]{:S(2)}) async-start(), calls=%async_computation.6 | async-start | bytes 1966080 | tf_op jit(solution)/shard_map/reduce_scatter | solution.py:231
  268.2 13.8 %copy-start.41 = (s32[1,1024]{1,0:T(1,128)S(1)}, s32[1,1024]{1,0:T(1,128)}, u32[]{:S(2)}) copy-start(s32[1,1024]{1,0:T(1,128)} %param.19) | copy-start | bytes 12292
  268.2 13.8 %copy-start.50 = (s32[1,256]{1,0:T(1,128)S(1)}, s32[1,256]{1,0:T(1,128)}, u32[]{:S(2)}) copy-start(s32[1,256]{1,0:T(1,128)} %copy-done.48) | copy-start | bytes 3076
  268.2 13.8 %copy-start.56 = (s32[256]{0:T(256)S(1)}, s32[256]{0:T(256)}, u32[]{:S(2)}) copy-start(s32[256]{0:T(256)} %copy-done.54) | copy-start | bytes 3076
  268.2 13.8 %copy-start.59 = (pred[1024]{0:T(1024)(128)(4,1)S(1)}, pred[1024]{0:T(1024)(128)(4,1)}, u32[]{:S(2)}) copy-start(pred[1024]{0:T(1024)(128)(4,1)} %copy-done.57) | copy-start | bytes 3076
  290.5 400.7 %reduce-scatter.8.cloned.1.call-start = ((), (), s32[]{:S(2)}) async-start(), calls=%async_computation.8 | async-start | bytes 30277632 | tf_op jit(solution)/shard_map/reduce_scatter | solution.py:250
  391.0 63.0 %copy-start.38 = (f32[2,768]{1,0:T(2,128)S(1)}, f32[2,768]{1,0:T(2,128)}, u32[]{:S(2)}) copy-start(f32[2,768]{1,0:T(2,128)} %param.22) | copy-start | bytes 18436
  391.1 62.9 %copy-start.52 = (f32[2,768]{1,0:T(2,128)S(1)}, f32[2,768]{1,0:T(2,128)}, u32[]{:S(2)}) copy-start(f32[2,768]{1,0:T(2,128)} %param.23) | copy-start | bytes 18436
  391.1 62.9 %copy-start.53 = (f32[2,768]{1,0:T(2,128)S(1)}, f32[2,768]{1,0:T(2,128)}, u32[]{:S(2)}) copy-start(f32[2,768]{1,0:T(2,128)} %param.24) | copy-start | bytes 18436
  391.1 63.6 %copy-start.3 = (f32[256,768]{1,0:T(8,128)S(1)}, f32[256,768]{1,0:T(8,128)}, u32[]{:S(2)}) copy-start(f32[256,768]{1,0:T(8,128)} %copy-done.2) | copy-start | bytes 2359300
  391.1 63.5 %copy-start.10 = (bf16[1,256,768]{2,1,0:T(8,128)(2,1)S(1)}, bf16[1,256,768]{2,1,0:T(8,128)(2,1)}, u32[]{:S(2)}) copy-start(bf16[1,256,768]{2,1,0:T(8,128)(2,1)} %param.18) | copy-start | bytes 1179652
  391.1 63.5 %copy-start.20 = (bf16[1,256,768]{2,1,0:T(8,128)(2,1)S(1)}, bf16[1,256,768]{2,1,0:T(8,128)(2,1)}, u32[]{:S(2)}) copy-start(bf16[1,256,768]{2,1,0:T(8,128)(2,1)} %param.31) | copy-start | bytes 1179652
  (56 other events, 263.6 us)
Sparse Core Ops, SparseCore 0:
  11.4 108.0 all-gather.5
  145.5 17.8 all-gather.9
  176.6 18.1 all-gather.7
  256.7 26.6 reduce-scatter.5
  290.6 26.1 reduce-scatter.3
  381.6 309.5 reduce-scatter.7
where the time goes:
time: 721 us; the launch traced here: 710 us
  waiting for transfers between devices  340 us (47%)
  local copies, waits for them, and re-layouts  144 us (20%)
  matrix products  96.7 us (13%)
  blocking collectives  75 us (10%)
  other arithmetic  35.5 us (5%)
  between operations  18.8 us (3%)
    reduce_scatter x1, waiting for transfers between devices, local(): lax.psum_scatter(slot_buffer(grad_sums, slot_tiles, tile_side, tile_count...  234 us
    all_gather x1, waiting for transfers between devices, local(): lax.all_gather(weight_slots.astype(jnp.bfloat16), ('dp', 'seq'), axis=0,...  105 us
    psum x1, blocking collectives, local(): gain_total = lax.psum(gain_grad, ('dp', 'seq'))  56.6 us
    unnamed x149, local copies, waits for them, and re-layouts  34 us
    gather x1, local copies, waits for them, and re-layouts, slot_buffer(): return stacked[jnp.minimum(slot_tiles, tile_count)]  26.1 us
    reshape x4, local copies, waits for them, and re-layouts, matrix_of(): tile_stack.reshape(height // tile_side, across // tile_side, tile_side, t...  18.9 us
    gather x1, local copies, waits for them, and re-layouts, local(): shared[position]  18.3 us
    sub x1, other arithmetic, local(): exps = jnp.exp(logits - row_max[:, :, None]) * allowed_float[None]  17.9 us
  transfers between devices with their start and end apart: 6, of which 2 were waited for; matrix products, arithmetic and copies ran while one was open for 18% of the time, Pallas kernels for 0%

commit v1 on v0

v1 whole, which is shorter than its diff:
```python
import functools

import jax
import jax.numpy as jnp
from jax import lax
from jax.experimental import pallas as pl
from jax.experimental.pallas import tpu as pltpu
from jax.sharding import PartitionSpec as P

H = 12
HD = 64
FF = 3072
STEP = 3
SPAN = 512
CHUNK = 256

select_scale = 0.2
fraction_slope = 2.0
first_decay = 0.5
second_decay = 0.5
adam_epsilon = 1e-08
weight_rate = 0.05
gain_rate = 0.2
decay_rate = 0.1
norm_epsilon = 1e-05
precise = lax.Precision.HIGHEST

BF = jnp.bfloat16
F32 = jnp.float32
VMEM = pltpu.VMEM
SMEM = pltpu.SMEM


def mm(a, b):
    return lax.dot_general(a, b, (((1,), (0,)), ((), ())), preferred_element_type=F32)


def mm_nt(a, b):
    return lax.dot_general(a, b, (((1,), (1,)), ((), ())), preferred_element_type=F32)


def split(x):
    high = x.astype(BF)
    return high, (x - high.astype(F32)).astype(BF)


def mm_split(x, exact):
    high, rest = split(x)
    return mm(high, exact) + mm(rest, exact)


def lane_half(shape, second):
    lane = lax.broadcasted_iota(jnp.int32, shape, 1)
    return (lane >= HD) if second else (lane < HD)


def keep_half(x, second):
    return jnp.where(lane_half(x.shape, second), x, jnp.zeros_like(x))


def norm_parts(x):
    centred = x - jnp.mean(x, axis=-1, keepdims=True)
    rate = lax.rsqrt(jnp.mean(centred * centred, axis=-1, keepdims=True) + norm_epsilon)
    return centred * rate, rate


def send_tile(tile_ref, dst, keep, send, sem):
    half = keep.shape[0]

    @pl.when(dst < half)
    def _():
        pltpu.make_async_copy(tile_ref, keep.at[dst], sem).start()

    @pl.when(dst >= half)
    def _():
        pltpu.make_async_copy(tile_ref, send.at[dst - half], sem).start()


def layer_kernel(
    tiles,
    src,
    dst,
    scal,
    thr,
    tok,
    gains,
    dy,
    segc,
    segr,
    w_hbm,
    out,
    ghid,
    gq,
    gk,
    gv,
    nrm_t,
    wqkv,
    q0,
    k0t,
    part0,
    mask0,
    colsum,
    small,
    keep,
    send,
    wall,
    nrm,
    q_s,
    q_e,
    k_s,
    v_s,
    kt_s,
    vt_s,
    bias,
    gsh,
    probs,
    mixt,
    mixb,
    mixbt,
    wout,
    hid,
    xhat,
    nm,
    nmt,
    acc,
    gmid,
    g_s,
    gt_s,
    wu,
    wd,
    stage,
    zero,
    wsem,
    gsem,
    zsem,
):
    n_qkv, n_out, n_up, n_down = tiles
    width = tok.shape[1]
    own = dy.shape[0]
    window = tok.shape[0]
    back = window - own
    side = wall.shape[-1]
    dt = width // side
    pairs = width // side
    total_slots = 2 * keep.shape[0]
    load = pltpu.make_async_copy(w_hbm, wall, wsem)
    load.start()
    zero[...] = jnp.zeros_like(zero)
    tile_count = n_qkv + n_out + n_up + n_down
    empty = total_slots - tile_count

    @pl.loop(0, empty)
    def _(e):
        send_tile(zero, dst[tile_count + e], keep, send, zsem)

    gain_pre = gains[0:1, :]
    gain_mid = gains[1:2, :]

    @pl.loop(0, window // own)
    def _(b):
        rows = pl.ds(pl.multiple_of(b * own, own), own)
        hat, _ = norm_parts(tok[rows, :].astype(F32))
        value = (hat * gain_pre).astype(BF)
        nrm[rows, :] = value
        nrm_t[:, rows] = value.T

    load.wait()
    per_row = 3 * dt

    @pl.loop(0, 3 * dt // 2)
    def _(j):
        for i in range(dt):
            for jj in range(2):
                wqkv[i * side : (i + 1) * side, pl.ds(pl.multiple_of((2 * j + jj) * side, side), side)] = wall[
                    src[i * per_row + 2 * j + jj]
                ]

    for i in range(dt):
        for j in range(dt):
            wout[i * side : (i + 1) * side, j * side : (j + 1) * side] = wall[src[n_qkv + i * dt + j]]

    @pl.loop(0, dt // 2)
    def _(j):
        cols = pl.ds(pl.multiple_of(2 * j * side, 2 * side), 2 * side)
        got = (mm(nrm[back:, :], wqkv[:, cols]) * 0.125).astype(BF)
        q_s[2 * j] = got[:, :side]
        q_s[2 * j + 1] = got[:, side:]

    q_e[...] = (mm(nrm[:back, :], wqkv[:, 0:side]) * 0.125).astype(BF)

    @pl.loop(0, dt // 2)
    def _(j):
        cols = pl.ds(pl.multiple_of(width + 2 * j * side, 2 * side), 2 * side)
        got = mm(nrm[...], wqkv[:, cols]).astype(BF)
        got_t = got.T
        k_s[2 * j] = got[:, :side]
        k_s[2 * j + 1] = got[:, side:]
        kt_s[2 * j] = got_t[:side, :]
        kt_s[2 * j + 1] = got_t[side:, :]

    @pl.loop(0, dt // 2)
    def _(j):
        cols = pl.ds(pl.multiple_of(2 * width + 2 * j * side, 2 * side), 2 * side)
        got = mm(nrm[...], wqkv[:, cols]).astype(BF)
        got_t = got.T
        v_s[2 * j] = got[:, :side]
        v_s[2 * j + 1] = got[:, side:]
        vt_s[2 * j] = got_t[:side, :]
        vt_s[2 * j + 1] = got_t[side:, :]

    q0[...] = q_s[0]
    k0t[...] = kt_s[0]

    valid_len = scal[0]
    start = scal[1]
    is_last = scal[2]
    key_at = lax.broadcasted_iota(jnp.int32, (window, own), 0)
    query_at = lax.broadcasted_iota(jnp.int32, (window, own), 1)
    key_valid = (key_at + (start - back)) < valid_len
    key_seg = segc[...]
    k_first = k_s[0]

    def selected(q_rows, first):
        s = mm_nt(k_first, keep_half(q_rows, False))
        same = key_seg == segr[:, first : first + own]
        strict = same & key_valid & (key_at < query_at + first)
        return s, same, jnp.where(strict, select_scale * jnp.maximum(s, 0.0), 0.0), strict

    prefix = jnp.zeros((window, 1), F32)
    for b in range(back // own):
        _, _, chosen, _ = selected(q_e[b * own : (b + 1) * own, :], b * own)
        prefix = prefix + jnp.sum(chosen, axis=1, keepdims=True)
    s_own, same, chosen, strict = selected(q_s[0], back)
    tri_row = lax.broadcasted_iota(jnp.int32, (own, own), 0)
    tri_col = lax.broadcasted_iota(jnp.int32, (own, own), 1)
    earlier = jnp.where(tri_row < tri_col, 1.0, 0.0).astype(BF)
    shadow = prefix + mm_split(chosen, earlier)
    allowed = strict | (same & (key_at == query_at + back))
    bias[...] = jnp.where(allowed, -shadow, -1e30)
    mask0[...] = jnp.where(strict & (s_own > 0.0), 1.0, 0.0).astype(BF)
    column_total = prefix + jnp.sum(chosen, axis=1, keepdims=True)
    key_col = lax.broadcasted_iota(jnp.int32, (window, 1), 0)
    key_pos = key_col + (start - back)
    counts = (key_pos >= 0) & (key_pos < valid_len) & ((key_col < own) | (is_last > 0))
    soft = 1.0 / (1.0 + jnp.exp(-fraction_slope * (column_total - thr[0])))
    counted = jnp.sum(jnp.where(counts, soft, 0.0), axis=0, keepdims=True)
    small[...] = jnp.zeros_like(small)
    small[1:2, :] = jnp.broadcast_to(counted / valid_len.astype(F32), (1, width))

    @pl.loop(0, pairs)
    def _(p):
        q2 = q_s[p]
        k2 = k_s[p]
        for hh in range(2):
            s = mm_nt(k2, keep_half(q2, hh == 1)) + bias[...]
            e = jnp.exp(s - jnp.max(s, axis=0, keepdims=True))
            pr = (e * (1.0 / jnp.sum(e, axis=0, keepdims=True))).astype(BF)
            probs[2 * p + hh] = pr
            vt = vt_s[p, hh * HD : (hh + 1) * HD, :]
            mixt[pl.ds(pl.multiple_of(p * side + hh * HD, HD), HD), :] = mm(vt, pr)

    mixbt[...] = mixt[...].astype(BF)
    mixb[...] = mixbt[...].T
    hid[...] = tok[back:, :].astype(F32) + mm(mixb[...], wout[...])
    hat, rate = norm_parts(hid[...])
    xhat[...] = hat
    nm[...] = (hat * gain_mid).astype(BF)
    nmt[...] = nm[...].T

    acc[...] = jnp.zeros_like(acc)
    gmid[...] = jnp.zeros_like(gmid)
    cw = CHUNK // side
    f_tiles = FF // side
    per_chunk = 2 * cw * dt
    chunks = FF // CHUNK

    @pl.loop(0, chunks)
    def _(c):
        slot = lax.rem(c, 2)
        for i in range(dt):
            for jj in range(cw):
                wu[i * side : (i + 1) * side, jj * side : (jj + 1) * side] = wall[
                    src[n_qkv + n_out + i * f_tiles + cw * c + jj]
                ]
        for ii in range(cw):
            for j in range(dt):
                wd[ii * side : (ii + 1) * side, j * side : (j + 1) * side] = wall[
                    src[n_qkv + n_out + n_up + (cw * c + ii) * dt + j]
                ]
        up = mm(nm[...], wu[...])
        cube = 0.7978845608028654 * (up + 0.044715 * up * up * up)
        th = jnp.tanh(cube)
        active = (0.5 * up * (1.0 + th)).astype(BF)
        slope = 0.5 * (1.0 + th) + 0.5 * up * (1.0 - th * th) * (
            0.7978845608028654 * (1.0 + 3.0 * 0.044715 * up * up)
        )
        acc[...] += mm(active, wd[...])
        gu = (mm_nt(dy[...], wd[...]) * slope).astype(BF)
        gmid[...] += mm_nt(gu, wu[...])

        @pl.when(c >= 2)
        def _():
            pltpu.make_async_copy(stage.at[slot], keep.at[pl.ds(0, per_chunk)], gsem.at[slot]).wait()

        g_down = mm(active.T, dy[...]).astype(BF)
        for ii in range(cw):
            for j in range(dt):
                at = ii * dt + j
                stage[slot, at] = g_down[ii * side : (ii + 1) * side, j * side : (j + 1) * side]
        g_up = mm(nmt[...], gu).astype(BF)
        for i in range(dt):
            for jj in range(cw):
                at = cw * dt + i * cw + jj
                stage[slot, at] = g_up[i * side : (i + 1) * side, jj * side : (jj + 1) * side]
        for ii in range(cw):
            for j in range(dt):
                at = ii * dt + j
                t = n_qkv + n_out + n_up + (cw * c + ii) * dt + j
                send_tile(stage.at[slot, at], dst[t], keep, send, gsem.at[slot])
        for i in range(dt):
            for jj in range(cw):
                at = cw * dt + i * cw + jj
                t = n_qkv + n_out + i * f_tiles + cw * c + jj
                send_tile(stage.at[slot, at], dst[t], keep, send, gsem.at[slot])

    out[...] = (hid[...] + acc[...]).astype(BF)
    hat = xhat[...]
    gm = gmid[...]
    small[0:1, :] = jnp.sum(gm * hat, axis=0, keepdims=True)
    scaled = gm * gain_mid
    gh = dy[...].astype(F32) + rate * (
        scaled
        - jnp.mean(scaled, axis=-1, keepdims=True)
        - hat * jnp.mean(scaled * hat, axis=-1, keepdims=True)
    )
    ghid[...] = gh
    gb = gh.astype(BF)
    gmix = mm_nt(gb, wout[...]).astype(BF)
    for p in range(pairs):
        g_s[p] = gmix[:, p * side : (p + 1) * side]
    gt_s[...] = gmix.T

    for slot in range(2):
        pltpu.make_async_copy(stage.at[slot], keep.at[pl.ds(0, per_chunk)], gsem.at[slot]).wait()
    half_out = dt // 2
    for part in range(2):
        g_out = mm(mixbt[part * half_out * side : (part + 1) * half_out * side, :], gb).astype(BF)
        for i in range(half_out):
            for j in range(dt):
                stage[part, i * dt + j] = g_out[i * side : (i + 1) * side, j * side : (j + 1) * side]
        for i in range(half_out):
            for j in range(dt):
                t = n_qkv + (part * half_out + i) * dt + j
                send_tile(stage.at[part, i * dt + j], dst[t], keep, send, gsem.at[part])

    gsh[...] = jnp.zeros_like(gsh)

    @pl.loop(0, pairs)
    def _(p):
        g2 = g_s[p]
        q2 = q_s[p]
        v2 = v_s[p]
        later = jnp.where(p > 0, 1.0, 0.0)
        dk = jnp.zeros((window, side), F32)
        dv = jnp.zeros((window, side), F32)
        dqs = []
        for hh in range(2):
            rows = pl.ds(pl.multiple_of(p * side + hh * HD, HD), HD)
            delta = jnp.sum(gt_s[rows, :].astype(F32) * mixt[rows, :], axis=0, keepdims=True)
            gm2 = keep_half(g2, hh == 1)
            pr = probs[2 * p + hh]
            dl = pr.astype(F32) * (mm_nt(v2, gm2) - delta)
            gsh[...] += dl
            dv = dv + mm(pr, gm2)
            gs = dl.astype(BF)
            dq = mm(kt_s[p, hh * HD : (hh + 1) * HD, :], gs)
            dk_h = mm(gs, keep_half(q2, hh == 1))
            if hh == 0:
                dq = dq * later
                dk_h = dk_h * later

                @pl.when(p == 0)
                def _():
                    part0[...] = dl

            dqs.append(dq)
            dk = dk + dk_h
        cols = pl.ds(pl.multiple_of(p * side, side), side)
        gq[:, cols] = (jnp.concatenate(dqs, axis=0) * 0.125).T.astype(BF)
        gk[:, cols] = dk.astype(BF)
        gv[:, cols] = dv.astype(BF)

    ones = jnp.ones((8, own), BF)
    high, rest = split(-gsh[...])
    colsum[...] = mm_nt(ones, high) + mm_nt(ones, rest)
    after = jnp.where(tri_row > tri_col, 1.0, 0.0).astype(BF)
    part0[...] += select_scale * mask0[...].astype(F32) * (mm(high, after) + mm(rest, after))

    for part in range(2):
        pltpu.make_async_copy(
            stage.at[part, pl.ds(0, half_out * dt)], keep.at[pl.ds(0, half_out * dt)], gsem.at[part]
        ).wait()
    pltpu.make_async_copy(keep.at[pl.ds(0, empty)], keep.at[pl.ds(0, empty)], zsem).wait()


def qkv_kernel(
    dst, part0, mask0, suffix, q0, k0t, gq, gk, gv, nrm_t, keep_in, send_in, gq_out, gk_out, keep, send, stage, gsem
):
    own, width = gq.shape
    window = gk.shape[0]
    side = stage.shape[-1]
    dt = width // side
    back = window - own
    column = jnp.broadcast_to(suffix[0:1, :], (side, window)).T
    column = jnp.concatenate([column] * (own // side), axis=1)
    gs = (part0[...] + select_scale * mask0[...].astype(F32) * column).astype(BF)
    dq = (mm(k0t[0:HD, :], gs) * 0.125).T
    dk = mm(gs, keep_half(q0[...], False)).astype(BF)
    gq_out[...] = gq[...]
    gk_out[...] = gk[...]
    gq_out[:, 0:side] = gq[:, 0:side] + jnp.concatenate([dq, jnp.zeros_like(dq)], axis=1).astype(BF)
    gk_out[:, 0:side] = gk[:, 0:side] + dk

    for which in range(3):
        for jc in range(dt // 2):
            cols = slice(2 * jc * side, 2 * (jc + 1) * side)
            if which == 0:
                g = mm(nrm_t[:, back:], gq_out[:, cols])
            elif which == 1:
                g = mm(nrm_t[...], gk_out[:, cols])
            else:
                g = mm(nrm_t[...], gv[:, cols])
            g = g.astype(BF)
            for i in range(dt):
                for jj in range(2):
                    j = which * dt + 2 * jc + jj
                    t = i * 3 * dt + j
                    stage[t] = g[i * side : (i + 1) * side, jj * side : (jj + 1) * side]
                    send_tile(stage.at[t], dst[t], keep, send, gsem)
    count = 3 * dt * dt
    pltpu.make_async_copy(stage, keep.at[pl.ds(0, count)], gsem).wait()


def pre_kernel(tok, gq, gk, gv, wqkv, far, near, mine, small):
    own, width = gq.shape
    window = gk.shape[0]
    back = window - own
    total = jnp.zeros((1, width), F32)
    for b in range(window // own):
        rows = slice(b * own, (b + 1) * own)
        g = mm_nt(gk[rows, :], wqkv[:, width : 2 * width]) + mm_nt(gv[rows, :], wqkv[:, 2 * width :])
        if b == window // own - 1:
            g = g + mm_nt(gq[...], wqkv[:, :width])
            mine[...] = g
        elif b == 0:
            far[...] = g.astype(far.dtype)
        else:
            near[...] = g.astype(near.dtype)
        hat, _ = norm_parts(tok[rows, :].astype(F32))
        total = total + jnp.sum(g * hat, axis=0, keepdims=True)
    small[...] = jnp.broadcast_to(total, small.shape)


def input_kernel(tok, gains, ghid, mine, near, far, out):
    hat, rate = norm_parts(tok[...].astype(F32))
    g = mine[...] + near[...].astype(F32) + far[...].astype(F32)
    scaled = g * gains[0:1, :]
    out[...] = ghid[...] + rate * (
        scaled
        - jnp.mean(scaled, axis=-1, keepdims=True)
        - hat * jnp.mean(scaled * hat, axis=-1, keepdims=True)
    )


def rotated_adam(grad_slots, first, second, left, right, weight, correction):
    turned = jnp.einsum("sji,sjk->sik", left, grad_slots, precision=precise)
    turned = jnp.einsum("sik,skl->sil", turned, right, precision=precise)
    first_new = first_decay * first + (1.0 - first_decay) * turned
    second_new = second_decay * second + (1.0 - second_decay) * turned * turned
    norm_step = first_new / correction / (jnp.sqrt(second_new / correction) + adam_epsilon)
    back = jnp.einsum("sik,skl->sil", left, norm_step, precision=precise)
    back = jnp.einsum("sil,sjl->sij", back, right, precision=precise)
    return (first_new, second_new, weight - weight_rate * back - weight_rate * decay_rate * weight)


def bit_plan(devices, per_device):
    bits = [1 << b for b in range(devices.bit_length() - 1)]
    first, rest = bits[0], bits[1:]
    if devices == 32:
        orders = [(2, 4, 8, 16), (4, 8, 2, 16), (8, 16, 2, 4)]
    else:
        orders = [tuple(rest[i:] + rest[:i]) for i in range(3)]
    third = per_device * 3 // 7
    sizes = [third, per_device - third] if per_device < 4 else [third, per_device * 5 // 14, 0]
    if len(sizes) == 3:
        sizes[2] = per_device - sizes[0] - sizes[1]
    plan = []
    at = 0
    for size, order in zip(sizes, orders):
        if size:
            plan.append((at, size, order))
            at += size
    return first, plan


def local(
    tokens,
    segment_ids,
    pad_lengths,
    threshold,
    gains,
    gain_first,
    gain_second,
    slot_tiles,
    weight_slots,
    first_moment,
    second_moment,
    basis_left,
    basis_right,
    out_grad,
):
    axes = ("dp", "seq")
    n_dp, n_seq = lax.axis_size("dp"), lax.axis_size("seq")
    devices = n_dp * n_seq
    me = lax.axis_index(axes)
    seq_at = lax.axis_index("seq")
    _, own, width = tokens.shape
    length = segment_ids.shape[1]
    side = weight_slots.shape[-1]
    per_device = weight_slots.shape[0]
    slot_total = slot_tiles.shape[0]
    dt = width // side
    tiles = (3 * dt * dt, dt * dt, dt * (FF // side), dt * (FF // side))
    tile_count = sum(tiles)
    back = SPAN
    window = back + own

    shared = lax.all_gather(weight_slots.astype(BF), axes, axis=0, tiled=True)

    slot_ids = jnp.arange(slot_total, dtype=jnp.int32)
    position = jnp.sum(
        jnp.where(slot_tiles[None, :] == slot_ids[:, None], slot_ids[None, :], 0), axis=1
    )
    owner = position // per_device
    inner = position % per_device
    apart = owner ^ me
    first_bit, plan = bit_plan(devices, per_device)
    half = slot_total // 2
    spread = devices // 2
    place = jnp.zeros_like(position)
    for at, size, order in plan:
        index = jnp.zeros_like(position)
        for bit in order:
            index = index * 2 + ((apart & bit) != 0).astype(jnp.int32)
        here = at * spread + index * size + (inner - at)
        place = jnp.where((inner >= at) & (inner < at + size), here, place)
    dst = place + jnp.where((apart & first_bit) != 0, half, 0)
    src = position

    mine_tok = tokens[0]
    pieces = []
    for step in range(back // own, 0, -1):
        pieces.append(lax.ppermute(mine_tok, "seq", [(i, i + step) for i in range(n_seq - step)]))
    tok = jnp.concatenate(pieces + [mine_tok], axis=0)
    start = seq_at * own
    seg_window = lax.dynamic_slice_in_dim(
        jnp.concatenate([jnp.full((back,), -1, jnp.int32), segment_ids[0]]), start, window
    )
    valid_len = length - pad_lengths[0]
    scal = jnp.stack([valid_len, start, (seq_at == n_seq - 1).astype(jnp.int32)])

    hbm = pl.BlockSpec(memory_space=pl.ANY)
    vm = pl.BlockSpec(memory_space=VMEM)
    sm = pl.BlockSpec(memory_space=SMEM)
    shp = jax.ShapeDtypeStruct
    tile_buffer = shp((half, side, side), BF)


    per_chunk = 2 * (CHUNK // side) * dt
    outs = pl.pallas_call(
        functools.partial(layer_kernel, tiles),
        out_shape=(
            shp((own, width), BF),
            shp((own, width), F32),
            shp((own, width), BF),
            shp((window, width), BF),
            shp((window, width), BF),
            shp((width, window), BF),
            shp((width, 3 * width), BF),
            shp((own, side), BF),
            shp((side, window), BF),
            shp((window, own), F32),
            shp((window, own), BF),
            shp((8, window), F32),
            shp((8, width), F32),
            tile_buffer,
            tile_buffer,
        ),
        in_specs=[sm] * 4 + [vm] * 5 + [hbm],
        out_specs=tuple([vm] * 13 + [hbm] * 2),
        scratch_shapes=[
            VMEM((slot_total, side, side), BF),
            VMEM((window, width), BF),
            VMEM((dt, own, side), BF),
            VMEM((back, side), BF),
            VMEM((dt, window, side), BF),
            VMEM((dt, window, side), BF),
            VMEM((dt, side, window), BF),
            VMEM((dt, side, window), BF),
            VMEM((window, own), F32),
            VMEM((window, own), F32),
            VMEM((H, window, own), BF),
            VMEM((width, own), F32),
            VMEM((own, width), BF),
            VMEM((width, own), BF),
            VMEM((width, width), BF),
            VMEM((own, width), F32),
            VMEM((own, width), F32),
            VMEM((own, width), BF),
            VMEM((width, own), BF),
            VMEM((own, width), F32),
            VMEM((own, width), F32),
            VMEM((dt, own, side), BF),
            VMEM((width, own), BF),
            VMEM((width, CHUNK), BF),
            VMEM((CHUNK, width), BF),
            VMEM((2, per_chunk, side, side), BF),
            VMEM((side, side), BF),
            pltpu.SemaphoreType.DMA,
            pltpu.SemaphoreType.DMA((2,)),
            pltpu.SemaphoreType.DMA,
        ],
        compiler_params=pltpu.CompilerParams(vmem_limit_bytes=60 << 20),
        name="layer",
    )(
        src,
        dst,
        scal,
        threshold,
        tok,
        gains,
        out_grad[0],
        seg_window[:, None],
        seg_window[None, :],
        shared,
    )
    (output, ghid, gq, gk, gv, nrm_t, wqkv, q0, k0t, part0, mask0, colsum, small, keep, send) = outs

    sums = colsum[0]
    suffix = jnp.zeros((window,), F32)
    for step in range(1, back // own + 1):
        reach = window - step * own
        got = lax.ppermute(sums[:reach], "seq", [(i, i - step) for i in range(step, n_seq)])
        suffix = suffix + jnp.concatenate([jnp.zeros((step * own,), F32), got])
    suffix = jnp.broadcast_to(suffix[None, :], (8, window))

    gq, gk, keep, send = pl.pallas_call(
        qkv_kernel,
        out_shape=(shp((own, width), BF), shp((window, width), BF), tile_buffer, tile_buffer),
        in_specs=[sm] + [vm] * 9 + [hbm] * 2,
        out_specs=(vm, vm, hbm, hbm),
        scratch_shapes=[VMEM((tiles[0], side, side), BF), pltpu.SemaphoreType.DMA],
        input_output_aliases={10: 2, 11: 3},
        compiler_params=pltpu.CompilerParams(vmem_limit_bytes=40 << 20),
        name="qkv_grad",
    )(dst, part0, mask0, suffix, q0, k0t, gq, gk, gv, nrm_t, keep, send)

    def swap(x, bit):
        return lax.ppermute(x, axes, [(i, i ^ bit) for i in range(devices)])

    def plus(a, b):
        return (a.astype(F32) + b.astype(F32)).astype(BF)

    parts = []
    for at, size, order in plan:
        rows = slice(at * spread, (at + size) * spread)
        parts.append(plus(keep[rows], swap(send[rows], first_bit)))
    for step in range(len(plan[0][2])):
        for which, (_, _, order) in enumerate(plan):
            middle = parts[which].shape[0] // 2
            parts[which] = plus(parts[which][:middle], swap(parts[which][middle:], order[step]))
    owned_grad = jnp.concatenate(parts, axis=0).astype(F32)

    far, near, mine, small_pre = pl.pallas_call(
        pre_kernel,
        out_shape=(
            shp((own, width), BF),
            shp((own, width), BF),
            shp((own, width), F32),
            shp((8, width), F32),
        ),
        in_specs=[vm] * 5,
        out_specs=tuple([vm] * 4),
        compiler_params=pltpu.CompilerParams(vmem_limit_bytes=40 << 20),
        name="pre_grad",
    )(tok, gq, gk, gv, wqkv)
    far = lax.ppermute(far, "seq", [(i, i - 2) for i in range(2, n_seq)])
    near = lax.ppermute(near, "seq", [(i, i - 1) for i in range(1, n_seq)])
    input_grad = pl.pallas_call(
        input_kernel,
        out_shape=shp((own, width), F32),
        in_specs=[vm] * 6,
        out_specs=vm,
        compiler_params=pltpu.CompilerParams(vmem_limit_bytes=20 << 20),
        name="input_grad",
    )(mine_tok, gains, ghid, mine, near, far)

    row_at = lax.axis_index("dp")
    spots = jnp.arange(width, dtype=jnp.int32)
    totals = jnp.stack([small_pre[0], small[0], jnp.where(spots == row_at, small[1], 0.0)])
    bit = 1
    while bit < devices:
        totals = totals + swap(totals, bit)
        bit *= 2
    gain_total = totals[:2]
    fraction = lax.dynamic_slice_in_dim(totals[2], row_at, 1)

    correction = 1.0 - first_decay**STEP
    moment_first, moment_second, new_weights = rotated_adam(
        owned_grad, first_moment, second_moment, basis_left, basis_right, weight_slots, correction
    )
    gain_moment = first_decay * gain_first + (1.0 - first_decay) * gain_total
    gain_square = second_decay * gain_second + (1.0 - second_decay) * gain_total * gain_total
    gain_update = gains - gain_rate * (gain_moment / correction) / (
        jnp.sqrt(gain_square / correction) + adam_epsilon
    )
    return (
        output[None],
        input_grad[None],
        fraction,
        moment_first,
        moment_second,
        new_weights,
        gain_update,
        gain_moment,
        gain_square,
    )


def solution(mesh):
    in_specs = (
        P("dp", "seq", None),
        P("dp", None),
        P("dp"),
        P(),
        P(),
        P(),
        P(),
        P(),
        P(("dp", "seq"), None, None),
        P(("dp", "seq"), None, None),
        P(("dp", "seq"), None, None),
        P(("dp", "seq"), None, None),
        P(("dp", "seq"), None, None),
        P("dp", "seq", None),
    )
    out_specs = (
        P("dp", "seq", None),
        P("dp", "seq", None),
        P("dp"),
        P(("dp", "seq"), None, None),
        P(("dp", "seq"), None, None),
        P(("dp", "seq"), None, None),
        P(),
        P(),
        P(),
    )
    return jax.shard_map(local, mesh=mesh, in_specs=in_specs, out_specs=out_specs, check_vma=False)
```

time: 721 us -> 349 us (0.48); the launches traced: 710 us -> 348 us
  waiting for transfers between devices: 340 us -> 183 us
  local copies, waits for them, and re-layouts: 144 us -> 26.8 us
  matrix products: 96.7 us -> 6.61 us
  blocking collectives: 75 us -> 0 us
  Pallas kernels: 0 us -> 70.8 us
  starting transfers between devices: 0.42 us -> 28.1 us
  other arithmetic: 35.5 us -> 16.4 us
    reduce_scatter x3 -> x0, waiting for transfers between devices: 234 us -> none  [the longest x1 234 us: local(): lax.psum_scatter(slot_buffer(grad_sums, slot_tiles, tile_side, tile_count...]
    ppermute x0 -> x26, waiting for transfers between devices: none -> 90.5 us  [the longest x20 79.8 us: swap(): return lax.ppermute(x, axes, [(i, i ^ bit) for i in range(devices)])]
    dot_general x20 -> x0, matrix products: 86.4 us -> none  [the longest x1 11.4 us: local(): jnp.einsum('hqk,qhd->khd', probs, grad_heads.astype(jnp.float32), precisi...]
    pallas_call x0 -> x4, Pallas kernels: none -> 70.8 us  [the longest x1 56.4 us: local(): pl.pallas_call(functools.partial(layer_kernel, tiles), out_shape=(shp((ow...]
    psum x2 -> x0, blocking collectives: 64.1 us -> none  [the longest x1 56.6 us: local(): gain_total = lax.psum(gain_grad, ('dp', 'seq'))]
    gather x2 -> x0, local copies, waits for them, and re-layouts: 44.4 us -> none  [the longest x1 26.1 us: slot_buffer(): return stacked[jnp.minimum(slot_tiles, tile_count)]]
    reshape x8 -> x0, local copies, waits for them, and re-layouts: 30.3 us -> none  [the longest x4 18.9 us: matrix_of(): tile_stack.reshape(height // tile_side, across // tile_side, tile_side, t...]
    ppermute x0 -> x26, starting transfers between devices: none -> 28.1 us  [the longest x20 15.6 us: swap(): return lax.ppermute(x, axes, [(i, i ^ bit) for i in range(devices)])]
  transfers between devices with their start and end apart: 6 -> 27, of which waited for: 2 -> 16; matrix products, arithmetic and copies ran while one was open for 18% -> 7% of each run, Pallas kernels for 0% -> 1%
where the time goes in v1:
time: 349 us; the launch traced here: 348 us
  waiting for transfers between devices  183 us (52%)
  Pallas kernels  70.8 us (20%)
  starting transfers between devices  28.1 us (8%)
  local copies, waits for them, and re-layouts  26.8 us (8%)
  other arithmetic  16.4 us (5%)
  between operations  16 us (5%)
  matrix products  6.61 us (2%)
    all_gather x1, waiting for transfers between devices, local(): shared = lax.all_gather(weight_slots.astype(BF), axes, axis=0, tiled=True)  92.3 us
    ppermute x20, waiting for transfers between devices, swap(): return lax.ppermute(x, axes, [(i, i ^ bit) for i in range(devices)])  79.8 us
    pallas_call x1, Pallas kernels, local(): pl.pallas_call(functools.partial(layer_kernel, tiles), out_shape=(shp((ow...  56.4 us
    ppermute x20, starting transfers between devices, swap(): return lax.ppermute(x, axes, [(i, i ^ bit) for i in range(devices)])  15.6 us
    unnamed x62, local copies, waits for them, and re-layouts  12.6 us
    pallas_call x1, Pallas kernels, local(): pl.pallas_call(qkv_kernel, out_shape=(shp((own, width), BF), shp((window,...  10.5 us
    convert_element_type x15, other arithmetic, plus(): return (a.astype(F32) + b.astype(F32)).astype(BF)  9.24 us
  transfers between devices with their start and end apart: 27, of which 16 were waited for; matrix products, arithmetic and copies ran while one was open for 7% of the time, Pallas kernels for 1%

profile of v1, /device:TPU:0, one launch (start us, length us, event | category | flops | bytes accessed | tf_op | source)
XLA Modules:
  0.0 347.5 jit_solution(16575501682334333731)
XLA Ops:
  7.2 2.1 convert_element_type.164
  9.4 2.4 collective-permute-start.1
  11.8 4.4 %collective-permute-start = (bf16[256,768]{1,0:T(8,128)(2,1)}, bf16[256,768]{1,0:T(8,128)(2,1)S(1)}, u32[]{:S(2)}, u32[]{:S(2)}) collective-permute-start(bf16[256,768]{1,0:T(8,128)(2,1)} %bitcast.17), channel_id=1, source_target_pairs={{0,2},{1,3},{4,6},{5,7},{8,10},{9,11},{12,14},{13,15},{16,18},{17,... | collective-permute-start | bytes 1179656 | tf_op jit(solution)/shard_map/ppermute | solution.py:563
  22.0 6.5 %collective-permute-done = bf16[256,768]{1,0:T(8,128)(2,1)S(1)} collective-permute-done((bf16[256,768]{1,0:T(8,128)(2,1)}, bf16[256,768]{1,0:T(8,128)(2,1)S(1)}, u32[]{:S(2)}, u32[]{:S(2)}) %collective-permute-start) | collective-permute-done | bytes 393248 | tf_op jit(solution)/shard_map/ppermute | solution.py:563
  29.6 92.3 %all-gather.2.cloned.1.call-done.w_hbm = bf16[448,128,128]{2,1,0:T(8,128)(2,1)} async-done(((bf16[14,128,128]{2,1,0:T(8,128)(2,1)}), bf16[448,128,128]{2,1,0:T(8,128)(2,1)}) %all-gather.2.cloned.1.call-update) | async-done | bytes 14680080 | tf_op jit(solution)/shard_map/all_gather | solution.py:538
  121.9 56.4 %layer.1 = (bf16[256,768]{1,0:T(8,128)(2,1)}, f32[256,768]{1,0:T(8,128)}, bf16[256,768]{1,0:T(8,128)(2,1)}, bf16[768,768]{1,0:T(8,128)(2,1)}, bf16[768,768]{1,0:...) custom-call(s32[448]{0:T(512)} %copy-done.28, ...), custom_call_target="tpu_custom_call" | custom-call | tf_op jit(solution)/shard_map/layer/pallas_call | solution.py:580
  182.3 4.2 %collective-permute-done.3 = f32[256]{0:T(256)S(1)} collective-permute-done((f32[256]{0:T(256)S(1)}, f32[256]{0:T(256)S(1)}, u32[]{:S(2)}, u32[]{:S(2)}) %collective-permute-start.3) | collective-permute-done | bytes 1056 | tf_op jit(solution)/shard_map/ppermute | solution.py:653
  186.5 3.1 copy-done.1
  198.3 10.5 %qkv_grad.1 = (bf16[256,768]{1,0:T(8,128)(2,1)S(1)}, bf16[768,768]{1,0:T(8,128)(2,1)S(1)}, bf16[224,128,128]{2,1,0:T(8,128)(2,1)S(1)}, bf16[224,128,128]{2,1,0:T(8,128)(2,1)}) custom-call(s32[448]{0:T(512)S(1)} %copy-done.16, f32[768,256]{1,0:T(8,128)S(1)} %copy-done.9, ...), custom_call_target="tpu_custom_call", output_to_operand_aliasing={{2}: (10, {}), {3}: (11, {})} | custom-call | tf_op jit(solution)/shard_map/qkv_grad/pallas_call | solution.py:657
  208.8 2.3 slice.129
  211.2 2.1 slice.139
  215.4 5.1 %collective-permute-done.16 = bf16[80,128,128]{2,1,0:T(8,128)(2,1)S(1)} collective-permute-done((bf16[80,128,128]{2,1,0:T(8,128)(2,1)S(1)}, bf16[80,128,128]{2,1,0:T(8,128)(2,1)S(1)}, u32[]{:S(2)}, u32[]{:S(2)}) %collective-permute-start.16) | collective-permute-done | bytes 2621472 | tf_op jit(solution)/shard_map/ppermute | solution.py:669
  230.9 2.4 pre_grad.1
  236.1 27.8 %collective-permute-done.7 = f32[3,768]{1,0:T(4,128)S(1)} collective-permute-done((f32[3,768]{1,0:T(4,128)S(1)}, f32[3,768]{1,0:T(4,128)S(1)}, u32[]{:S(2)}, u32[]{:S(2)}) %collective-permute-start.7) | collective-permute-done | bytes 9248 | tf_op jit(solution)/shard_map/ppermute | solution.py:669
  264.7 2.9 collective-permute-done.8
  268.2 3.1 collective-permute-done.9
  286.7 13.0 %collective-permute-done.23 = bf16[12,128,128]{2,1,0:T(8,128)(2,1)S(1)} collective-permute-done((bf16[12,128,128]{2,1,0:T(8,128)(2,1)S(1)}, bf16[12,128,128]{2,1,0:T(8,128)(2,1)S(1)}, u32[]{:S(2)}, u32[]{:S(2)}) %collective-permute-start.23) | collective-permute-done | bytes 393248 | tf_op jit(solution)/shard_map/ppermute | solution.py:669
  299.9 2.4 collective-permute-start.24
  304.5 2.9 collective-permute-done.24
  312.2 5.2 %collective-permute-done.19 = bf16[10,128,128]{2,1,0:T(8,128)(2,1)S(1)} collective-permute-done((bf16[10,128,128]{2,1,0:T(8,128)(2,1)S(1)}, bf16[10,128,128]{2,1,0:T(8,128)(2,1)S(1)}, u32[]{:S(2)}, u32[]{:S(2)}) %collective-permute-start.19) | collective-permute-done | bytes 327712 | tf_op jit(solution)/shard_map/ppermute | solution.py:669
  317.6 4.0 %collective-permute-done.14 = bf16[12,128,128]{2,1,0:T(8,128)(2,1)S(1)} collective-permute-done((bf16[12,128,128]{2,1,0:T(8,128)(2,1)S(1)}, bf16[12,128,128]{2,1,0:T(8,128)(2,1)S(1)}, u32[]{:S(2)}, u32[]{:S(2)}) %collective-permute-start.14) | collective-permute-done | bytes 393248 | tf_op jit(solution)/shard_map/ppermute | solution.py:669
  321.9 8.9 %collective-permute-done.20 = bf16[5,128,128]{2,1,0:T(8,128)(2,1)S(1)} collective-permute-done((bf16[5,128,128]{2,1,0:T(8,128)(2,1)S(1)}, bf16[5,128,128]{2,1,0:T(8,128)(2,1)S(1)}, u32[]{:S(2)}, u32[]{:S(2)}) %collective-permute-start.20) | collective-permute-done | bytes 163872 | tf_op jit(solution)/shard_map/ppermute | solution.py:669
  330.8 2.8 collective-permute-done.15
  337.7 3.0 fusion.1
  (154 shorter events, 61.8 us)
Async XLA Ops:
  7.2 114.7 %all-gather.2.cloned.1.call-start = ((), (), s32[]{:S(2)}) async-start(), calls=%async_computation | async-start | bytes 15138816 | tf_op jit(solution)/shard_map/all_gather | solution.py:538
  9.4 12.6 %collective-permute-start.1 = (bf16[256,768]{1,0:T(8,128)(2,1)}, bf16[256,768]{1,0:T(8,128)(2,1)S(1)}, u32[]{:S(2)}, u32[]{:S(2)}) collective-permute-start(bf16[256,768]{1,0:T(8,128)(2,1)} %bitcast.16), channel_id=1, source_target_pairs={{0,1},{1,2},{2,3},{4,5},{5,6},{6,7},{8,9},{9,10},{10,11},{12,13},{... | collective-permute-start | bytes 1179656 | tf_op jit(solution)/shard_map/ppermute | solution.py:563
  11.8 16.7 %collective-permute-start = (bf16[256,768]{1,0:T(8,128)(2,1)}, bf16[256,768]{1,0:T(8,128)(2,1)S(1)}, u32[]{:S(2)}, u32[]{:S(2)}) collective-permute-start(bf16[256,768]{1,0:T(8,128)(2,1)} %bitcast.17), channel_id=1, source_target_pairs={{0,2},{1,3},{4,6},{5,7},{8,10},{9,11},{12,14},{13,15},{16,18},{17,... | collective-permute-start | bytes 1179656 | tf_op jit(solution)/shard_map/ppermute | solution.py:563
  179.0 7.4 %collective-permute-start.2 = (f32[512]{0:T(512)S(1)}, f32[512]{0:T(512)S(1)}, u32[]{:S(2)}, u32[]{:S(2)}) collective-permute-start(f32[512]{0:T(512)S(1)} %bitcast.23), channel_id=1, source_target_pairs={{1,0},{2,1},{3,2},{5,4},{6,5},{7,6},{9,8},{10,9},{11,10},{13,12},{... | collective-permute-start | bytes 6152 | tf_op jit(solution)/shard_map/ppermute | solution.py:653
  181.0 5.5 %collective-permute-start.3 = (f32[256]{0:T(256)S(1)}, f32[256]{0:T(256)S(1)}, u32[]{:S(2)}, u32[]{:S(2)}) collective-permute-start(f32[256]{0:T(256)S(1)} %bitcast.24), channel_id=1, source_target_pairs={{2,0},{3,1},{6,4},{7,5},{10,8},{11,9},{14,12},{15,13},{18,16},{19,... | collective-permute-start | bytes 3080 | tf_op jit(solution)/shard_map/ppermute | solution.py:653
  211.1 13.3 %collective-permute-start.11 = (bf16[96,128,128]{2,1,0:T(8,128)(2,1)S(1)}, bf16[96,128,128]{2,1,0:T(8,128)(2,1)S(1)}, u32[]{:S(2)}, u32[]{:S(2)}) collective-permute-start(bf16[96,128,128]{2,1,0:T(8,128)(2,1)S(1)} %slice.129), channel_id=1, source_target_pairs={{0,1},{1,0},{2,3},{3,2},{4,5},{5,4},{6,7},{7,6},{8,9},{9,8},{10,11... | collective-permute-start | bytes 9437192 | tf_op jit(solution)/shard_map/ppermute | solution.py:669
  213.2 7.3 %collective-permute-start.16 = (bf16[80,128,128]{2,1,0:T(8,128)(2,1)S(1)}, bf16[80,128,128]{2,1,0:T(8,128)(2,1)S(1)}, u32[]{:S(2)}, u32[]{:S(2)}) collective-permute-start(bf16[80,128,128]{2,1,0:T(8,128)(2,1)S(1)} %slice.139), channel_id=1, source_target_pairs={{0,1},{1,0},{2,3},{3,2},{4,5},{5,4},{6,7},{7,6},{8,9},{9,8},{10,11... | collective-permute-start | bytes 7864328 | tf_op jit(solution)/shard_map/ppermute | solution.py:669
  215.4 11.8 %collective-permute-start.21 = (bf16[48,128,128]{2,1,0:T(8,128)(2,1)S(1)}, bf16[48,128,128]{2,1,0:T(8,128)(2,1)S(1)}, u32[]{:S(2)}, u32[]{:S(2)}) collective-permute-start(bf16[48,128,128]{2,1,0:T(8,128)(2,1)S(1)} %slice.149), channel_id=1, source_target_pairs={{0,1},{1,0},{2,3},{3,2},{4,5},{5,4},{6,7},{7,6},{8,9},{9,8},{10,11... | collective-permute-start | bytes 4718600 | tf_op jit(solution)/shard_map/ppermute | solution.py:669
  222.9 58.3 %collective-permute-start.17 = (bf16[40,128,128]{2,1,0:T(8,128)(2,1)}, bf16[40,128,128]{2,1,0:T(8,128)(2,1)}, u32[]{:S(2)}, u32[]{:S(2)}) collective-permute-start(bf16[40,128,128]{2,1,0:T(8,128)(2,1)} %slice.169), channel_id=1, source_target_pairs={{0,4},{1,5},{2,6},{3,7},{4,0},{5,1},{6,2},{7,3},{8,12},{9,13},{10,... | collective-permute-start | bytes 3932168 | tf_op jit(solution)/shard_map/ppermute | solution.py:669
  227.2 56.5 %collective-permute-start.12 = (bf16[48,128,128]{2,1,0:T(8,128)(2,1)}, bf16[48,128,128]{2,1,0:T(8,128)(2,1)}, u32[]{:S(2)}, u32[]{:S(2)}) collective-permute-start(bf16[48,128,128]{2,1,0:T(8,128)(2,1)} %slice.161), channel_id=1, source_target_pairs={{0,2},{1,3},{2,0},{3,1},{4,6},{5,7},{6,4},{7,5},{8,10},{9,11},{10,... | collective-permute-start | bytes 4718600 | tf_op jit(solution)/shard_map/ppermute | solution.py:669
  228.9 49.1 %collective-permute-start.22 = (bf16[24,128,128]{2,1,0:T(8,128)(2,1)}, bf16[24,128,128]{2,1,0:T(8,128)(2,1)}, u32[]{:S(2)}, u32[]{:S(2)}) collective-permute-start(bf16[24,128,128]{2,1,0:T(8,128)(2,1)} %slice.177), channel_id=1, source_target_pairs={{0,8},{1,9},{2,10},{3,11},{4,12},{5,13},{6,14},{7,15},{8,0},{9,1},... | collective-permute-start | bytes 2359304 | tf_op jit(solution)/shard_map/ppermute | solution.py:669
  234.6 29.2 %collective-permute-start.7 = (f32[3,768]{1,0:T(4,128)S(1)}, f32[3,768]{1,0:T(4,128)S(1)}, u32[]{:S(2)}, u32[]{:S(2)}) collective-permute-start(f32[3,768]{1,0:T(4,128)S(1)} %fusion.41), channel_id=1, source_target_pairs={{0,2},{1,3},{2,0},{3,1},{4,6},{5,7},{6,4},{7,5},{8,10},{9,11},{10,... | collective-permute-start | bytes 27656 | tf_op jit(solution)/shard_map/ppermute | solution.py:669
  271.3 4.6 %collective-permute-start.10 = (f32[3,768]{1,0:T(4,128)S(1)}, f32[3,768]{1,0:T(4,128)S(1)}, u32[]{:S(2)}, u32[]{:S(2)}) collective-permute-start(f32[3,768]{1,0:T(4,128)S(1)} %add.186), channel_id=1, source_target_pairs={{0,16},{1,17},{2,18},{3,19},{4,20},{5,21},{6,22},{7,23},{8,24},{9,... | collective-permute-start | bytes 27656 | tf_op jit(solution)/shard_map/ppermute | solution.py:669
  272.8 30.1 %collective-permute-start.4 = (bf16[256,768]{1,0:T(8,128)(2,1)S(1)}, bf16[256,768]{1,0:T(8,128)(2,1)S(1)}, u32[]{:S(2)}, u32[]{:S(2)}) collective-permute-start(bf16[256,768]{1,0:T(8,128)(2,1)S(1)} %get-tuple-element.49), channel_id=1, source_target_pairs={{1,0},{2,1},{3,2},{5,4},{6,5},{7,6},{9,8},{10,9},{11,10},{13,12},{... | collective-permute-start | bytes 1179656 | tf_op jit(solution)/shard_map/ppermute | solution.py:698
  275.9 27.1 %collective-permute-start.5 = (bf16[256,768]{1,0:T(8,128)(2,1)S(1)}, bf16[256,768]{1,0:T(8,128)(2,1)S(1)}, u32[]{:S(2)}, u32[]{:S(2)}) collective-permute-start(bf16[256,768]{1,0:T(8,128)(2,1)S(1)} %get-tuple-element.50), channel_id=1, source_target_pairs={{2,0},{3,1},{6,4},{7,5},{10,8},{11,9},{14,12},{15,13},{18,16},{19,... | collective-permute-start | bytes 1179656 | tf_op jit(solution)/shard_map/ppermute | solution.py:697
  279.7 20.0 %collective-permute-start.23 = (bf16[12,128,128]{2,1,0:T(8,128)(2,1)S(1)}, bf16[12,128,128]{2,1,0:T(8,128)(2,1)S(1)}, u32[]{:S(2)}, u32[]{:S(2)}) collective-permute-start(bf16[12,128,128]{2,1,0:T(8,128)(2,1)S(1)} %slice.179), channel_id=1, source_target_pairs={{0,16},{1,17},{2,18},{3,19},{4,20},{5,21},{6,22},{7,23},{8,24},{9,... | collective-permute-start | bytes 1179656 | tf_op jit(solution)/shard_map/ppermute | solution.py:669
  283.1 25.2 %collective-permute-start.18 = (bf16[20,128,128]{2,1,0:T(8,128)(2,1)S(1)}, bf16[20,128,128]{2,1,0:T(8,128)(2,1)S(1)}, u32[]{:S(2)}, u32[]{:S(2)}) collective-permute-start(bf16[20,128,128]{2,1,0:T(8,128)(2,1)S(1)} %slice.171), channel_id=1, source_target_pairs={{0,8},{1,9},{2,10},{3,11},{4,12},{5,13},{6,14},{7,15},{8,0},{9,1},... | collective-permute-start | bytes 1966088 | tf_op jit(solution)/shard_map/ppermute | solution.py:669
  285.8 24.6 %collective-permute-start.13 = (bf16[24,128,128]{2,1,0:T(8,128)(2,1)S(1)}, bf16[24,128,128]{2,1,0:T(8,128)(2,1)S(1)}, u32[]{:S(2)}, u32[]{:S(2)}) collective-permute-start(bf16[24,128,128]{2,1,0:T(8,128)(2,1)S(1)} %slice.163), channel_id=1, source_target_pairs={{0,4},{1,5},{2,6},{3,7},{4,0},{5,1},{6,2},{7,3},{8,12},{9,13},{10,... | collective-permute-start | bytes 2359304 | tf_op jit(solution)/shard_map/ppermute | solution.py:669
  299.9 7.5 %collective-permute-start.24 = (bf16[6,128,128]{2,1,0:T(8,128)(2,1)S(1)}, bf16[6,128,128]{2,1,0:T(8,128)(2,1)S(1)}, u32[]{:S(2)}, u32[]{:S(2)}) collective-permute-start(bf16[6,128,128]{2,1,0:T(8,128)(2,1)S(1)} %slice.181), channel_id=1, source_target_pairs={{0,2},{1,3},{2,0},{3,1},{4,6},{5,7},{6,4},{7,5},{8,10},{9,11},{10,... | collective-permute-start | bytes 589832 | tf_op jit(solution)/shard_map/ppermute | solution.py:669
  307.4 4.7 %collective-permute-start.25 = (bf16[3,128,128]{2,1,0:T(8,128)(2,1)S(1)}, bf16[3,128,128]{2,1,0:T(8,128)(2,1)S(1)}, u32[]{:S(2)}, u32[]{:S(2)}) collective-permute-start(bf16[3,128,128]{2,1,0:T(8,128)(2,1)S(1)} %slice.183), channel_id=1, source_target_pairs={{0,4},{1,5},{2,6},{3,7},{4,0},{5,1},{6,2},{7,3},{8,12},{9,13},{10,... | collective-permute-start | bytes 294920 | tf_op jit(solution)/shard_map/ppermute | solution.py:669
  308.6 8.8 %collective-permute-start.19 = (bf16[10,128,128]{2,1,0:T(8,128)(2,1)S(1)}, bf16[10,128,128]{2,1,0:T(8,128)(2,1)S(1)}, u32[]{:S(2)}, u32[]{:S(2)}) collective-permute-start(bf16[10,128,128]{2,1,0:T(8,128)(2,1)S(1)} %slice.173), channel_id=1, source_target_pairs={{0,2},{1,3},{2,0},{3,1},{4,6},{5,7},{6,4},{7,5},{8,10},{9,11},{10,... | collective-permute-start | bytes 983048 | tf_op jit(solution)/shard_map/ppermute | solution.py:669
  310.7 11.0 %collective-permute-start.14 = (bf16[12,128,128]{2,1,0:T(8,128)(2,1)S(1)}, bf16[12,128,128]{2,1,0:T(8,128)(2,1)S(1)}, u32[]{:S(2)}, u32[]{:S(2)}) collective-permute-start(bf16[12,128,128]{2,1,0:T(8,128)(2,1)S(1)} %slice.165), channel_id=1, source_target_pairs={{0,8},{1,9},{2,10},{3,11},{4,12},{5,13},{6,14},{7,15},{8,0},{9,1},... | collective-permute-start | bytes 1179656 | tf_op jit(solution)/shard_map/ppermute | solution.py:669
  317.5 13.2 %collective-permute-start.20 = (bf16[5,128,128]{2,1,0:T(8,128)(2,1)S(1)}, bf16[5,128,128]{2,1,0:T(8,128)(2,1)S(1)}, u32[]{:S(2)}, u32[]{:S(2)}) collective-permute-start(bf16[5,128,128]{2,1,0:T(8,128)(2,1)S(1)} %slice.175), channel_id=1, source_target_pairs={{0,16},{1,17},{2,18},{3,19},{4,20},{5,21},{6,22},{7,23},{8,24},{9,... | collective-permute-start | bytes 491528 | tf_op jit(solution)/shard_map/ppermute | solution.py:669
  321.8 11.8 %collective-permute-start.15 = (bf16[6,128,128]{2,1,0:T(8,128)(2,1)S(1)}, bf16[6,128,128]{2,1,0:T(8,128)(2,1)S(1)}, u32[]{:S(2)}, u32[]{:S(2)}) collective-permute-start(bf16[6,128,128]{2,1,0:T(8,128)(2,1)S(1)} %slice.167), channel_id=1, source_target_pairs={{0,16},{1,17},{2,18},{3,19},{4,20},{5,21},{6,22},{7,23},{8,24},{9,... | collective-permute-start | bytes 589832 | tf_op jit(solution)/shard_map/ppermute | solution.py:669
  (34 other events, 701.0 us)
Sparse Core Ops, SparseCore 0:
  11.4 110.4 all-gather.1

commit v2 on v1

--- a/solution.py
+++ b/solution.py
@@ -12,7 +12,8 @@
 FF = 3072
 STEP = 3
 SPAN = 512
-CHUNK = 256
+CHUNK = 768
+ADAM_GROUP = 7
 
 select_scale = 0.2
 fraction_slope = 2.0
@@ -23,7 +24,6 @@
 gain_rate = 0.2
 decay_rate = 0.1
 norm_epsilon = 1e-05
-precise = lax.Precision.HIGHEST
 
 BF = jnp.bfloat16
 F32 = jnp.float32
@@ -64,76 +64,96 @@
     return centred * rate, rate
 
 
-def send_tile(tile_ref, dst, keep, send, sem):
-    half = keep.shape[0]
+def send_tile(tile_ref, dst, sums, sem):
+    stay, away = sums
+    half = stay.shape[0]
 
     @pl.when(dst < half)
     def _():
-        pltpu.make_async_copy(tile_ref, keep.at[dst], sem).start()
+        pltpu.make_async_copy(tile_ref, stay.at[dst], sem).start()
 
     @pl.when(dst >= half)
     def _():
-        pltpu.make_async_copy(tile_ref, send.at[dst - half], sem).start()
-
-
-def layer_kernel(
-    tiles,
-    src,
-    dst,
-    scal,
-    thr,
-    tok,
-    gains,
-    dy,
-    segc,
-    segr,
-    w_hbm,
-    out,
-    ghid,
-    gq,
-    gk,
-    gv,
-    nrm_t,
-    wqkv,
-    q0,
-    k0t,
-    part0,
-    mask0,
-    colsum,
-    small,
-    keep,
-    send,
-    wall,
-    nrm,
-    q_s,
-    q_e,
-    k_s,
-    v_s,
-    kt_s,
-    vt_s,
-    bias,
-    gsh,
-    probs,
-    mixt,
-    mixb,
-    mixbt,
-    wout,
-    hid,
-    xhat,
-    nm,
-    nmt,
-    acc,
-    gmid,
-    g_s,
-    gt_s,
-    wu,
-    wd,
-    stage,
-    zero,
-    wsem,
-    gsem,
-    zsem,
-):
+        pltpu.make_async_copy(tile_ref, away.at[dst - half], sem).start()
+
+
+def wait_tiles(stage_ref, sums, sem):
+    pltpu.make_async_copy(stage_ref, sums[0].at[pl.ds(0, stage_ref.shape[0])], sem).wait()
+
+
+def mm3(a, b):
+    (ah, al), (bh, bl) = a, b
+    return mm(jnp.concatenate([ah, ah, al], axis=1), jnp.concatenate([bh, bl, bh], axis=0))
+
+
+def mm3_nt(a, b):
+    (ah, al), (bh, bl) = a, b
+    return mm_nt(jnp.concatenate([ah, ah, al], axis=1), jnp.concatenate([bh, bl, bh], axis=1))
+
+
+def lane_half(shape, second):
+    lane = lax.broadcasted_iota(jnp.int32, shape, 1)
+    return (lane >= HD) if second else (lane < HD)
+
+
+def keep_half(x, second):
+    return jnp.where(lane_half(x.shape, second), x, jnp.zeros_like(x))
+
+
+def norm_parts(x):
+    centred = x - jnp.mean(x, axis=-1, keepdims=True)
+    rate = lax.rsqrt(jnp.mean(centred * centred, axis=-1, keepdims=True) + norm_epsilon)
+    return centred * rate, rate
+
+
+def send_tile(tile_ref, dst, sums, sem):
+    stay, away = sums
+    half = stay.shape[0]
+
+    @pl.when(dst < half)
+    def _():
+        pltpu.make_async_copy(tile_ref, stay.at[dst], sem).start()
+
+    @pl.when(dst >= half)
+    def _():
+        pltpu.make_async_copy(tile_ref, away.at[dst - half], sem).start()
+
+
+def wait_tiles(stage_ref, sums, sem):
+    pltpu.make_async_copy(stage_ref, sums[0].at[pl.ds(0, stage_ref.shape[0])], sem).wait()
+
+
+def mm3(a, b):
+    (ah, al), (bh, bl) = a, b
+    return mm(ah, bh) + (mm(ah, bl) + mm(al, bh))
+
+
+def mm3_nt(a, b):
+    (ah, al), (bh, bl) = a, b
+    return mm_nt(ah, bh) + (mm_nt(ah, bl) + mm_nt(al, bh))
+
+
+def layer_kernel(tiles, sizes, *refs):
+    (src, dst, scal, thr, tok, gains, dy, segc, segr), refs = refs[:9], refs[9:]
+    w_parts, refs = refs[: len(sizes)], refs[len(sizes) :]
+    (out_h, ghid_h, gq_h, gk_h, gv_h, nrm_t_h, wqkv_h, q0_h, k0t_h, part0_h, mask0_h, colsum, small, *sums), refs = (
+        refs[:15],
+        refs[15:],
+    )
+    (out, ghid, gq, gk, gv, nrm_t, wqkv, part0, mask0), refs = refs[:9], refs[9:]
+    (wall, nrm, q_s, q_e, k_s, v_s, kt_s, vt_s, bias, gsh, probs, mixt, mixb, mixbt, wout, hid, xhat), refs = (
+        refs[:17],
+        refs[17:],
+    )
+    nm, nmt, acc, gmid, g_s, gt_s, wu, wd, stage, zero, wsem, gsem, zsem, osem = refs
+
+    writes = []
+
+    def write(ref, target):
+        copy = pltpu.make_async_copy(ref, target, osem.at[len(writes)])
+        copy.start()
+        writes.append(copy)
+
     n_qkv, n_out, n_up, n_down = tiles
     width = tok.shape[1]
     own = dy.shape[0]
@@ -142,16 +162,20 @@
     side = wall.shape[-1]
     dt = width // side
     pairs = width // side
-    total_slots = 2 * keep.shape[0]
-    load = pltpu.make_async_copy(w_hbm, wall, wsem)
-    load.start()
+    total_slots = 2 * sums[0].shape[0]
+    loads = []
+    at = 0
+    for index, (part, size) in enumerate(zip(w_parts, sizes)):
+        loads.append(pltpu.make_async_copy(part, wall.at[pl.ds(at, size)], wsem.at[index]))
+        loads[-1].start()
+        at += size
     zero[...] = jnp.zeros_like(zero)
     tile_count = n_qkv + n_out + n_up + n_down
     empty = total_slots - tile_count
 
     @pl.loop(0, empty)
     def _(e):
-        send_tile(zero, dst[tile_count + e], keep, send, zsem)
+        send_tile(zero, dst[tile_count + e], sums, zsem)
 
     gain_pre = gains[0:1, :]
     gain_mid = gains[1:2, :]
@@ -164,7 +188,9 @@
         nrm[rows, :] = value
         nrm_t[:, rows] = value.T
 
-    load.wait()
+    write(nrm_t, nrm_t_h)
+    for load in loads:
+        load.wait()
     per_row = 3 * dt
 
     @pl.loop(0, 3 * dt // 2)
@@ -175,6 +201,7 @@
                     src[i * per_row + 2 * j + jj]
                 ]
 
+    write(wqkv, wqkv_h)
     for i in range(dt):
         for j in range(dt):
             wout[i * side : (i + 1) * side, j * side : (j + 1) * side] = wall[src[n_qkv + i * dt + j]]
@@ -208,8 +235,8 @@
         vt_s[2 * j] = got_t[:side, :]
         vt_s[2 * j + 1] = got_t[side:, :]
 
-    q0[...] = q_s[0]
-    k0t[...] = kt_s[0]
+    write(q_s.at[0], q0_h)
+    write(kt_s.at[0], k0t_h)
 
     valid_len = scal[0]
     start = scal[1]
@@ -238,6 +265,7 @@
     allowed = strict | (same & (key_at == query_at + back))
     bias[...] = jnp.where(allowed, -shadow, -1e30)
     mask0[...] = jnp.where(strict & (s_own > 0.0), 1.0, 0.0).astype(BF)
+    write(mask0, mask0_h)
     column_total = prefix + jnp.sum(chosen, axis=1, keepdims=True)
     key_col = lax.broadcasted_iota(jnp.int32, (window, 1), 0)
     key_pos = key_col + (start - back)
@@ -251,13 +279,16 @@
     def _(p):
         q2 = q_s[p]
         k2 = k_s[p]
+        both = [mm_nt(k2, keep_half(q2, hh == 1)) for hh in range(2)]
+        prs = []
         for hh in range(2):
-            s = mm_nt(k2, keep_half(q2, hh == 1)) + bias[...]
+            s = both[hh] + bias[...]
             e = jnp.exp(s - jnp.max(s, axis=0, keepdims=True))
-            pr = (e * (1.0 / jnp.sum(e, axis=0, keepdims=True))).astype(BF)
-            probs[2 * p + hh] = pr
-            vt = vt_s[p, hh * HD : (hh + 1) * HD, :]
-            mixt[pl.ds(pl.multiple_of(p * side + hh * HD, HD), HD), :] = mm(vt, pr)
+            prs.append((e * (1.0 / jnp.sum(e, axis=0, keepdims=True))).astype(BF))
+        for hh in range(2):
+            probs[2 * p + hh] = prs[hh]
+        mixed = [mm(vt_s[p, hh * HD : (hh + 1) * HD, :], prs[hh]) for hh in range(2)]
+        mixt[pl.ds(pl.multiple_of(p * side, side), side), :] = jnp.concatenate(mixed, axis=0)
 
     mixbt[...] = mixt[...].astype(BF)
     mixb[...] = mixbt[...].T
@@ -300,7 +331,7 @@
 
         @pl.when(c >= 2)
         def _():
-            pltpu.make_async_copy(stage.at[slot], keep.at[pl.ds(0, per_chunk)], gsem.at[slot]).wait()
+            wait_tiles(stage.at[slot], sums, gsem.at[slot])
 
         g_down = mm(active.T, dy[...]).astype(BF)
         for ii in range(cw):
@@ -316,14 +347,15 @@
             for j in range(dt):
                 at = ii * dt + j
                 t = n_qkv + n_out + n_up + (cw * c + ii) * dt + j
-                send_tile(stage.at[slot, at], dst[t], keep, send, gsem.at[slot])
+                send_tile(stage.at[slot, at], dst[t], sums, gsem.at[slot])
         for i in range(dt):
             for jj in range(cw):
                 at = cw * dt + i * cw + jj
                 t = n_qkv + n_out + i * f_tiles + cw * c + jj
-                send_tile(stage.at[slot, at], dst[t], keep, send, gsem.at[slot])
+                send_tile(stage.at[slot, at], dst[t], sums, gsem.at[slot])
 
     out[...] = (hid[...] + acc[...]).astype(BF)
+    write(out, out_h)
     hat = xhat[...]
     gm = gmid[...]
     small[0:1, :] = jnp.sum(gm * hat, axis=0, keepdims=True)
@@ -334,6 +366,7 @@
         - hat * jnp.mean(scaled * hat, axis=-1, keepdims=True)
     )
     ghid[...] = gh
+    write(ghid, ghid_h)
     gb = gh.astype(BF)
     gmix = mm_nt(gb, wout[...]).astype(BF)
     for p in range(pairs):
@@ -341,7 +374,7 @@
     gt_s[...] = gmix.T
 
     for slot in range(2):
-        pltpu.make_async_copy(stage.at[slot], keep.at[pl.ds(0, per_chunk)], gsem.at[slot]).wait()
+        wait_tiles(stage.at[slot], sums, gsem.at[slot])
     half_out = dt // 2
     for part in range(2):
         g_out = mm(mixbt[part * half_out * side : (part + 1) * half_out * side, :], gb).astype(BF)
@@ -351,7 +384,7 @@
         for i in range(half_out):
             for j in range(dt):
                 t = n_qkv + (part * half_out + i) * dt + j
-                send_tile(stage.at[part, i * dt + j], dst[t], keep, send, gsem.at[part])
+                send_tile(stage.at[part, i * dt + j], dst[t], sums, gsem.at[part])
 
     gsh[...] = jnp.zeros_like(gsh)
 
@@ -361,90 +394,136 @@
         q2 = q_s[p]
         v2 = v_s[p]
         later = jnp.where(p > 0, 1.0, 0.0)
-        dk = jnp.zeros((window, side), F32)
-        dv = jnp.zeros((window, side), F32)
-        dqs = []
+        halves = [keep_half(g2, hh == 1) for hh in range(2)]
+        dps = [mm_nt(v2, halves[hh]) for hh in range(2)]
+        prs = [probs[2 * p + hh] for hh in range(2)]
+        rows = pl.ds(pl.multiple_of(p * side, side), side)
+        product = gt_s[rows, :].astype(F32) * mixt[rows, :]
+        dls = []
         for hh in range(2):
-            rows = pl.ds(pl.multiple_of(p * side + hh * HD, HD), HD)
-            delta = jnp.sum(gt_s[rows, :].astype(F32) * mixt[rows, :], axis=0, keepdims=True)
-            gm2 = keep_half(g2, hh == 1)
-            pr = probs[2 * p + hh]
-            dl = pr.astype(F32) * (mm_nt(v2, gm2) - delta)
-            gsh[...] += dl
-            dv = dv + mm(pr, gm2)
-            gs = dl.astype(BF)
-            dq = mm(kt_s[p, hh * HD : (hh + 1) * HD, :], gs)
-            dk_h = mm(gs, keep_half(q2, hh == 1))
-            if hh == 0:
-                dq = dq * later
-                dk_h = dk_h * later
-
-                @pl.when(p == 0)
-                def _():
-                    part0[...] = dl
-
-            dqs.append(dq)
-            dk = dk + dk_h
+            delta = jnp.sum(product[hh * HD : (hh + 1) * HD, :], axis=0, keepdims=True)
+            dls.append(prs[hh].astype(F32) * (dps[hh] - delta))
+        gsh[...] += dls[0] + dls[1]
+
+        @pl.when(p == 0)
+        def _():
+            part0[...] = dls[0]
+
+        gs = [(dls[0] * later).astype(BF), dls[1].astype(BF)]
+        dv = mm(prs[0], halves[0]) + mm(prs[1], halves[1])
+        dk = mm(gs[0], keep_half(q2, False)) + mm(gs[1], keep_half(q2, True))
+        dqs = [mm(kt_s[p, hh * HD : (hh + 1) * HD, :], gs[hh]) for hh in range(2)]
         cols = pl.ds(pl.multiple_of(p * side, side), side)
         gq[:, cols] = (jnp.concatenate(dqs, axis=0) * 0.125).T.astype(BF)
         gk[:, cols] = dk.astype(BF)
         gv[:, cols] = dv.astype(BF)
 
+    write(gq, gq_h)
+    write(gk, gk_h)
+    write(gv, gv_h)
     ones = jnp.ones((8, own), BF)
     high, rest = split(-gsh[...])
     colsum[...] = mm_nt(ones, high) + mm_nt(ones, rest)
     after = jnp.where(tri_row > tri_col, 1.0, 0.0).astype(BF)
     part0[...] += select_scale * mask0[...].astype(F32) * (mm(high, after) + mm(rest, after))
+    write(part0, part0_h)
 
     for part in range(2):
-        pltpu.make_async_copy(
-            stage.at[part, pl.ds(0, half_out * dt)], keep.at[pl.ds(0, half_out * dt)], gsem.at[part]
-        ).wait()
-    pltpu.make_async_copy(keep.at[pl.ds(0, empty)], keep.at[pl.ds(0, empty)], zsem).wait()
-
-
-def qkv_kernel(
-    dst, part0, mask0, suffix, q0, k0t, gq, gk, gv, nrm_t, keep_in, send_in, gq_out, gk_out, keep, send, stage, gsem
-):
+        wait_tiles(stage.at[part, pl.ds(0, half_out * dt)], sums, gsem.at[part])
+    pltpu.make_async_copy(sums[0].at[pl.ds(0, empty)], sums[0].at[pl.ds(0, empty)], zsem).wait()
+    for copy in writes:
+        copy.wait()
+
+
+def load_all(pairs, sem):
+    copies = [pltpu.make_async_copy(a, b, sem.at[i]) for i, (a, b) in enumerate(pairs)]
+    for copy in copies:
+        copy.start()
+    return copies
+
+
+def qkv_kernel(dst, gq_h, gk_h, gv_h, nrm_h, stay_in, away_in, stay, away, gq, gk, gv, nrm_t, stage, lsem, gsem):
     own, width = gq.shape
-    window = gk.shape[0]
     side = stage.shape[-1]
     dt = width // side
+    back = gk.shape[0] - own
+    sums = (stay, away)
+    copies = load_all([(nrm_h, nrm_t), (gv_h, gv), (gk_h, gk), (gq_h, gq)], lsem)
+    copies[0].wait()
+    count = 0
+    for which, copy in ((2, copies[1]), (1, copies[2]), (0, copies[3])):
+        copy.wait()
+        bounds = [(c, c + 2) for c in range(0, dt, 2)] if which == 2 else [(1, 2)] + [(c, c + 2) for c in range(2, dt, 2)]
+        for lo, hi in bounds:
+            cols = slice(lo * side, hi * side)
+            if which == 0:
+                g = mm(nrm_t[:, back:], gq[:, cols])
+            else:
+                g = mm(nrm_t[...], (gk if which == 1 else gv)[:, cols])
+            g = g.astype(BF)
+            for i in range(dt):
+                for j in range(lo, hi):
+                    stage[count] = g[i * side : (i + 1) * side, (j - lo) * side : (j - lo + 1) * side]
+                    send_tile(stage.at[count], dst[i * 3 * dt + which * dt + j], sums, gsem)
+                    count += 1
+    wait_tiles(stage, sums, gsem)
+
+
+def head_kernel(
+    dst, suffix, part0_h, mask0_h, q0_h, k0t_h, gq_h, gk_h, nrm_h, stay_in, away_in, gq_out, gk_out, stay, away,
+    part0, mask0, q0, k0t, gq, gk, nrm_t, stage, lsem, gsem,
+):
+    own, side = gq.shape
+    window = gk.shape[0]
     back = window - own
+    dt = nrm_t.shape[0] // side
+    sums = (stay, away)
+    head = pl.ds(0, side)
+    copies = load_all(
+        [
+            (part0_h, part0),
+            (mask0_h, mask0),
+            (k0t_h, k0t),
+            (q0_h, q0),
+            (gq_h.at[:, head], gq),
+            (gk_h.at[:, head], gk),
+            (nrm_h, nrm_t),
+        ],
+        lsem,
+    )
     column = jnp.broadcast_to(suffix[0:1, :], (side, window)).T
     column = jnp.concatenate([column] * (own // side), axis=1)
+    for copy in copies[:-1]:
+        copy.wait()
     gs = (part0[...] + select_scale * mask0[...].astype(F32) * column).astype(BF)
     dq = (mm(k0t[0:HD, :], gs) * 0.125).T
     dk = mm(gs, keep_half(q0[...], False)).astype(BF)
-    gq_out[...] = gq[...]
-    gk_out[...] = gk[...]
-    gq_out[:, 0:side] = gq[:, 0:side] + jnp.concatenate([dq, jnp.zeros_like(dq)], axis=1).astype(BF)
-    gk_out[:, 0:side] = gk[:, 0:side] + dk
-
-    for which in range(3):
-        for jc in range(dt // 2):
-            cols = slice(2 * jc * side, 2 * (jc + 1) * side)
-            if which == 0:
-                g = mm(nrm_t[:, back:], gq_out[:, cols])
-            elif which == 1:
-                g = mm(nrm_t[...], gk_out[:, cols])
-            else:
-                g = mm(nrm_t[...], gv[:, cols])
-            g = g.astype(BF)
-            for i in range(dt):
-                for jj in range(2):
-                    j = which * dt + 2 * jc + jj
-                    t = i * 3 * dt + j
-                    stage[t] = g[i * side : (i + 1) * side, jj * side : (jj + 1) * side]
-                    send_tile(stage.at[t], dst[t], keep, send, gsem)
-    count = 3 * dt * dt
-    pltpu.make_async_copy(stage, keep.at[pl.ds(0, count)], gsem).wait()
-
-
-def pre_kernel(tok, gq, gk, gv, wqkv, far, near, mine, small):
+    gq_new = gq[...] + jnp.concatenate([dq, jnp.zeros_like(dq)], axis=1).astype(BF)
+    gk_new = gk[...] + dk
+    gq_out[...] = gq_new
+    gk_out[...] = gk_new
+    copies[-1].wait()
+    g_q = mm(nrm_t[:, back:], gq_new).astype(BF)
+    g_k = mm(nrm_t[...], gk_new).astype(BF)
+    for which, g in ((0, g_q), (1, g_k)):
+        for i in range(dt):
+            stage[which * dt + i] = g[i * side : (i + 1) * side, :]
+            send_tile(stage.at[which * dt + i], dst[i * 3 * dt + which * dt], sums, gsem)
+    wait_tiles(stage, sums, gsem)
+
+
+def pre_kernel(tok, gq_head, gk_head, gq_h, gk_h, gv_h, wqkv_h, far, near, mine, small, gq, gk, gv, wqkv, lsem):
     own, width = gq.shape
     window = gk.shape[0]
-    back = window - own
+    side = gq_head.shape[1]
+    rest = pl.ds(side, width - side)
+    copies = load_all(
+        [(wqkv_h, wqkv), (gk_h.at[:, rest], gk.at[:, rest]), (gv_h, gv), (gq_h.at[:, rest], gq.at[:, rest])], lsem
+    )
+    gq[:, 0:side] = gq_head[...]
+    gk[:, 0:side] = gk_head[...]
+    for copy in copies:
+        copy.wait()
     total = jnp.zeros((1, width), F32)
     for b in range(window // own):
         rows = slice(b * own, (b + 1) * own)
@@ -472,15 +551,35 @@
     )
 
 
-def rotated_adam(grad_slots, first, second, left, right, weight, correction):
-    turned = jnp.einsum("sji,sjk->sik", left, grad_slots, precision=precise)
-    turned = jnp.einsum("sik,skl->sil", turned, right, precision=precise)
-    first_new = first_decay * first + (1.0 - first_decay) * turned
-    second_new = second_decay * second + (1.0 - second_decay) * turned * turned
-    norm_step = first_new / correction / (jnp.sqrt(second_new / correction) + adam_epsilon)
-    back = jnp.einsum("sik,skl->sil", left, norm_step, precision=precise)
-    back = jnp.einsum("sil,sjl->sij", back, right, precision=precise)
-    return (first_new, second_new, weight - weight_rate * back - weight_rate * decay_rate * weight)
+def adam_kernel(correction, parts, *refs):
+    grads, refs = refs[: 2 * len(parts)], refs[2 * len(parts) :]
+    holds, first, second, left, right, weight, first_out, second_out, weight_out = refs
+    slots = []
+    for index, (at, size, _) in enumerate(parts):
+        slots += [(at + k, grads[2 * index], grads[2 * index + 1], k) for k in range(size)]
+    for low in range(0, len(slots), ADAM_GROUP):
+        group = slots[low : low + ADAM_GROUP]
+        rights, turned, steps, undone = {}, {}, {}, {}
+        for slot, mine, other, k in group:
+            grad = mine[k].astype(F32) + other[k].astype(F32)
+            grad = jnp.where(holds[slot] > 0, grad, 0.0)
+            rights[slot] = split(right[slot])
+            turned[slot] = mm3(split(grad), rights[slot])
+        for slot, *_ in group:
+            turned[slot] = mm3(split(left[slot].T), split(turned[slot]))
+        for slot, *_ in group:
+            t = turned[slot]
+            first_new = first_decay * first[slot] + (1.0 - first_decay) * t
+            second_new = second_decay * second[slot] + (1.0 - second_decay) * t * t
+            first_out[slot] = first_new
+            second_out[slot] = second_new
+            steps[slot] = first_new / correction / (jnp.sqrt(second_new / correction) + adam_epsilon)
+        for slot, *_ in group:
+            undone[slot] = mm3_nt(split(steps[slot]), rights[slot])
+        for slot, *_ in group:
+            back = mm3(split(left[slot]), split(undone[slot]))
+            w = weight[slot]
+            weight_out[slot] = w - weight_rate * back - weight_rate * decay_rate * w
 
 
 def bit_plan(devices, per_device):
@@ -501,6 +600,14 @@
             plan.append((at, size, order))
             at += size
     return first, plan
+
+
+def gather_parts(devices, per_device):
+    if devices != 32 or per_device < 8:
+        return per_device, []
+    size = per_device * 2 // 7
+    first = per_device - 2 * size
+    return first, [(first, size, (16, 8, 4, 2, 1)), (first + size, size, (16, 8, 2, 4, 1))]
 
 
 def local(
@@ -535,7 +642,8 @@
     back = SPAN
     window = back + own
 
-    shared = lax.all_gather(weight_slots.astype(BF), axes, axis=0, tiled=True)
+    def swap(x, bit):
+        return lax.ppermute(x, axes, [(i, i ^ bit) for i in range(devices)])
 
     slot_ids = jnp.arange(slot_total, dtype=jnp.int32)
     position = jnp.sum(
@@ -555,13 +663,22 @@
         here = at * spread + index * size + (inner - at)
         place = jnp.where((inner >= at) & (inner < at + size), here, place)
     dst = place + jnp.where((apart & first_bit) != 0, half, 0)
-    src = position
+    by_gather, gather_plan = gather_parts(devices, per_device)
+    src = owner * by_gather + inner
+    base = devices * by_gather
+    for at, size, order in gather_plan:
+        index = jnp.zeros_like(position)
+        for bit in reversed(order):
+            index = index * 2 + ((apart & bit) != 0).astype(jnp.int32)
+        here = base + index * size + (inner - at)
+        src = jnp.where((inner >= at) & (inner < at + size), here, src)
+        base += devices * size
 
     mine_tok = tokens[0]
-    pieces = []
+    seen = []
     for step in range(back // own, 0, -1):
-        pieces.append(lax.ppermute(mine_tok, "seq", [(i, i + step) for i in range(n_seq - step)]))
-    tok = jnp.concatenate(pieces + [mine_tok], axis=0)
+        seen.append(lax.ppermute(mine_tok, "seq", [(i, i + step) for i in range(n_seq - step)]))
+    tok = jnp.concatenate(seen + [mine_tok], axis=0)
     start = seq_at * own
     seg_window = lax.dynamic_slice_in_dim(
         jnp.concatenate([jnp.full((back,), -1, jnp.int32), segment_ids[0]]), start, window
@@ -569,16 +686,28 @@
     valid_len = length - pad_lengths[0]
     scal = jnp.stack([valid_len, start, (seq_at == n_seq - 1).astype(jnp.int32)])
 
-    hbm = pl.BlockSpec(memory_space=pl.ANY)
+    segc, segr = seg_window[:, None], seg_window[None, :]
+
+    rounded = weight_slots.astype(BF)
+    pieces = [lax.all_gather(rounded[:by_gather], axes, axis=0, tiled=True)]
+    held = [rounded[at : at + size] for at, size, _ in gather_plan]
+    for step in range(len(gather_plan[0][2]) - 2 if gather_plan else 0):
+        held = [jnp.concatenate([h, swap(h, o[2][step])], axis=0) for h, o in zip(held, gather_plan)]
+        if step == 1:
+            held, tok, src, dst, scal, segc, segr = lax.optimization_barrier((held, tok, src, dst, scal, segc, segr))
+    for h, (_, _, order) in zip(held, gather_plan):
+        two = [h, swap(h, order[-2])]
+        pieces += two + [swap(x, order[-1]) for x in two]
+    sizes = [p.shape[0] for p in pieces]
+
+    hbm = pl.BlockSpec(memory_space=pltpu.HBM)
     vm = pl.BlockSpec(memory_space=VMEM)
     sm = pl.BlockSpec(memory_space=SMEM)
     shp = jax.ShapeDtypeStruct
-    tile_buffer = shp((half, side, side), BF)
-
-
+    sums_shape = shp((half, side, side), BF)
     per_chunk = 2 * (CHUNK // side) * dt
     outs = pl.pallas_call(
-        functools.partial(layer_kernel, tiles),
+        functools.partial(layer_kernel, tiles, sizes),
         out_shape=(
             shp((own, width), BF),
             shp((own, width), F32),
@@ -593,12 +722,21 @@
             shp((window, own), BF),
             shp((8, window), F32),
             shp((8, width), F32),
-            tile_buffer,
-            tile_buffer,
+            sums_shape,
+            sums_shape,
         ),
-        in_specs=[sm] * 4 + [vm] * 5 + [hbm],
-        out_specs=tuple([vm] * 13 + [hbm] * 2),
+        in_specs=[sm] * 4 + [vm] * 5 + [hbm] * len(sizes),
+        out_specs=tuple([hbm] * 11 + [vm] * 2 + [hbm] * 2),
         scratch_shapes=[
+            VMEM((own, width), BF),
+            VMEM((own, width), F32),
+            VMEM((own, width), BF),
+            VMEM((window, width), BF),
+            VMEM((window, width), BF),
+            VMEM((width, window), BF),
+            VMEM((width, 3 * width), BF),
+            VMEM((window, own), F32),
+            VMEM((window, own), BF),
             VMEM((slot_total, side, side), BF),
             VMEM((window, width), BF),
             VMEM((dt, own, side), BF),
@@ -626,9 +764,10 @@
             VMEM((CHUNK, width), BF),
             VMEM((2, per_chunk, side, side), BF),
             VMEM((side, side), BF),
-            pltpu.SemaphoreType.DMA,
+            pltpu.SemaphoreType.DMA((len(sizes),)),
             pltpu.SemaphoreType.DMA((2,)),
             pltpu.SemaphoreType.DMA,
+            pltpu.SemaphoreType.DMA((11,)),
         ],
         compiler_params=pltpu.CompilerParams(vmem_limit_bytes=60 << 20),
         name="layer",
@@ -640,46 +779,69 @@
         tok,
         gains,
         out_grad[0],
-        seg_window[:, None],
-        seg_window[None, :],
-        shared,
-    )
-    (output, ghid, gq, gk, gv, nrm_t, wqkv, q0, k0t, part0, mask0, colsum, small, keep, send) = outs
-
-    sums = colsum[0]
+        segc,
+        segr,
+        *pieces,
+    )
+    (output, ghid, gq, gk, gv, nrm_t, wqkv, q0, k0t, part0, mask0, colsum, small, stay, away) = outs
+
+    columns = colsum[0]
     suffix = jnp.zeros((window,), F32)
     for step in range(1, back // own + 1):
         reach = window - step * own
-        got = lax.ppermute(sums[:reach], "seq", [(i, i - step) for i in range(step, n_seq)])
+        got = lax.ppermute(columns[:reach], "seq", [(i, i - step) for i in range(step, n_seq)])
         suffix = suffix + jnp.concatenate([jnp.zeros((step * own,), F32), got])
     suffix = jnp.broadcast_to(suffix[None, :], (8, window))
 
-    gq, gk, keep, send = pl.pallas_call(
+    main_tiles = tiles[0] - 2 * dt
+    stay, away = pl.pallas_call(
         qkv_kernel,
-        out_shape=(shp((own, width), BF), shp((window, width), BF), tile_buffer, tile_buffer),
-        in_specs=[sm] + [vm] * 9 + [hbm] * 2,
+        out_shape=(sums_shape, sums_shape),
+        in_specs=[sm] + [hbm] * 6,
+        out_specs=(hbm, hbm),
+        scratch_shapes=[
+            VMEM((own, width), BF),
+            VMEM((window, width), BF),
+            VMEM((window, width), BF),
+            VMEM((width, window), BF),
+            VMEM((main_tiles, side, side), BF),
+            pltpu.SemaphoreType.DMA((4,)),
+            pltpu.SemaphoreType.DMA,
+        ],
+        input_output_aliases={5: 0, 6: 1},
+        compiler_params=pltpu.CompilerParams(vmem_limit_bytes=60 << 20),
+        cost_estimate=pl.CostEstimate(
+            flops=2 * (2 * window + own) * width * width, bytes_accessed=8 << 20, transcendentals=0
+        ),
+        name="qkv_grad",
+    )(dst, gq, gk, gv, nrm_t, stay, away)
+    gq_head, gk_head, stay, away = pl.pallas_call(
+        head_kernel,
+        out_shape=(shp((own, side), BF), shp((window, side), BF), sums_shape, sums_shape),
+        in_specs=[sm, vm] + [hbm] * 9,
         out_specs=(vm, vm, hbm, hbm),
-        scratch_shapes=[VMEM((tiles[0], side, side), BF), pltpu.SemaphoreType.DMA],
-        input_output_aliases={10: 2, 11: 3},
-        compiler_params=pltpu.CompilerParams(vmem_limit_bytes=40 << 20),
-        name="qkv_grad",
-    )(dst, part0, mask0, suffix, q0, k0t, gq, gk, gv, nrm_t, keep, send)
-
-    def swap(x, bit):
-        return lax.ppermute(x, axes, [(i, i ^ bit) for i in range(devices)])
+        scratch_shapes=[
+            VMEM((window, own), F32),
+            VMEM((window, own), BF),
+            VMEM((own, side), BF),
+            VMEM((side, window), BF),
+            VMEM((own, side), BF),
+            VMEM((window, side), BF),
+            VMEM((width, window), BF),
+            VMEM((2 * dt, side, side), BF),
+            pltpu.SemaphoreType.DMA((7,)),
+            pltpu.SemaphoreType.DMA,
+        ],
+        input_output_aliases={9: 2, 10: 3},
+        compiler_params=pltpu.CompilerParams(vmem_limit_bytes=60 << 20),
+        cost_estimate=pl.CostEstimate(flops=1 << 30, bytes_accessed=4 << 20, transcendentals=0),
+        name="head_grad",
+    )(dst, suffix, part0, mask0, q0, k0t, gq, gk, nrm_t, stay, away)
 
     def plus(a, b):
         return (a.astype(F32) + b.astype(F32)).astype(BF)
 
-    parts = []
-    for at, size, order in plan:
-        rows = slice(at * spread, (at + size) * spread)
-        parts.append(plus(keep[rows], swap(send[rows], first_bit)))
-    for step in range(len(plan[0][2])):
-        for which, (_, _, order) in enumerate(plan):
-            middle = parts[which].shape[0] // 2
-            parts[which] = plus(parts[which][:middle], swap(parts[which][middle:], order[step]))
-    owned_grad = jnp.concatenate(parts, axis=0).astype(F32)
+    got = swap(away, first_bit)
 
     far, near, mine, small_pre = pl.pallas_call(
         pre_kernel,
@@ -689,13 +851,66 @@
             shp((own, width), F32),
             shp((8, width), F32),
         ),
-        in_specs=[vm] * 5,
+        in_specs=[vm] * 3 + [hbm] * 4,
         out_specs=tuple([vm] * 4),
-        compiler_params=pltpu.CompilerParams(vmem_limit_bytes=40 << 20),
+        scratch_shapes=[
+            VMEM((own, width), BF),
+            VMEM((window, width), BF),
+            VMEM((window, width), BF),
+            VMEM((width, 3 * width), BF),
+            pltpu.SemaphoreType.DMA((4,)),
+        ],
+        compiler_params=pltpu.CompilerParams(vmem_limit_bytes=30 << 20),
+        cost_estimate=pl.CostEstimate(
+            flops=2 * (2 * window + own) * width * width, bytes_accessed=10 << 20, transcendentals=0
+        ),
         name="pre_grad",
-    )(tok, gq, gk, gv, wqkv)
-    far = lax.ppermute(far, "seq", [(i, i - 2) for i in range(2, n_seq)])
-    near = lax.ppermute(near, "seq", [(i, i - 1) for i in range(1, n_seq)])
+    )(tok, gq_head, gk_head, gq, gk, gv, wqkv)
+    row_at = lax.axis_index("dp")
+    spots = jnp.arange(width, dtype=jnp.int32)
+    totals = jnp.stack([small_pre[0], small[0], jnp.where(spots == row_at, small[1], 0.0)])
+    totals = jnp.pad(totals.reshape(3 * dt, side), ((0, side // 2 - 3 * dt), (0, 0)))
+    got, totals = lax.optimization_barrier((got, totals))
+    gathered = lax.all_gather(totals, axes)
+    steps = len(plan[0][2])
+    sent = []
+    for at, size, _ in plan:
+        rows = slice(at * spread + size * spread // 2, (at + size) * spread)
+        got, piece = lax.optimization_barrier((got, plus(stay[rows], got[rows])))
+        sent.append(piece)
+    came = [swap(piece, order[0]) for piece, (_, _, order) in zip(sent, plan)]
+    left = []
+    for at, size, _ in plan:
+        rows = slice(at * spread, at * spread + size * spread // 2)
+        left.append(plus(stay[rows], got[rows]))
+    for step in range(1, steps):
+        for which, (_, _, order) in enumerate(plan):
+            middle = left[which].shape[0] // 2
+            piece = plus(left[which][middle:], came[which][middle:])
+            if which == 0 and step == 1:
+                piece, far, near = lax.optimization_barrier((piece, far, near))
+                far = lax.ppermute(far, "seq", [(i, i - 2) for i in range(2, n_seq)])
+                near = lax.ppermute(near, "seq", [(i, i - 1) for i in range(1, n_seq)])
+                first_piece = piece
+            if which == 2 and step == 2:
+                piece, first_piece = lax.optimization_barrier((piece, first_piece))
+            if which == 0 and step == steps - 1:
+                piece, far, near, mine, gathered = lax.optimization_barrier((piece, far, near, mine, gathered))
+            rest = plus(left[which][:middle], came[which][:middle])
+            came[which] = swap(piece, order[step])
+            left[which] = rest
+    pairs = list(zip(left, came))
+    totals = jnp.sum(gathered[:, : 3 * dt], axis=0).reshape(3, width)
+    correction = 1.0 - first_decay**STEP
+    holds = lax.dynamic_slice_in_dim((slot_tiles < tile_count).astype(jnp.int32), me * per_device, per_device)
+    moment_first, moment_second, new_weights = pl.pallas_call(
+        functools.partial(adam_kernel, correction, plan),
+        out_shape=tuple([shp(weight_slots.shape, F32)] * 3),
+        in_specs=[vm] * (2 * len(plan)) + [sm] + [vm] * 5,
+        out_specs=tuple([vm] * 3),
+        compiler_params=pltpu.CompilerParams(vmem_limit_bytes=30 << 20),
+        name="adam",
+    )(*[x for pair in pairs for x in pair], holds, first_moment, second_moment, basis_left, basis_right, weight_slots)
     input_grad = pl.pallas_call(
         input_kernel,
         out_shape=shp((own, width), F32),
@@ -705,20 +920,9 @@
         name="input_grad",
     )(mine_tok, gains, ghid, mine, near, far)
 
-    row_at = lax.axis_index("dp")
-    spots = jnp.arange(width, dtype=jnp.int32)
-    totals = jnp.stack([small_pre[0], small[0], jnp.where(spots == row_at, small[1], 0.0)])
-    bit = 1
-    while bit < devices:
-        totals = totals + swap(totals, bit)
-        bit *= 2
     gain_total = totals[:2]
     fraction = lax.dynamic_slice_in_dim(totals[2], row_at, 1)
 
-    correction = 1.0 - first_decay**STEP
-    moment_first, moment_second, new_weights = rotated_adam(
-        owned_grad, first_moment, second_moment, basis_left, basis_right, weight_slots, correction
-    )
     gain_moment = first_decay * gain_first + (1.0 - first_decay) * gain_total
     gain_square = second_decay * gain_second + (1.0 - second_decay) * gain_total * gain_total
     gain_update = gains - gain_rate * (gain_moment / correction) / (

time: 349 us -> 287 us (0.82)
  waiting for transfers between devices: 183 us -> 119 us
  other arithmetic: 16.4 us -> 32 us
  starting transfers between devices: 28.1 us -> 41.3 us
  local copies, waits for them, and re-layouts: 26.8 us -> 14.1 us
  Pallas kernels: 70.8 us -> 63.5 us
  matrix products: 6.61 us -> 0 us
    all_gather x1 -> x2, waiting for transfers between devices: 92.3 us -> 0.01 us  [the longest x1 0.01 us: local(): pieces = [lax.all_gather(rounded[:by_gather], axes, axis=0, tiled=True)]]
    ppermute x20 -> x25, waiting for transfers between devices: 79.8 us -> 119 us  [swap(): return lax.ppermute(x, axes, [(i, i ^ bit) for i in range(devices)])]
    convert_element_type x15, other arithmetic: 9.24 us -> 25.5 us  [plus(): return (a.astype(F32) + b.astype(F32)).astype(BF)]
    ppermute x20 -> x25, starting transfers between devices: 15.6 us -> 29.3 us  [swap(): return lax.ppermute(x, axes, [(i, i ^ bit) for i in range(devices)])]
    slice x18 -> x6, local copies, waits for them, and re-layouts: 11.3 us -> 2.14 us  [the longest x2 1.42 us: local(): columns[:reach]]
    pallas_call x2 -> x4, Pallas kernels: 66.9 us -> 58.7 us  [the longest x1 42.9 us: local(): pl.pallas_call(functools.partial(layer_kernel, tiles, sizes), out_shape=(...]
    dot_general x4 -> x0, matrix products: 6.61 us -> none  [the longest x1 2.96 us: rotated_adam(): back = jnp.einsum('sil,sjl->sij', back, right, precision=precise)]
    ppermute x2, waiting for transfers between devices: 6.53 us -> 0.01 us  [local(): lax.ppermute(mine_tok, 'seq', [(i, i + step) for i in range(n_seq - step)])]
  transfers between devices with their start and end apart: 27 -> 33, of which waited for: 16 -> 18; matrix products, arithmetic and copies ran while one was open for 7% -> 10% of each run, Pallas kernels for 1% -> 4%
where the time goes in v2:
time: 287 us; the launch traced here: 286 us
  waiting for transfers between devices  119 us (41%)
  Pallas kernels  63.5 us (22%)
  starting transfers between devices  41.3 us (14%)
  other arithmetic  32 us (11%)
  between operations  15.9 us (6%)
  local copies, waits for them, and re-layouts  14.1 us (5%)
    ppermute x25, waiting for transfers between devices, swap(): return lax.ppermute(x, axes, [(i, i ^ bit) for i in range(devices)])  119 us
    pallas_call x1, Pallas kernels, local(): pl.pallas_call(functools.partial(layer_kernel, tiles, sizes), out_shape=(...  42.9 us
    ppermute x25, starting transfers between devices, swap(): return lax.ppermute(x, axes, [(i, i ^ bit) for i in range(devices)])  29.3 us
    convert_element_type x15, other arithmetic, plus(): return (a.astype(F32) + b.astype(F32)).astype(BF)  25.5 us
    unnamed x50, local copies, waits for them, and re-layouts  8.33 us
    ppermute x2, starting transfers between devices, local(): lax.ppermute(mine_tok, 'seq', [(i, i + step) for i in range(n_seq - step)])  6.38 us
    pallas_call x1, Pallas kernels, local(): pl.pallas_call(qkv_kernel, out_shape=(sums_shape, sums_shape), in_specs=[...  6.33 us
  transfers between devices with their start and end apart: 33, of which 18 were waited for; matrix products, arithmetic and copies ran while one was open for 10% of the time, Pallas kernels for 4%

profile of v2, /device:TPU:0, one launch (start us, length us, event | category | flops | bytes accessed | tf_op | source)
XLA Modules:
  0.0 286.0 jit_solution(9218226222331240021)
XLA Ops:
  9.3 4.9 %collective-permute-start.4 = (bf16[256,768]{1,0:T(8,128)(2,1)S(1)}, bf16[256,768]{1,0:T(8,128)(2,1)S(1)}, u32[]{:S(2)}, u32[]{:S(2)}) collective-permute-start(bf16[256,768]{1,0:T(8,128)(2,1)S(1)} %bitcast.12), channel_id=1, source_target_pairs={{0,2},{1,3},{4,6},{5,7},{8,10},{9,11},{12,14},{13,15},{16,18},{17,... | collective-permute-start | bytes 1179656 | tf_op jit(solution)/shard_map/ppermute | solution.py:680
  15.8 2.7 collective-permute-start.2
  19.5 10.8 %collective-permute-done.2 = bf16[4,128,128]{2,1,0:T(8,128)(2,1)S(1)} collective-permute-done((bf16[4,128,128]{2,1,0:T(8,128)(2,1)S(1)}, bf16[4,128,128]{2,1,0:T(8,128)(2,1)S(1)}, u32[]{:S(2)}, u32[]{:S(2)}) %collective-permute-start.2) | collective-permute-done | bytes 131104 | tf_op jit(solution)/shard_map/ppermute | solution.py:646
  30.6 3.1 %collective-permute-done = bf16[4,128,128]{2,1,0:T(8,128)(2,1)S(1)} collective-permute-done((bf16[4,128,128]{2,1,0:T(8,128)(2,1)S(1)}, bf16[4,128,128]{2,1,0:T(8,128)(2,1)S(1)}, u32[]{:S(2)}, u32[]{:S(2)}) %collective-permute-start) | collective-permute-done | bytes 131104 | tf_op jit(solution)/shard_map/ppermute | solution.py:646
  37.1 3.7 %collective-permute-done.3 = bf16[8,128,128]{2,1,0:T(8,128)(2,1)S(1)} collective-permute-done((bf16[8,128,128]{2,1,0:T(8,128)(2,1)S(1)}, bf16[8,128,128]{2,1,0:T(8,128)(2,1)S(1)}, u32[]{:S(2)}, u32[]{:S(2)}) %collective-permute-start.3) | collective-permute-done | bytes 262176 | tf_op jit(solution)/shard_map/ppermute | solution.py:646
  40.8 8.0 %collective-permute-done.1 = bf16[8,128,128]{2,1,0:T(8,128)(2,1)S(1)} collective-permute-done((bf16[8,128,128]{2,1,0:T(8,128)(2,1)S(1)}, bf16[8,128,128]{2,1,0:T(8,128)(2,1)S(1)}, u32[]{:S(2)}, u32[]{:S(2)}) %collective-permute-start.1) | collective-permute-done | bytes 262176 | tf_op jit(solution)/shard_map/ppermute | solution.py:646
  51.6 12.0 %collective-permute-done.10 = bf16[16,128,128]{2,1,0:T(8,128)(2,1)S(1)} collective-permute-done((bf16[16,128,128]{2,1,0:T(8,128)(2,1)S(1)}, bf16[16,128,128]{2,1,0:T(8,128)(2,1)S(1)}, u32[]{:S(2)}, u32[]{:S(2)}) %collective-permute-start.10) | collective-permute-done | bytes 524320 | tf_op jit(solution)/shard_map/ppermute | solution.py:646
  67.4 30.2 %collective-permute-done.11.refs_15_ = bf16[32,128,128]{2,1,0:T(8,128)(2,1)S(1)} collective-permute-done((bf16[32,128,128]{2,1,0:T(8,128)(2,1)S(1)}, bf16[32,128,128]{2,1,0:T(8,128)(2,1)S(1)}, u32[]{:S(2)}, u32[]{:S(2)}) %collective-permute-start.11) | collective-permute-done | bytes 1048608 | tf_op jit(solution)/shard_map/ppermute | solution.py:646
  102.1 42.9 %layer.1 = (bf16[256,768]{1,0:T(8,128)(2,1)}, f32[256,768]{1,0:T(8,128)}, bf16[256,768]{1,0:T(8,128)(2,1)}, bf16[768,768]{1,0:T(8,128)(2,1)}, bf16[768,768]{1,0:...) custom-call(s32[448]{0:T(512)} %get-tuple-element.62.refs_0_, ...), custom_call_target="tpu_custom_call" | custom-call | tf_op jit(solution)/shard_map/layer/pallas_call | solution.py:709
  149.3 6.3 %qkv_grad.1 = (bf16[224,128,128]{2,1,0:T(8,128)(2,1)}, bf16[224,128,128]{2,1,0:T(8,128)(2,1)}) custom-call(s32[448]{0:T(512)} %get-tuple-element.63.refs_1_.dst, bf16[256,768]{1,0:T(8,128)(2,1)} %get-tuple-element.77.gq_h, bf16[768,768]{1,0:T(8,128)(2,1)} %get-tuple-element.78.gk_h, ...), custom_call_target="tpu_custom_call", output_to_operand_aliasing={{0}: (5, {}), {1}: (6, {})} | custom-call | flops 2113929216 | bytes 8388608 | tf_op jit(solution)/shard_map/qkv_grad/pallas_call | solution.py:797
  156.2 4.9 %head_grad.1 = (bf16[256,128]{1,0:T(8,128)(2,1)}, bf16[768,128]{1,0:T(8,128)(2,1)}, bf16[224,128,128]{2,1,0:T(8,128)(2,1)}, bf16[224,128,128]{2,1,0:T(8,128)(2,1)}) custom-call(s32[448]{0:T(512)} %get-tuple-element.63.refs_1_.dst, f32[8,768]{1,0:T(8,128)} %broadcast_in_dim.52.suffix, ...), custom_call_target="tpu_custom_call", output_to_operand_aliasing={{2}: (9, {}), {3}: (10, {})} | custom-call | flops 1073741824 | bytes 4194304 | tf_op jit(solution)/shard_map/head_grad/pallas_call | solution.py:818
  168.2 3.4 %pre_grad.1 = (bf16[256,768]{1,0:T(8,128)(2,1)}, bf16[256,768]{1,0:T(8,128)(2,1)}, f32[256,768]{1,0:T(8,128)S(1)}, f32[8,768]{1,0:T(8,128)S(1)}) custom-call(bf16[768,768]{1,0:T(8,128)(2,1)S(1)} %copy-done, bf16[256,128]{1,0:T(8,128)(2,1)S(1)} %copy-done.16, bf16[768,128]{1,0:T(8,128)(2,1)S(1)} %copy-done.15, bf16[256,768]{1,0:T(8,128)(2,1)S(1)} %copy-done.4, ...), custom_call_target="tpu_custom_call" | custom-call | flops 2113929216 | bytes 10485760 | tf_op jit(solution)/shard_map/pre_grad/pallas_call | solution.py:846
  173.9 3.9 %add_convert_fusion.1 = bf16[48,128,128]{2,1,0:T(8,128)(2,1)} fusion(bf16[224,128,128]{2,1,0:T(8,128)(2,1)} %collective-permute-done.16, bf16[224,128,128]{2,1,0:T(8,128)(2,1)} %get-tuple-element.85), kind=kLoop, calls=%fused_computation.1 | loop fusion | flops 3145728 | bytes 4718592 | tf_op jit(solution)/shard_map/convert_element_type | solution.py:842
  189.9 2.4 add_convert_fusion
  192.3 12.5 %collective-permute-done.27 = bf16[24,128,128]{2,1,0:T(8,128)(2,1)} collective-permute-done((bf16[24,128,128]{2,1,0:T(8,128)(2,1)S(1)}, bf16[24,128,128]{2,1,0:T(8,128)(2,1)}, u32[]{:S(2)}, u32[]{:S(2)}) %collective-permute-start.27) | collective-permute-done | bytes 786464 | tf_op jit(solution)/shard_map/ppermute | solution.py:646
  206.2 5.9 %collective-permute-start.28 = (bf16[12,128,128]{2,1,0:T(8,128)(2,1)S(1)}, bf16[12,128,128]{2,1,0:T(8,128)(2,1)S(1)}, u32[]{:S(2)}, u32[]{:S(2)}) collective-permute-start(bf16[12,128,128]{2,1,0:T(8,128)(2,1)S(1)} %get-tuple-element.123), channel_id=1, source_target_pairs={{0,16},{1,17},{2,18},{3,19},{4,20},{5,21},{6,22},{7,23},{8,24},{9,... | collective-permute-start | bytes 1179656 | tf_op jit(solution)/shard_map/ppermute | solution.py:646
  213.5 2.5 add_convert_fusion.9
  218.3 2.7 add_convert_fusion.6
  222.4 8.1 %collective-permute-done.28 = bf16[12,128,128]{2,1,0:T(8,128)(2,1)S(1)} collective-permute-done((bf16[12,128,128]{2,1,0:T(8,128)(2,1)S(1)}, bf16[12,128,128]{2,1,0:T(8,128)(2,1)S(1)}, u32[]{:S(2)}, u32[]{:S(2)}) %collective-permute-start.28) | collective-permute-done | bytes 393248 | tf_op jit(solution)/shard_map/ppermute | solution.py:646
  234.1 7.7 %collective-permute-done.24 = bf16[20,128,128]{2,1,0:T(8,128)(2,1)} collective-permute-done((bf16[20,128,128]{2,1,0:T(8,128)(2,1)}, bf16[20,128,128]{2,1,0:T(8,128)(2,1)}, u32[]{:S(2)}, u32[]{:S(2)}) %collective-permute-start.24) | collective-permute-done | bytes 655392 | tf_op jit(solution)/shard_map/ppermute | solution.py:646
  247.6 10.5 %collective-permute-done.25 = bf16[10,128,128]{2,1,0:T(8,128)(2,1)S(1)} collective-permute-done((bf16[10,128,128]{2,1,0:T(8,128)(2,1)S(1)}, bf16[10,128,128]{2,1,0:T(8,128)(2,1)S(1)}, u32[]{:S(2)}, u32[]{:S(2)}) %collective-permute-start.25) | collective-permute-done | bytes 327712 | tf_op jit(solution)/shard_map/ppermute | solution.py:646
  259.6 3.0 %collective-permute-start.22 = (bf16[6,128,128]{2,1,0:T(8,128)(2,1)}, bf16[6,128,128]{2,1,0:T(8,128)(2,1)}, u32[]{:S(2)}, u32[]{:S(2)}) collective-permute-start(bf16[6,128,128]{2,1,0:T(8,128)(2,1)} %get-tuple-element.108), channel_id=1, source_target_pairs={{0,16},{1,17},{2,18},{3,19},{4,20},{5,21},{6,22},{7,23},{8,24},{9,... | collective-permute-start | bytes 589832 | tf_op jit(solution)/shard_map/ppermute | solution.py:646
  268.7 3.8 %collective-permute-done.26.refs_3_ = bf16[5,128,128]{2,1,0:T(8,128)(2,1)} collective-permute-done((bf16[5,128,128]{2,1,0:T(8,128)(2,1)}, bf16[5,128,128]{2,1,0:T(8,128)(2,1)}, u32[]{:S(2)}, u32[]{:S(2)}) %collective-permute-start.26) | collective-permute-done | bytes 163872 | tf_op jit(solution)/shard_map/ppermute | solution.py:646
  274.6 4.6 %adam.1 = (f32[14,128,128]{2,1,0:T(8,128)}, f32[14,128,128]{2,1,0:T(8,128)}, f32[14,128,128]{2,1,0:T(8,128)}) custom-call(bf16[6,128,128]{2,1,0:T(8,128)(2,1)S(1)} %get-tuple-element.130.refs_0_, bf16[6,128,128]{2,1,0:T(8,128)(2,1)} %collective-permute-done.22.refs_1_, bf16[5,128,128]{2,1,0:T(8,128)(2,1)S(1)} %get-tuple-element.133.refs_2_, ...), custom_call_target="tpu_custom_call" | custom-call | tf_op jit(solution)/shard_map/adam/pallas_call | solution.py:906
  (149 shorter events, 69.8 us)
Async XLA Ops:
  7.2 94.9 %all-gather.4.cloned.1.call-start = ((), (), s32[]{:S(2)}) async-start(), calls=%async_computation | async-start | bytes 6488064 | tf_op jit(solution)/shard_map/all_gather | solution.py:692
  9.3 250.4 %all-gather.6.cloned.1.call-start = ((), (), s32[]{:S(2)}) async-start(), calls=%async_computation.1 | async-start | bytes 1081344 | tf_op jit(solution)/shard_map/all_gather | solution.py:874
  9.3 39.6 %collective-permute-start.4 = (bf16[256,768]{1,0:T(8,128)(2,1)S(1)}, bf16[256,768]{1,0:T(8,128)(2,1)S(1)}, u32[]{:S(2)}, u32[]{:S(2)}) collective-permute-start(bf16[256,768]{1,0:T(8,128)(2,1)S(1)} %bitcast.12), channel_id=1, source_target_pairs={{0,2},{1,3},{4,6},{5,7},{8,10},{9,11},{12,14},{13,15},{16,18},{17,... | collective-permute-start | bytes 1179656 | tf_op jit(solution)/shard_map/ppermute | solution.py:680
  14.2 34.7 %collective-permute-start.5 = (bf16[256,768]{1,0:T(8,128)(2,1)S(1)}, bf16[256,768]{1,0:T(8,128)(2,1)S(1)}, u32[]{:S(2)}, u32[]{:S(2)}) collective-permute-start(bf16[256,768]{1,0:T(8,128)(2,1)S(1)} %bitcast.13), channel_id=1, source_target_pairs={{0,1},{1,2},{2,3},{4,5},{5,6},{6,7},{8,9},{9,10},{10,11},{12,13},{... | collective-permute-start | bytes 1179656 | tf_op jit(solution)/shard_map/ppermute | solution.py:680
  15.8 14.6 %collective-permute-start.2 = (bf16[4,128,128]{2,1,0:T(8,128)(2,1)S(1)}, bf16[4,128,128]{2,1,0:T(8,128)(2,1)S(1)}, u32[]{:S(2)}, u32[]{:S(2)}) collective-permute-start(bf16[4,128,128]{2,1,0:T(8,128)(2,1)S(1)} %get-tuple-element.134), channel_id=1, source_target_pairs={{0,16},{1,17},{2,18},{3,19},{4,20},{5,21},{6,22},{7,23},{8,24},{9,... | collective-permute-start | bytes 393224 | tf_op jit(solution)/shard_map/ppermute | solution.py:646
  18.4 15.3 %collective-permute-start = (bf16[4,128,128]{2,1,0:T(8,128)(2,1)S(1)}, bf16[4,128,128]{2,1,0:T(8,128)(2,1)S(1)}, u32[]{:S(2)}, u32[]{:S(2)}) collective-permute-start(bf16[4,128,128]{2,1,0:T(8,128)(2,1)S(1)} %get-tuple-element.135), channel_id=1, source_target_pairs={{0,16},{1,17},{2,18},{3,19},{4,20},{5,21},{6,22},{7,23},{8,24},{9,... | collective-permute-start | bytes 393224 | tf_op jit(solution)/shard_map/ppermute | solution.py:646
  33.7 15.1 %collective-permute-start.1 = (bf16[8,128,128]{2,1,0:T(8,128)(2,1)S(1)}, bf16[8,128,128]{2,1,0:T(8,128)(2,1)S(1)}, u32[]{:S(2)}, u32[]{:S(2)}) collective-permute-start(bf16[8,128,128]{2,1,0:T(8,128)(2,1)S(1)} %pad_maximum_fusion.3), channel_id=1, source_target_pairs={{0,8},{1,9},{2,10},{3,11},{4,12},{5,13},{6,14},{7,15},{8,0},{9,1},... | collective-permute-start | bytes 786440 | tf_op jit(solution)/shard_map/ppermute | solution.py:646
  50.0 15.3 %collective-permute-start.6 = (bf16[16,128,128]{2,1,0:T(8,128)(2,1)S(1)}, bf16[16,128,128]{2,1,0:T(8,128)(2,1)S(1)}, u32[]{:S(2)}, u32[]{:S(2)}) collective-permute-start(bf16[16,128,128]{2,1,0:T(8,128)(2,1)S(1)} %pad_maximum_fusion.1), channel_id=1, source_target_pairs={{0,4},{1,5},{2,6},{3,7},{4,0},{5,1},{6,2},{7,3},{8,12},{9,13},{10,... | collective-permute-start | bytes 1572872 | tf_op jit(solution)/shard_map/ppermute | solution.py:646
  63.7 33.9 %collective-permute-start.11 = (bf16[32,128,128]{2,1,0:T(8,128)(2,1)S(1)}, bf16[32,128,128]{2,1,0:T(8,128)(2,1)S(1)}, u32[]{:S(2)}, u32[]{:S(2)}) collective-permute-start(bf16[32,128,128]{2,1,0:T(8,128)(2,1)S(1)} %constant_dynamic-update-slice_fusion.2.refs_14_), channel_id=1, source_target_pairs={{0,4},{1,5},{2,6},{3,7},{4,0},{5,1},{6,2},{7,3},{8,12},{9,13},{10,... | collective-permute-start | bytes 3145736 | tf_op jit(solution)/shard_map/ppermute | solution.py:646
  65.4 32.3 %collective-permute-start.7 = (bf16[32,128,128]{2,1,0:T(8,128)(2,1)S(1)}, bf16[32,128,128]{2,1,0:T(8,128)(2,1)}, u32[]{:S(2)}, u32[]{:S(2)}) collective-permute-start(bf16[32,128,128]{2,1,0:T(8,128)(2,1)S(1)} %constant_dynamic-update-slice_fusion.refs_10_), channel_id=1, source_target_pairs={{0,2},{1,3},{2,0},{3,1},{4,6},{5,7},{6,4},{7,5},{8,10},{9,11},{10,... | collective-permute-start | bytes 3145736 | tf_op jit(solution)/shard_map/ppermute | solution.py:646
  66.9 32.8 %collective-permute-start.12 = (bf16[32,128,128]{2,1,0:T(8,128)(2,1)S(1)}, bf16[32,128,128]{2,1,0:T(8,128)(2,1)}, u32[]{:S(2)}, u32[]{:S(2)}) collective-permute-start(bf16[32,128,128]{2,1,0:T(8,128)(2,1)S(1)} %constant_dynamic-update-slice_fusion.2.refs_14_), channel_id=1, source_target_pairs={{0,1},{1,0},{2,3},{3,2},{4,5},{5,4},{6,7},{7,6},{8,9},{9,8},{10,11... | collective-permute-start | bytes 3145736 | tf_op jit(solution)/shard_map/ppermute | solution.py:646
  66.9 32.8 %collective-permute-start.8 = (bf16[32,128,128]{2,1,0:T(8,128)(2,1)S(1)}, bf16[32,128,128]{2,1,0:T(8,128)(2,1)}, u32[]{:S(2)}, u32[]{:S(2)}) collective-permute-start(bf16[32,128,128]{2,1,0:T(8,128)(2,1)S(1)} %constant_dynamic-update-slice_fusion.refs_10_), channel_id=1, source_target_pairs={{0,1},{1,0},{2,3},{3,2},{4,5},{5,4},{6,7},{7,6},{8,9},{9,8},{10,11... | collective-permute-start | bytes 3145736 | tf_op jit(solution)/shard_map/ppermute | solution.py:646
  180.0 38.4 %collective-permute-start.17 = (bf16[48,128,128]{2,1,0:T(8,128)(2,1)}, bf16[48,128,128]{2,1,0:T(8,128)(2,1)}, u32[]{:S(2)}, u32[]{:S(2)}) collective-permute-start(bf16[48,128,128]{2,1,0:T(8,128)(2,1)} %add_convert_fusion.1), channel_id=1, source_target_pairs={{0,2},{1,3},{2,0},{3,1},{4,6},{5,7},{6,4},{7,5},{8,10},{9,11},{10,... | collective-permute-start | bytes 4718600 | tf_op jit(solution)/shard_map/ppermute | solution.py:646
  182.4 31.1 %collective-permute-start.23 = (bf16[40,128,128]{2,1,0:T(8,128)(2,1)S(1)}, bf16[40,128,128]{2,1,0:T(8,128)(2,1)}, u32[]{:S(2)}, u32[]{:S(2)}) collective-permute-start(bf16[40,128,128]{2,1,0:T(8,128)(2,1)S(1)} %add_convert_fusion.3), channel_id=1, source_target_pairs={{0,4},{1,5},{2,6},{3,7},{4,0},{5,1},{6,2},{7,3},{8,12},{9,13},{10,... | collective-permute-start | bytes 3932168 | tf_op jit(solution)/shard_map/ppermute | solution.py:646
  185.2 19.6 %collective-permute-start.27 = (bf16[24,128,128]{2,1,0:T(8,128)(2,1)S(1)}, bf16[24,128,128]{2,1,0:T(8,128)(2,1)}, u32[]{:S(2)}, u32[]{:S(2)}) collective-permute-start(bf16[24,128,128]{2,1,0:T(8,128)(2,1)S(1)} %add_convert_fusion.7), channel_id=1, source_target_pairs={{0,8},{1,9},{2,10},{3,11},{4,12},{5,13},{6,14},{7,15},{8,0},{9,1},... | collective-permute-start | bytes 2359304 | tf_op jit(solution)/shard_map/ppermute | solution.py:646
  206.2 24.3 %collective-permute-start.28 = (bf16[12,128,128]{2,1,0:T(8,128)(2,1)S(1)}, bf16[12,128,128]{2,1,0:T(8,128)(2,1)S(1)}, u32[]{:S(2)}, u32[]{:S(2)}) collective-permute-start(bf16[12,128,128]{2,1,0:T(8,128)(2,1)S(1)} %get-tuple-element.123), channel_id=1, source_target_pairs={{0,16},{1,17},{2,18},{3,19},{4,20},{5,21},{6,22},{7,23},{8,24},{9,... | collective-permute-start | bytes 1179656 | tf_op jit(solution)/shard_map/ppermute | solution.py:646
  216.0 25.8 %collective-permute-start.24 = (bf16[20,128,128]{2,1,0:T(8,128)(2,1)}, bf16[20,128,128]{2,1,0:T(8,128)(2,1)}, u32[]{:S(2)}, u32[]{:S(2)}) collective-permute-start(bf16[20,128,128]{2,1,0:T(8,128)(2,1)} %get-tuple-element.121), channel_id=1, source_target_pairs={{0,8},{1,9},{2,10},{3,11},{4,12},{5,13},{6,14},{7,15},{8,0},{9,1},... | collective-permute-start | bytes 1966088 | tf_op jit(solution)/shard_map/ppermute | solution.py:646
  221.1 22.7 %collective-permute-start.18 = (bf16[24,128,128]{2,1,0:T(8,128)(2,1)}, bf16[24,128,128]{2,1,0:T(8,128)(2,1)}, u32[]{:S(2)}, u32[]{:S(2)}) collective-permute-start(bf16[24,128,128]{2,1,0:T(8,128)(2,1)} %get-tuple-element.99), channel_id=1, source_target_pairs={{0,4},{1,5},{2,6},{3,7},{4,0},{5,1},{6,2},{7,3},{8,12},{9,13},{10,... | collective-permute-start | bytes 2359304 | tf_op jit(solution)/shard_map/ppermute | solution.py:646
  230.6 14.6 %collective-permute-start.29 = (bf16[6,128,128]{2,1,0:T(8,128)(2,1)S(1)}, bf16[6,128,128]{2,1,0:T(8,128)(2,1)S(1)}, u32[]{:S(2)}, u32[]{:S(2)}) collective-permute-start(bf16[6,128,128]{2,1,0:T(8,128)(2,1)S(1)} %get-tuple-element.111), channel_id=1, source_target_pairs={{0,2},{1,3},{2,0},{3,1},{4,6},{5,7},{6,4},{7,5},{8,10},{9,11},{10,... | collective-permute-start | bytes 589832 | tf_op jit(solution)/shard_map/ppermute | solution.py:646
  231.3 28.4 %collective-permute-start.20 = (bf16[256,768]{1,0:T(8,128)(2,1)}, bf16[256,768]{1,0:T(8,128)(2,1)S(1)}, u32[]{:S(2)}, u32[]{:S(2)}) collective-permute-start(bf16[256,768]{1,0:T(8,128)(2,1)} %get-tuple-element.100), channel_id=1, source_target_pairs={{2,0},{3,1},{6,4},{7,5},{10,8},{11,9},{14,12},{15,13},{18,16},{19,... | collective-permute-start | bytes 1179656 | tf_op jit(solution)/shard_map/ppermute | solution.py:892
  232.6 27.1 %collective-permute-start.21 = (bf16[256,768]{1,0:T(8,128)(2,1)}, bf16[256,768]{1,0:T(8,128)(2,1)S(1)}, u32[]{:S(2)}, u32[]{:S(2)}) collective-permute-start(bf16[256,768]{1,0:T(8,128)(2,1)} %get-tuple-element.101), channel_id=1, source_target_pairs={{1,0},{2,1},{3,2},{5,4},{6,5},{7,6},{9,8},{10,9},{11,10},{13,12},{... | collective-permute-start | bytes 1179656 | tf_op jit(solution)/shard_map/ppermute | solution.py:893
  243.1 14.9 %collective-permute-start.25 = (bf16[10,128,128]{2,1,0:T(8,128)(2,1)S(1)}, bf16[10,128,128]{2,1,0:T(8,128)(2,1)S(1)}, u32[]{:S(2)}, u32[]{:S(2)}) collective-permute-start(bf16[10,128,128]{2,1,0:T(8,128)(2,1)S(1)} %get-tuple-element.127), channel_id=1, source_target_pairs={{0,2},{1,3},{2,0},{3,1},{4,6},{5,7},{6,4},{7,5},{8,10},{9,11},{10,... | collective-permute-start | bytes 983048 | tf_op jit(solution)/shard_map/ppermute | solution.py:646
  245.9 22.8 %collective-permute-start.30 = (bf16[3,128,128]{2,1,0:T(8,128)(2,1)}, bf16[3,128,128]{2,1,0:T(8,128)(2,1)}, u32[]{:S(2)}, u32[]{:S(2)}) collective-permute-start(bf16[3,128,128]{2,1,0:T(8,128)(2,1)} %get-tuple-element.136), channel_id=1, source_target_pairs={{0,4},{1,5},{2,6},{3,7},{4,0},{5,1},{6,2},{7,3},{8,12},{9,13},{10,... | collective-permute-start | bytes 294920 | tf_op jit(solution)/shard_map/ppermute | solution.py:646
  259.6 14.9 %collective-permute-start.22 = (bf16[6,128,128]{2,1,0:T(8,128)(2,1)}, bf16[6,128,128]{2,1,0:T(8,128)(2,1)}, u32[]{:S(2)}, u32[]{:S(2)}) collective-permute-start(bf16[6,128,128]{2,1,0:T(8,128)(2,1)} %get-tuple-element.108), channel_id=1, source_target_pairs={{0,16},{1,17},{2,18},{3,19},{4,20},{5,21},{6,22},{7,23},{8,24},{9,... | collective-permute-start | bytes 589832 | tf_op jit(solution)/shard_map/ppermute | solution.py:646
  (33 other events, 347.7 us)
Sparse Core Ops, SparseCore 0:
  11.5 84.5 all-gather.3
  187.8 64.7 all-gather.5

commit v3 on v2

--- a/solution.py
+++ b/solution.py
@@ -65,16 +65,15 @@
 
 
 def send_tile(tile_ref, dst, sums, sem):
-    stay, away = sums
-    half = stay.shape[0]
-
-    @pl.when(dst < half)
-    def _():
-        pltpu.make_async_copy(tile_ref, stay.at[dst], sem).start()
-
-    @pl.when(dst >= half)
-    def _():
-        pltpu.make_async_copy(tile_ref, away.at[dst - half], sem).start()
+    low = 0
+    for buffer in sums:
+        high = low + buffer.shape[0]
+
+        @pl.when((dst >= low) & (dst < high))
+        def _(buffer=buffer, low=low):
+            pltpu.make_async_copy(tile_ref, buffer.at[dst - low], sem).start()
+
+        low = high
 
 
 def wait_tiles(stage_ref, sums, sem):
@@ -89,56 +88,14 @@
 def mm3_nt(a, b):
     (ah, al), (bh, bl) = a, b
     return mm_nt(jnp.concatenate([ah, ah, al], axis=1), jnp.concatenate([bh, bl, bh], axis=1))
-
-
-def lane_half(shape, second):
-    lane = lax.broadcasted_iota(jnp.int32, shape, 1)
-    return (lane >= HD) if second else (lane < HD)
-
-
-def keep_half(x, second):
-    return jnp.where(lane_half(x.shape, second), x, jnp.zeros_like(x))
-
-
-def norm_parts(x):
-    centred = x - jnp.mean(x, axis=-1, keepdims=True)
-    rate = lax.rsqrt(jnp.mean(centred * centred, axis=-1, keepdims=True) + norm_epsilon)
-    return centred * rate, rate
-
-
-def send_tile(tile_ref, dst, sums, sem):
-    stay, away = sums
-    half = stay.shape[0]
-
-    @pl.when(dst < half)
-    def _():
-        pltpu.make_async_copy(tile_ref, stay.at[dst], sem).start()
-
-    @pl.when(dst >= half)
-    def _():
-        pltpu.make_async_copy(tile_ref, away.at[dst - half], sem).start()
-
-
-def wait_tiles(stage_ref, sums, sem):
-    pltpu.make_async_copy(stage_ref, sums[0].at[pl.ds(0, stage_ref.shape[0])], sem).wait()
-
-
-def mm3(a, b):
-    (ah, al), (bh, bl) = a, b
-    return mm(ah, bh) + (mm(ah, bl) + mm(al, bh))
-
-
-def mm3_nt(a, b):
-    (ah, al), (bh, bl) = a, b
-    return mm_nt(ah, bh) + (mm_nt(ah, bl) + mm_nt(al, bh))
 
 
 def layer_kernel(tiles, sizes, *refs):
     (src, dst, scal, thr, tok, gains, dy, segc, segr), refs = refs[:9], refs[9:]
     w_parts, refs = refs[: len(sizes)], refs[len(sizes) :]
     (out_h, ghid_h, gq_h, gk_h, gv_h, nrm_t_h, wqkv_h, q0_h, k0t_h, part0_h, mask0_h, colsum, small, *sums), refs = (
-        refs[:15],
-        refs[15:],
+        refs[:16],
+        refs[16:],
     )
     (out, ghid, gq, gk, gv, nrm_t, wqkv, part0, mask0), refs = refs[:9], refs[9:]
     (wall, nrm, q_s, q_e, k_s, v_s, kt_s, vt_s, bias, gsh, probs, mixt, mixb, mixbt, wout, hid, xhat), refs = (
@@ -206,7 +163,7 @@
         for j in range(dt):
             wout[i * side : (i + 1) * side, j * side : (j + 1) * side] = wall[src[n_qkv + i * dt + j]]
 
-    @pl.loop(0, dt // 2)
+    @pl.loop(0, dt // 2, unroll=True)
     def _(j):
         cols = pl.ds(pl.multiple_of(2 * j * side, 2 * side), 2 * side)
         got = (mm(nrm[back:, :], wqkv[:, cols]) * 0.125).astype(BF)
@@ -215,7 +172,7 @@
 
     q_e[...] = (mm(nrm[:back, :], wqkv[:, 0:side]) * 0.125).astype(BF)
 
-    @pl.loop(0, dt // 2)
+    @pl.loop(0, dt // 2, unroll=True)
     def _(j):
         cols = pl.ds(pl.multiple_of(width + 2 * j * side, 2 * side), 2 * side)
         got = mm(nrm[...], wqkv[:, cols]).astype(BF)
@@ -225,7 +182,7 @@
         kt_s[2 * j] = got_t[:side, :]
         kt_s[2 * j + 1] = got_t[side:, :]
 
-    @pl.loop(0, dt // 2)
+    @pl.loop(0, dt // 2, unroll=True)
     def _(j):
         cols = pl.ds(pl.multiple_of(2 * width + 2 * j * side, 2 * side), 2 * side)
         got = mm(nrm[...], wqkv[:, cols]).astype(BF)
@@ -275,7 +232,7 @@
     small[...] = jnp.zeros_like(small)
     small[1:2, :] = jnp.broadcast_to(counted / valid_len.astype(F32), (1, width))
 
-    @pl.loop(0, pairs)
+    @pl.loop(0, pairs, unroll=2)
     def _(p):
         q2 = q_s[p]
         k2 = k_s[p]
@@ -442,12 +399,13 @@
     return copies
 
 
-def qkv_kernel(dst, gq_h, gk_h, gv_h, nrm_h, stay_in, away_in, stay, away, gq, gk, gv, nrm_t, stage, lsem, gsem):
+def qkv_kernel(dst, gq_h, gk_h, gv_h, nrm_h, *refs):
+    sums = refs[3:6]
+    gq, gk, gv, nrm_t, stage, lsem, gsem = refs[6:]
     own, width = gq.shape
     side = stage.shape[-1]
     dt = width // side
     back = gk.shape[0] - own
-    sums = (stay, away)
     copies = load_all([(nrm_h, nrm_t), (gv_h, gv), (gk_h, gk), (gq_h, gq)], lsem)
     copies[0].wait()
     count = 0
@@ -469,15 +427,14 @@
     wait_tiles(stage, sums, gsem)
 
 
-def head_kernel(
-    dst, suffix, part0_h, mask0_h, q0_h, k0t_h, gq_h, gk_h, nrm_h, stay_in, away_in, gq_out, gk_out, stay, away,
-    part0, mask0, q0, k0t, gq, gk, nrm_t, stage, lsem, gsem,
-):
+def head_kernel(dst, near_sums, far_sums, part0_h, mask0_h, q0_h, k0t_h, gq_h, gk_h, nrm_h, *refs):
+    gq_out, gk_out = refs[3:5]
+    sums = refs[5:8]
+    part0, mask0, q0, k0t, gq, gk, nrm_t, stage, lsem, gsem = refs[8:]
     own, side = gq.shape
     window = gk.shape[0]
     back = window - own
     dt = nrm_t.shape[0] // side
-    sums = (stay, away)
     head = pl.ds(0, side)
     copies = load_all(
         [
@@ -491,7 +448,10 @@
         ],
         lsem,
     )
-    column = jnp.broadcast_to(suffix[0:1, :], (side, window)).T
+    none = jnp.zeros((1, own), F32)
+    suffix = jnp.concatenate([none, near_sums[0:1, : window - own]], axis=1)
+    suffix = suffix + jnp.concatenate([none, none, far_sums[0:1, : window - 2 * own]], axis=1)
+    column = jnp.broadcast_to(suffix, (side, window)).T
     column = jnp.concatenate([column] * (own // side), axis=1)
     for copy in copies[:-1]:
         copy.wait()
@@ -582,6 +542,10 @@
             weight_out[slot] = w - weight_rate * back - weight_rate * decay_rate * w
 
 
+def after(x, earlier):
+    return lax.optimization_barrier((x, earlier))[0]
+
+
 def bit_plan(devices, per_device):
     bits = [1 << b for b in range(devices.bit_length() - 1)]
     first, rest = bits[0], bits[1:]
@@ -589,10 +553,11 @@
         orders = [(2, 4, 8, 16), (4, 8, 2, 16), (8, 16, 2, 4)]
     else:
         orders = [tuple(rest[i:] + rest[:i]) for i in range(3)]
-    third = per_device * 3 // 7
-    sizes = [third, per_device - third] if per_device < 4 else [third, per_device * 5 // 14, 0]
-    if len(sizes) == 3:
-        sizes[2] = per_device - sizes[0] - sizes[1]
+    if per_device < 4:
+        sizes = [1] * per_device
+    else:
+        sizes = [per_device * 3 // 7, per_device * 5 // 14]
+        sizes.append(per_device - sum(sizes))
     plan = []
     at = 0
     for size, order in zip(sizes, orders):
@@ -606,8 +571,12 @@
     if devices != 32 or per_device < 8:
         return per_device, []
     size = per_device * 2 // 7
-    first = per_device - 2 * size
-    return first, [(first, size, (16, 8, 4, 2, 1)), (first + size, size, (16, 8, 2, 4, 1))]
+    first = per_device * 3 // 14
+    return first, [
+        (first, size, (16, 8, 4, 2, 1)),
+        (first + size, size, (16, 8, 2, 4, 1)),
+        (first + 2 * size, per_device - first - 2 * size, (4, 2, 16, 8, 1)),
+    ]
 
 
 def local(
@@ -694,7 +663,9 @@
     for step in range(len(gather_plan[0][2]) - 2 if gather_plan else 0):
         held = [jnp.concatenate([h, swap(h, o[2][step])], axis=0) for h, o in zip(held, gather_plan)]
         if step == 1:
-            held, tok, src, dst, scal, segc, segr = lax.optimization_barrier((held, tok, src, dst, scal, segc, segr))
+            held[0], tok, src, dst, scal, segc, segr = lax.optimization_barrier(
+                (held[0], tok, src, dst, scal, segc, segr)
+            )
     for h, (_, _, order) in zip(held, gather_plan):
         two = [h, swap(h, order[-2])]
         pieces += two + [swap(x, order[-1]) for x in two]
@@ -704,7 +675,8 @@
     vm = pl.BlockSpec(memory_space=VMEM)
     sm = pl.BlockSpec(memory_space=SMEM)
     shp = jax.ShapeDtypeStruct
-    sums_shape = shp((half, side, side), BF)
+    first_rows = plan[0][1] * spread
+    sums_shapes = [shp((n, side, side), BF) for n in (half, first_rows, half - first_rows)]
     per_chunk = 2 * (CHUNK // side) * dt
     outs = pl.pallas_call(
         functools.partial(layer_kernel, tiles, sizes),
@@ -722,11 +694,10 @@
             shp((window, own), BF),
             shp((8, window), F32),
             shp((8, width), F32),
-            sums_shape,
-            sums_shape,
+            *sums_shapes,
         ),
         in_specs=[sm] * 4 + [vm] * 5 + [hbm] * len(sizes),
-        out_specs=tuple([hbm] * 11 + [vm] * 2 + [hbm] * 2),
+        out_specs=tuple([hbm] * 11 + [vm] * 2 + [hbm] * 3),
         scratch_shapes=[
             VMEM((own, width), BF),
             VMEM((own, width), F32),
@@ -783,22 +754,17 @@
         segr,
         *pieces,
     )
-    (output, ghid, gq, gk, gv, nrm_t, wqkv, q0, k0t, part0, mask0, colsum, small, stay, away) = outs
-
-    columns = colsum[0]
-    suffix = jnp.zeros((window,), F32)
-    for step in range(1, back // own + 1):
-        reach = window - step * own
-        got = lax.ppermute(columns[:reach], "seq", [(i, i - step) for i in range(step, n_seq)])
-        suffix = suffix + jnp.concatenate([jnp.zeros((step * own,), F32), got])
-    suffix = jnp.broadcast_to(suffix[None, :], (8, window))
-
+    (output, ghid, gq, gk, gv, nrm_t, wqkv, q0, k0t, part0, mask0, colsum, small, *sums) = outs
+
+    near_sums, far_sums = [
+        lax.ppermute(colsum, "seq", [(i, i - step) for i in range(step, n_seq)]) for step in (1, 2)
+    ]
     main_tiles = tiles[0] - 2 * dt
-    stay, away = pl.pallas_call(
+    sums = pl.pallas_call(
         qkv_kernel,
-        out_shape=(sums_shape, sums_shape),
-        in_specs=[sm] + [hbm] * 6,
-        out_specs=(hbm, hbm),
+        out_shape=sums_shapes,
+        in_specs=[sm] + [hbm] * 7,
+        out_specs=[hbm] * 3,
         scratch_shapes=[
             VMEM((own, width), BF),
             VMEM((window, width), BF),
@@ -808,18 +774,18 @@
             pltpu.SemaphoreType.DMA((4,)),
             pltpu.SemaphoreType.DMA,
         ],
-        input_output_aliases={5: 0, 6: 1},
+        input_output_aliases={5: 0, 6: 1, 7: 2},
         compiler_params=pltpu.CompilerParams(vmem_limit_bytes=60 << 20),
         cost_estimate=pl.CostEstimate(
             flops=2 * (2 * window + own) * width * width, bytes_accessed=8 << 20, transcendentals=0
         ),
         name="qkv_grad",
-    )(dst, gq, gk, gv, nrm_t, stay, away)
-    gq_head, gk_head, stay, away = pl.pallas_call(
+    )(dst, gq, gk, gv, nrm_t, *sums)
+    gq_head, gk_head, stay, *aways = pl.pallas_call(
         head_kernel,
-        out_shape=(shp((own, side), BF), shp((window, side), BF), sums_shape, sums_shape),
-        in_specs=[sm, vm] + [hbm] * 9,
-        out_specs=(vm, vm, hbm, hbm),
+        out_shape=(shp((own, side), BF), shp((window, side), BF), *sums_shapes),
+        in_specs=[sm, vm, vm] + [hbm] * 10,
+        out_specs=(vm, vm, hbm, hbm, hbm),
         scratch_shapes=[
             VMEM((window, own), F32),
             VMEM((window, own), BF),
@@ -832,17 +798,34 @@
             pltpu.SemaphoreType.DMA((7,)),
             pltpu.SemaphoreType.DMA,
         ],
-        input_output_aliases={9: 2, 10: 3},
+        input_output_aliases={10: 2, 11: 3, 12: 4},
         compiler_params=pltpu.CompilerParams(vmem_limit_bytes=60 << 20),
         cost_estimate=pl.CostEstimate(flops=1 << 30, bytes_accessed=4 << 20, transcendentals=0),
         name="head_grad",
-    )(dst, suffix, part0, mask0, q0, k0t, gq, gk, nrm_t, stay, away)
+    )(dst, near_sums, far_sums, part0, mask0, q0, k0t, gq, gk, nrm_t, *sums)
 
     def plus(a, b):
         return (a.astype(F32) + b.astype(F32)).astype(BF)
 
-    got = swap(away, first_bit)
-
+    got = [swap(aways[0], first_bit)]
+    aways[1] = after(aways[1], got[0])
+    got.append(swap(aways[1], first_bit))
+    steps = len(plan[0][2])
+
+    def from_got(which, low, high):
+        at, size, _ = plan[which]
+        start = at * spread
+        source, base = (got[0], 0) if which == 0 else (got[1], first_rows)
+        rows = slice(start + low * size * spread // 2, start + high * size * spread // 2)
+        return plus(stay[rows], source[rows.start - base : rows.stop - base])
+
+    sent = [from_got(0, 1, 2)]
+    for which in range(1, len(plan)):
+        got[1] = after(got[1], sent[-1])
+        sent.append(from_got(which, 1, 2))
+    gq_head = after(gq_head, sent[-1])
+    came = [swap(piece, order[0]) for piece, (_, _, order) in zip(sent, plan)]
+    left = [from_got(which, 0, 1) for which in range(len(plan))]
     far, near, mine, small_pre = pl.pallas_call(
         pre_kernel,
         out_shape=(
@@ -870,35 +853,25 @@
     spots = jnp.arange(width, dtype=jnp.int32)
     totals = jnp.stack([small_pre[0], small[0], jnp.where(spots == row_at, small[1], 0.0)])
     totals = jnp.pad(totals.reshape(3 * dt, side), ((0, side // 2 - 3 * dt), (0, 0)))
-    got, totals = lax.optimization_barrier((got, totals))
     gathered = lax.all_gather(totals, axes)
-    steps = len(plan[0][2])
-    sent = []
-    for at, size, _ in plan:
-        rows = slice(at * spread + size * spread // 2, (at + size) * spread)
-        got, piece = lax.optimization_barrier((got, plus(stay[rows], got[rows])))
-        sent.append(piece)
-    came = [swap(piece, order[0]) for piece, (_, _, order) in zip(sent, plan)]
-    left = []
-    for at, size, _ in plan:
-        rows = slice(at * spread, at * spread + size * spread // 2)
-        left.append(plus(stay[rows], got[rows]))
+    last = (sent[-1], totals)
     for step in range(1, steps):
-        for which, (_, _, order) in enumerate(plan):
+        for which in reversed(range(len(plan))):
+            order = plan[which][2]
+            came[which] = after(came[which], last)
             middle = left[which].shape[0] // 2
             piece = plus(left[which][middle:], came[which][middle:])
+            rest = plus(left[which][:middle], came[which][:middle])
             if which == 0 and step == 1:
-                piece, far, near = lax.optimization_barrier((piece, far, near))
+                far, near = after(far, piece), after(near, piece)
                 far = lax.ppermute(far, "seq", [(i, i - 2) for i in range(2, n_seq)])
                 near = lax.ppermute(near, "seq", [(i, i - 1) for i in range(1, n_seq)])
-                first_piece = piece
-            if which == 2 and step == 2:
-                piece, first_piece = lax.optimization_barrier((piece, first_piece))
             if which == 0 and step == steps - 1:
-                piece, far, near, mine, gathered = lax.optimization_barrier((piece, far, near, mine, gathered))
-            rest = plus(left[which][:middle], came[which][:middle])
+                far, near, mine = after(far, piece), after(near, piece), after(mine, piece)
+                rest, gathered = lax.optimization_barrier((rest, gathered))
             came[which] = swap(piece, order[step])
             left[which] = rest
+            last = piece
     pairs = list(zip(left, came))
     totals = jnp.sum(gathered[:, : 3 * dt], axis=0).reshape(3, width)
     correction = 1.0 - first_decay**STEP

time: 287 us -> 279 us (0.972)
  local copies, waits for them, and re-layouts: 14.1 us -> 8.6 us
  waiting for transfers between devices: 119 us -> 116 us
    unnamed x50 -> x61, local copies, waits for them, and re-layouts: 8.33 us -> 3.64 us
    ppermute x25 -> x32, waiting for transfers between devices: 119 us -> 116 us  [swap(): return lax.ppermute(x, axes, [(i, i ^ bit) for i in range(devices)])]
    ppermute x25 -> x32, starting transfers between devices: 29.3 us -> 31.2 us  [swap(): return lax.ppermute(x, axes, [(i, i ^ bit) for i in range(devices)])]
    convert_element_type x15 -> x13, other arithmetic: 25.5 us -> 25.1 us  [plus(): return (a.astype(F32) + b.astype(F32)).astype(BF)]
  transfers between devices with their start and end apart: 33 -> 40, of which waited for: 18 -> 19; matrix products, arithmetic and copies ran while one was open for 10% -> 13% of each run, Pallas kernels for 4% -> 4%
where the time goes in v3:
time: 279 us; the launch traced here: 278 us
  waiting for transfers between devices  116 us (42%)
  Pallas kernels  62.8 us (23%)
  starting transfers between devices  43.3 us (16%)
  other arithmetic  31.9 us (11%)
  between operations  16 us (6%)
  local copies, waits for them, and re-layouts  8.6 us (3%)
    ppermute x32, waiting for transfers between devices, swap(): return lax.ppermute(x, axes, [(i, i ^ bit) for i in range(devices)])  116 us
    pallas_call x1, Pallas kernels, local(): pl.pallas_call(functools.partial(layer_kernel, tiles, sizes), out_shape=(...  41.2 us
    ppermute x32, starting transfers between devices, swap(): return lax.ppermute(x, axes, [(i, i ^ bit) for i in range(devices)])  31.2 us
    convert_element_type x13, other arithmetic, plus(): return (a.astype(F32) + b.astype(F32)).astype(BF)  25.1 us
    ppermute x2, starting transfers between devices, local(): lax.ppermute(mine_tok, 'seq', [(i, i + step) for i in range(n_seq - step)])  6.38 us
    pallas_call x1, Pallas kernels, local(): pl.pallas_call(qkv_kernel, out_shape=sums_shapes, in_specs=[sm] + [hbm] *...  6.28 us
  transfers between devices with their start and end apart: 40, of which 19 were waited for; matrix products, arithmetic and copies ran while one was open for 13% of the time, Pallas kernels for 4%

profile of v3, /device:TPU:0, one launch (start us, length us, event | category | flops | bytes accessed | tf_op | source)
XLA Modules:
  0.0 278.4 jit_solution(5859230011394450049)
XLA Ops:
  9.3 4.9 %collective-permute-start.2 = (bf16[256,768]{1,0:T(8,128)(2,1)S(1)}, bf16[256,768]{1,0:T(8,128)(2,1)S(1)}, u32[]{:S(2)}, u32[]{:S(2)}) collective-permute-start(bf16[256,768]{1,0:T(8,128)(2,1)S(1)} %bitcast.10), channel_id=1, source_target_pairs={{0,2},{1,3},{4,6},{5,7},{8,10},{9,11},{12,14},{13,15},{16,18},{17,... | collective-permute-start | bytes 1179656 | tf_op jit(solution)/shard_map/ppermute | solution.py:649
  21.7 7.6 %collective-permute-done = bf16[4,128,128]{2,1,0:T(8,128)(2,1)S(1)} collective-permute-done((bf16[4,128,128]{2,1,0:T(8,128)(2,1)S(1)}, bf16[4,128,128]{2,1,0:T(8,128)(2,1)S(1)}, u32[]{:S(2)}, u32[]{:S(2)}) %collective-permute-start) | collective-permute-done | bytes 131104 | tf_op jit(solution)/shard_map/ppermute | solution.py:615
  32.9 6.2 %collective-permute-done.1 = bf16[8,128,128]{2,1,0:T(8,128)(2,1)S(1)} collective-permute-done((bf16[8,128,128]{2,1,0:T(8,128)(2,1)S(1)}, bf16[8,128,128]{2,1,0:T(8,128)(2,1)S(1)}, u32[]{:S(2)}, u32[]{:S(2)}) %collective-permute-start.1) | collective-permute-done | bytes 262176 | tf_op jit(solution)/shard_map/ppermute | solution.py:615
  41.8 3.5 %collective-permute-done.9 = bf16[8,128,128]{2,1,0:T(8,128)(2,1)S(1)} collective-permute-done((bf16[8,128,128]{2,1,0:T(8,128)(2,1)S(1)}, bf16[8,128,128]{2,1,0:T(8,128)(2,1)S(1)}, u32[]{:S(2)}, u32[]{:S(2)}) %collective-permute-start.9) | collective-permute-done | bytes 262176 | tf_op jit(solution)/shard_map/ppermute | solution.py:615
  47.2 8.0 %collective-permute-done.4 = bf16[16,128,128]{2,1,0:T(8,128)(2,1)S(1)} collective-permute-done((bf16[16,128,128]{2,1,0:T(8,128)(2,1)S(1)}, bf16[16,128,128]{2,1,0:T(8,128)(2,1)S(1)}, u32[]{:S(2)}, u32[]{:S(2)}) %collective-permute-start.4) | collective-permute-done | bytes 524320 | tf_op jit(solution)/shard_map/ppermute | solution.py:615
  58.9 8.6 %collective-permute-done.16 = bf16[12,128,128]{2,1,0:T(8,128)(2,1)S(1)} collective-permute-done((bf16[12,128,128]{2,1,0:T(8,128)(2,1)S(1)}, bf16[12,128,128]{2,1,0:T(8,128)(2,1)S(1)}, u32[]{:S(2)}, u32[]{:S(2)}) %collective-permute-start.16) | collective-permute-done | bytes 393248 | tf_op jit(solution)/shard_map/ppermute | solution.py:615
  68.2 25.3 %collective-permute-done.17.refs_19_ = bf16[24,128,128]{2,1,0:T(8,128)(2,1)} collective-permute-done((bf16[24,128,128]{2,1,0:T(8,128)(2,1)S(1)}, bf16[24,128,128]{2,1,0:T(8,128)(2,1)}, u32[]{:S(2)}, u32[]{:S(2)}) %collective-permute-start.17) | collective-permute-done | bytes 786464 | tf_op jit(solution)/shard_map/ppermute | solution.py:615
  97.7 2.9 %collective-permute-done.19.refs_21_ = bf16[24,128,128]{2,1,0:T(8,128)(2,1)} collective-permute-done((bf16[24,128,128]{2,1,0:T(8,128)(2,1)}, bf16[24,128,128]{2,1,0:T(8,128)(2,1)}, u32[]{:S(2)}, u32[]{:S(2)}) %collective-permute-start.19) | collective-permute-done | bytes 786464 | tf_op jit(solution)/shard_map/ppermute | solution.py:615
  100.6 41.2 %layer.1 = (bf16[256,768]{1,0:T(8,128)(2,1)}, f32[256,768]{1,0:T(8,128)}, bf16[256,768]{1,0:T(8,128)(2,1)}, bf16[768,768]{1,0:T(8,128)(2,1)}, bf16[768,768]{1,0:...) custom-call(s32[448]{0:T(512)} %get-tuple-element.67.refs_0_, ...), custom_call_target="tpu_custom_call" | custom-call | tf_op jit(solution)/shard_map/layer/pallas_call | solution.py:681
  144.6 6.3 %qkv_grad.1 = (bf16[224,128,128]{2,1,0:T(8,128)(2,1)}, bf16[96,128,128]{2,1,0:T(8,128)(2,1)}, bf16[128,128,128]{2,1,0:T(8,128)(2,1)}) custom-call(s32[448]{0:T(512)} %get-tuple-element.68.refs_1_.dst, bf16[256,768]{1,0:T(8,128)(2,1)} %get-tuple-element.81.gq_h, ...), custom_call_target="tpu_custom_call", output_to_operand_aliasing={{0}: (5, {}), {1}: (6, {}), {2}: (7, {})} | custom-call | flops 2113929216 | bytes 8388608 | tf_op jit(solution)/shard_map/qkv_grad/pallas_call | solution.py:763
  151.5 4.8 %head_grad.1 = (bf16[256,128]{1,0:T(8,128)(2,1)}, bf16[768,128]{1,0:T(8,128)(2,1)}, bf16[224,128,128]{2,1,0:T(8,128)(2,1)}, bf16[96,128,128]{2,1,0:T(8,128)(2,1)}, bf16[128,128,128]{2,1,0:T(8,128)(2,1)}) custom-call(s32[448]{0:T(512)} %get-tuple-element.68.refs_1_.dst, ...), custom_call_target="tpu_custom_call", output_to_operand_aliasing={{2}: (10, {}), {3}: (11, {}), {4}: (12, {})} | custom-call | flops 1073741824 | bytes 4194304 | tf_op jit(solution)/shard_map/head_grad/pallas_call | solution.py:784
  157.6 5.5 %collective-permute-done.22 = bf16[96,128,128]{2,1,0:T(8,128)(2,1)S(1)} collective-permute-done((bf16[96,128,128]{2,1,0:T(8,128)(2,1)}, bf16[96,128,128]{2,1,0:T(8,128)(2,1)S(1)}, u32[]{:S(2)}, u32[]{:S(2)}) %collective-permute-start.22) | collective-permute-done | bytes 3145760 | tf_op jit(solution)/shard_map/ppermute | solution.py:615
  163.4 4.3 %add_convert_fusion = (bf16[48,128,128]{2,1,0:T(8,128)(2,1)S(1)}, bf16[48,128,128]{2,1,0:T(8,128)(2,1)}) fusion(bf16[96,128,128]{2,1,0:T(8,128)(2,1)S(1)} %collective-permute-done.22, bf16[224,128,128]{2,1,0:T(8,128)(2,1)} %get-tuple-element.92), kind=kLoop, calls=%fused_computation | loop fusion | flops 6291456 | bytes 9437184 | tf_op jit(solution)/shard_map/convert_element_type | solution.py:808
  170.4 4.0 %add_convert_fusion.3 = bf16[40,128,128]{2,1,0:T(8,128)(2,1)} fusion(bf16[128,128,128]{2,1,0:T(8,128)(2,1)S(1)} %collective-permute-done.23, bf16[224,128,128]{2,1,0:T(8,128)(2,1)} %get-tuple-element.92), kind=kLoop, calls=%fused_computation.3 | loop fusion | flops 2621440 | bytes 3932160 | tf_op jit(solution)/shard_map/convert_element_type | solution.py:808
  179.5 3.4 %pre_grad.1 = (bf16[256,768]{1,0:T(8,128)(2,1)}, bf16[256,768]{1,0:T(8,128)(2,1)}, f32[256,768]{1,0:T(8,128)S(1)}, f32[8,768]{1,0:T(8,128)S(1)}) custom-call(bf16[768,768]{1,0:T(8,128)(2,1)S(1)} %copy-done.1, bf16[256,128]{1,0:T(8,128)(2,1)S(1)} %copy-done.16, bf16[768,128]{1,0:T(8,128)(2,1)S(1)} %copy-done.15, bf16[256,768]{1,0:T(8,128)(2,1)S(1)} %copy-done.4, ...), custom_call_target="tpu_custom_call" | custom-call | flops 2113929216 | bytes 10485760 | tf_op jit(solution)/shard_map/pre_grad/pallas_call | solution.py:829
  187.9 9.7 %collective-permute-done.26 = bf16[24,128,128]{2,1,0:T(8,128)(2,1)} collective-permute-done((bf16[24,128,128]{2,1,0:T(8,128)(2,1)S(1)}, bf16[24,128,128]{2,1,0:T(8,128)(2,1)}, u32[]{:S(2)}, u32[]{:S(2)}) %collective-permute-start.26) | collective-permute-done | bytes 786464 | tf_op jit(solution)/shard_map/ppermute | solution.py:615
  202.4 3.8 %collective-permute-done.25 = bf16[40,128,128]{2,1,0:T(8,128)(2,1)} collective-permute-done((bf16[40,128,128]{2,1,0:T(8,128)(2,1)}, bf16[40,128,128]{2,1,0:T(8,128)(2,1)}, u32[]{:S(2)}, u32[]{:S(2)}) %collective-permute-start.25) | collective-permute-done | bytes 1310752 | tf_op jit(solution)/shard_map/ppermute | solution.py:615
  209.1 2.8 %add_convert_fusion.4 = (bf16[24,128,128]{2,1,0:T(8,128)(2,1)}, bf16[24,128,128]{2,1,0:T(8,128)(2,1)S(1)}) fusion(bf16[48,128,128]{2,1,0:T(8,128)(2,1)S(1)} %get-tuple-element.130, bf16[48,128,128]{2,1,0:T(8,128)(2,1)} %collective-permute-done.24), kind=kLoop, calls=%fused_computation.4 | loop fusion | flops 3145728 | bytes 4718592 | tf_op jit(solution)/shard_map/convert_element_type | solution.py:808
  213.7 6.6 %collective-permute-done.29 = bf16[12,128,128]{2,1,0:T(8,128)(2,1)} collective-permute-done((bf16[12,128,128]{2,1,0:T(8,128)(2,1)}, bf16[12,128,128]{2,1,0:T(8,128)(2,1)}, u32[]{:S(2)}, u32[]{:S(2)}) %collective-permute-start.29) | collective-permute-done | bytes 393248 | tf_op jit(solution)/shard_map/ppermute | solution.py:615
  226.8 8.3 %collective-permute-done.28 = bf16[20,128,128]{2,1,0:T(8,128)(2,1)} collective-permute-done((bf16[20,128,128]{2,1,0:T(8,128)(2,1)}, bf16[20,128,128]{2,1,0:T(8,128)(2,1)}, u32[]{:S(2)}, u32[]{:S(2)}) %collective-permute-start.28) | collective-permute-done | bytes 655392 | tf_op jit(solution)/shard_map/ppermute | solution.py:615
  240.8 9.6 %collective-permute-done.31 = bf16[10,128,128]{2,1,0:T(8,128)(2,1)S(1)} collective-permute-done((bf16[10,128,128]{2,1,0:T(8,128)(2,1)S(1)}, bf16[10,128,128]{2,1,0:T(8,128)(2,1)S(1)}, u32[]{:S(2)}, u32[]{:S(2)}) %collective-permute-start.31) | collective-permute-done | bytes 327712 | tf_op jit(solution)/shard_map/ppermute | solution.py:615
  252.0 2.9 %collective-permute-start.35 = (bf16[6,128,128]{2,1,0:T(8,128)(2,1)}, bf16[6,128,128]{2,1,0:T(8,128)(2,1)}, u32[]{:S(2)}, u32[]{:S(2)}) collective-permute-start(bf16[6,128,128]{2,1,0:T(8,128)(2,1)} %get-tuple-element.143), channel_id=1, source_target_pairs={{0,16},{1,17},{2,18},{3,19},{4,20},{5,21},{6,22},{7,23},{8,24},{9,... | collective-permute-start | bytes 589832 | tf_op jit(solution)/shard_map/ppermute | solution.py:615
  261.1 3.2 %collective-permute-done.36.refs_3_ = bf16[5,128,128]{2,1,0:T(8,128)(2,1)} collective-permute-done((bf16[5,128,128]{2,1,0:T(8,128)(2,1)}, bf16[5,128,128]{2,1,0:T(8,128)(2,1)}, u32[]{:S(2)}, u32[]{:S(2)}) %collective-permute-start.36) | collective-permute-done | bytes 163872 | tf_op jit(solution)/shard_map/ppermute | solution.py:615
  267.2 4.4 %adam.1 = (f32[14,128,128]{2,1,0:T(8,128)}, f32[14,128,128]{2,1,0:T(8,128)}, f32[14,128,128]{2,1,0:T(8,128)}) custom-call(bf16[6,128,128]{2,1,0:T(8,128)(2,1)S(1)} %get-tuple-element.121.refs_0_, bf16[6,128,128]{2,1,0:T(8,128)(2,1)} %collective-permute-done.35.refs_1_, bf16[5,128,128]{2,1,0:T(8,128)(2,1)S(1)} %get-tuple-element.146.refs_2_, ...), custom_call_target="tpu_custom_call" | custom-call | tf_op jit(solution)/shard_map/adam/pallas_call | solution.py:879
  (171 shorter events, 74.7 us)
Async XLA Ops:
  7.2 93.4 %all-gather.4.cloned.1.call-start = ((), (), s32[]{:S(2)}) async-start(), calls=%async_computation | async-start | bytes 3244032 | tf_op jit(solution)/shard_map/all_gather | solution.py:661
  9.2 242.7 %all-gather.6.cloned.1.call-start = ((), (), s32[]{:S(2)}) async-start(), calls=%async_computation.1 | async-start | bytes 1081344 | tf_op jit(solution)/shard_map/all_gather | solution.py:856
  9.3 29.9 %collective-permute-start.2 = (bf16[256,768]{1,0:T(8,128)(2,1)S(1)}, bf16[256,768]{1,0:T(8,128)(2,1)S(1)}, u32[]{:S(2)}, u32[]{:S(2)}) collective-permute-start(bf16[256,768]{1,0:T(8,128)(2,1)S(1)} %bitcast.10), channel_id=1, source_target_pairs={{0,2},{1,3},{4,6},{5,7},{8,10},{9,11},{12,14},{13,15},{16,18},{17,... | collective-permute-start | bytes 1179656 | tf_op jit(solution)/shard_map/ppermute | solution.py:649
  14.2 25.0 %collective-permute-start.3 = (bf16[256,768]{1,0:T(8,128)(2,1)S(1)}, bf16[256,768]{1,0:T(8,128)(2,1)S(1)}, u32[]{:S(2)}, u32[]{:S(2)}) collective-permute-start(bf16[256,768]{1,0:T(8,128)(2,1)S(1)} %bitcast.11), channel_id=1, source_target_pairs={{0,1},{1,2},{2,3},{4,5},{5,6},{6,7},{8,9},{9,10},{10,11},{12,13},{... | collective-permute-start | bytes 1179656 | tf_op jit(solution)/shard_map/ppermute | solution.py:649
  30.7 14.7 %collective-permute-start.15 = (bf16[6,128,128]{2,1,0:T(8,128)(2,1)S(1)}, bf16[6,128,128]{2,1,0:T(8,128)(2,1)S(1)}, u32[]{:S(2)}, u32[]{:S(2)}) collective-permute-start(bf16[6,128,128]{2,1,0:T(8,128)(2,1)S(1)} %pad_maximum_fusion.8), channel_id=1, source_target_pairs={{0,2},{1,3},{2,0},{3,1},{4,6},{5,7},{6,4},{7,5},{8,10},{9,11},{10,... | collective-permute-start | bytes 589832 | tf_op jit(solution)/shard_map/ppermute | solution.py:615
  40.3 14.9 %collective-permute-start.4 = (bf16[16,128,128]{2,1,0:T(8,128)(2,1)S(1)}, bf16[16,128,128]{2,1,0:T(8,128)(2,1)S(1)}, u32[]{:S(2)}, u32[]{:S(2)}) collective-permute-start(bf16[16,128,128]{2,1,0:T(8,128)(2,1)S(1)} %pad_maximum_fusion.3), channel_id=1, source_target_pairs={{0,4},{1,5},{2,6},{3,7},{4,0},{5,1},{6,2},{7,3},{8,12},{9,13},{10,... | collective-permute-start | bytes 1572872 | tf_op jit(solution)/shard_map/ppermute | solution.py:615
  45.5 22.0 %collective-permute-start.16 = (bf16[12,128,128]{2,1,0:T(8,128)(2,1)S(1)}, bf16[12,128,128]{2,1,0:T(8,128)(2,1)S(1)}, u32[]{:S(2)}, u32[]{:S(2)}) collective-permute-start(bf16[12,128,128]{2,1,0:T(8,128)(2,1)S(1)} %pad_maximum_fusion.5), channel_id=1, source_target_pairs={{0,16},{1,17},{2,18},{3,19},{4,20},{5,21},{6,22},{7,23},{8,24},{9,... | collective-permute-start | bytes 1179656 | tf_op jit(solution)/shard_map/ppermute | solution.py:615
  55.4 38.1 %collective-permute-start.5 = (bf16[32,128,128]{2,1,0:T(8,128)(2,1)S(1)}, bf16[32,128,128]{2,1,0:T(8,128)(2,1)}, u32[]{:S(2)}, u32[]{:S(2)}) collective-permute-start(bf16[32,128,128]{2,1,0:T(8,128)(2,1)S(1)} %constant_dynamic-update-slice_fusion.refs_10_), channel_id=1, source_target_pairs={{0,2},{1,3},{2,0},{3,1},{4,6},{5,7},{6,4},{7,5},{8,10},{9,11},{10,... | collective-permute-start | bytes 3145736 | tf_op jit(solution)/shard_map/ppermute | solution.py:615
  57.6 36.3 %collective-permute-start.11 = (bf16[32,128,128]{2,1,0:T(8,128)(2,1)S(1)}, bf16[32,128,128]{2,1,0:T(8,128)(2,1)}, u32[]{:S(2)}, u32[]{:S(2)}) collective-permute-start(bf16[32,128,128]{2,1,0:T(8,128)(2,1)S(1)} %pad_maximum_fusion.1.refs_14_), channel_id=1, source_target_pairs={{0,4},{1,5},{2,6},{3,7},{4,0},{5,1},{6,2},{7,3},{8,12},{9,13},{10,... | collective-permute-start | bytes 3145736 | tf_op jit(solution)/shard_map/ppermute | solution.py:615
  67.5 25.9 %collective-permute-start.17 = (bf16[24,128,128]{2,1,0:T(8,128)(2,1)S(1)}, bf16[24,128,128]{2,1,0:T(8,128)(2,1)}, u32[]{:S(2)}, u32[]{:S(2)}) collective-permute-start(bf16[24,128,128]{2,1,0:T(8,128)(2,1)S(1)} %pad_maximum_fusion.2.refs_18_), channel_id=1, source_target_pairs={{0,8},{1,9},{2,10},{3,11},{4,12},{5,13},{6,14},{7,15},{8,0},{9,1},... | collective-permute-start | bytes 2359304 | tf_op jit(solution)/shard_map/ppermute | solution.py:615
  67.6 26.4 %collective-permute-start.18 = (bf16[24,128,128]{2,1,0:T(8,128)(2,1)S(1)}, bf16[24,128,128]{2,1,0:T(8,128)(2,1)S(1)}, u32[]{:S(2)}, u32[]{:S(2)}) collective-permute-start(bf16[24,128,128]{2,1,0:T(8,128)(2,1)S(1)} %pad_maximum_fusion.2.refs_18_), channel_id=1, source_target_pairs={{0,1},{1,0},{2,3},{3,2},{4,5},{5,4},{6,7},{7,6},{8,9},{9,8},{10,11... | collective-permute-start | bytes 2359304 | tf_op jit(solution)/shard_map/ppermute | solution.py:615
  67.7 29.3 %collective-permute-start.6 = (bf16[32,128,128]{2,1,0:T(8,128)(2,1)S(1)}, bf16[32,128,128]{2,1,0:T(8,128)(2,1)}, u32[]{:S(2)}, u32[]{:S(2)}) collective-permute-start(bf16[32,128,128]{2,1,0:T(8,128)(2,1)S(1)} %constant_dynamic-update-slice_fusion.refs_10_), channel_id=1, source_target_pairs={{0,1},{1,0},{2,3},{3,2},{4,5},{5,4},{6,7},{7,6},{8,9},{9,8},{10,11... | collective-permute-start | bytes 3145736 | tf_op jit(solution)/shard_map/ppermute | solution.py:615
  167.8 41.3 %collective-permute-start.24 = (bf16[48,128,128]{2,1,0:T(8,128)(2,1)}, bf16[48,128,128]{2,1,0:T(8,128)(2,1)}, u32[]{:S(2)}, u32[]{:S(2)}) collective-permute-start(bf16[48,128,128]{2,1,0:T(8,128)(2,1)} %get-tuple-element.131), channel_id=1, source_target_pairs={{0,2},{1,3},{2,0},{3,1},{4,6},{5,7},{6,4},{7,5},{8,10},{9,11},{10,... | collective-permute-start | bytes 4718600 | tf_op jit(solution)/shard_map/ppermute | solution.py:615
  174.5 31.7 %collective-permute-start.25 = (bf16[40,128,128]{2,1,0:T(8,128)(2,1)}, bf16[40,128,128]{2,1,0:T(8,128)(2,1)}, u32[]{:S(2)}, u32[]{:S(2)}) collective-permute-start(bf16[40,128,128]{2,1,0:T(8,128)(2,1)} %add_convert_fusion.3), channel_id=1, source_target_pairs={{0,4},{1,5},{2,6},{3,7},{4,0},{5,1},{6,2},{7,3},{8,12},{9,13},{10,... | collective-permute-start | bytes 3932168 | tf_op jit(solution)/shard_map/ppermute | solution.py:615
  178.0 19.7 %collective-permute-start.26 = (bf16[24,128,128]{2,1,0:T(8,128)(2,1)S(1)}, bf16[24,128,128]{2,1,0:T(8,128)(2,1)}, u32[]{:S(2)}, u32[]{:S(2)}) collective-permute-start(bf16[24,128,128]{2,1,0:T(8,128)(2,1)S(1)} %get-tuple-element.129), channel_id=1, source_target_pairs={{0,8},{1,9},{2,10},{3,11},{4,12},{5,13},{6,14},{7,15},{8,0},{9,1},... | collective-permute-start | bytes 2359304 | tf_op jit(solution)/shard_map/ppermute | solution.py:615
  199.9 20.4 %collective-permute-start.29 = (bf16[12,128,128]{2,1,0:T(8,128)(2,1)}, bf16[12,128,128]{2,1,0:T(8,128)(2,1)}, u32[]{:S(2)}, u32[]{:S(2)}) collective-permute-start(bf16[12,128,128]{2,1,0:T(8,128)(2,1)} %get-tuple-element.139), channel_id=1, source_target_pairs={{0,16},{1,17},{2,18},{3,19},{4,20},{5,21},{6,22},{7,23},{8,24},{9,... | collective-permute-start | bytes 1179656 | tf_op jit(solution)/shard_map/ppermute | solution.py:615
  208.8 26.3 %collective-permute-start.28 = (bf16[20,128,128]{2,1,0:T(8,128)(2,1)}, bf16[20,128,128]{2,1,0:T(8,128)(2,1)}, u32[]{:S(2)}, u32[]{:S(2)}) collective-permute-start(bf16[20,128,128]{2,1,0:T(8,128)(2,1)} %get-tuple-element.135), channel_id=1, source_target_pairs={{0,8},{1,9},{2,10},{3,11},{4,12},{5,13},{6,14},{7,15},{8,0},{9,1},... | collective-permute-start | bytes 1966088 | tf_op jit(solution)/shard_map/ppermute | solution.py:615
  211.9 27.0 %collective-permute-start.27 = (bf16[24,128,128]{2,1,0:T(8,128)(2,1)}, bf16[24,128,128]{2,1,0:T(8,128)(2,1)S(1)}, u32[]{:S(2)}, u32[]{:S(2)}) collective-permute-start(bf16[24,128,128]{2,1,0:T(8,128)(2,1)} %get-tuple-element.132), channel_id=1, source_target_pairs={{0,4},{1,5},{2,6},{3,7},{4,0},{5,1},{6,2},{7,3},{8,12},{9,13},{10,... | collective-permute-start | bytes 2359304 | tf_op jit(solution)/shard_map/ppermute | solution.py:615
  221.6 17.6 %collective-permute-start.32 = (bf16[6,128,128]{2,1,0:T(8,128)(2,1)S(1)}, bf16[6,128,128]{2,1,0:T(8,128)(2,1)S(1)}, u32[]{:S(2)}, u32[]{:S(2)}) collective-permute-start(bf16[6,128,128]{2,1,0:T(8,128)(2,1)S(1)} %get-tuple-element.145), channel_id=1, source_target_pairs={{0,2},{1,3},{2,0},{3,1},{4,6},{5,7},{6,4},{7,5},{8,10},{9,11},{10,... | collective-permute-start | bytes 589832 | tf_op jit(solution)/shard_map/ppermute | solution.py:615
  223.9 32.7 %collective-permute-start.34 = (bf16[256,768]{1,0:T(8,128)(2,1)}, bf16[256,768]{1,0:T(8,128)(2,1)}, u32[]{:S(2)}, u32[]{:S(2)}) collective-permute-start(bf16[256,768]{1,0:T(8,128)(2,1)} %get-tuple-element.118), channel_id=1, source_target_pairs={{2,0},{3,1},{6,4},{7,5},{10,8},{11,9},{14,12},{15,13},{18,16},{19,... | collective-permute-start | bytes 1179656 | tf_op jit(solution)/shard_map/ppermute | solution.py:867
  225.2 31.4 %collective-permute-start.33 = (bf16[256,768]{1,0:T(8,128)(2,1)}, bf16[256,768]{1,0:T(8,128)(2,1)}, u32[]{:S(2)}, u32[]{:S(2)}) collective-permute-start(bf16[256,768]{1,0:T(8,128)(2,1)} %get-tuple-element.115), channel_id=1, source_target_pairs={{1,0},{2,1},{3,2},{5,4},{6,5},{7,6},{9,8},{10,9},{11,10},{13,12},{... | collective-permute-start | bytes 1179656 | tf_op jit(solution)/shard_map/ppermute | solution.py:868
  236.3 14.1 %collective-permute-start.31 = (bf16[10,128,128]{2,1,0:T(8,128)(2,1)S(1)}, bf16[10,128,128]{2,1,0:T(8,128)(2,1)S(1)}, u32[]{:S(2)}, u32[]{:S(2)}) collective-permute-start(bf16[10,128,128]{2,1,0:T(8,128)(2,1)S(1)} %get-tuple-element.141), channel_id=1, source_target_pairs={{0,2},{1,3},{2,0},{3,1},{4,6},{5,7},{6,4},{7,5},{8,10},{9,11},{10,... | collective-permute-start | bytes 983048 | tf_op jit(solution)/shard_map/ppermute | solution.py:615
  239.9 21.2 %collective-permute-start.37 = (bf16[3,128,128]{2,1,0:T(8,128)(2,1)}, bf16[3,128,128]{2,1,0:T(8,128)(2,1)}, u32[]{:S(2)}, u32[]{:S(2)}) collective-permute-start(bf16[3,128,128]{2,1,0:T(8,128)(2,1)} %get-tuple-element.153), channel_id=1, source_target_pairs={{0,4},{1,5},{2,6},{3,7},{4,0},{5,1},{6,2},{7,3},{8,12},{9,13},{10,... | collective-permute-start | bytes 294920 | tf_op jit(solution)/shard_map/ppermute | solution.py:615
  252.0 15.2 %collective-permute-start.35 = (bf16[6,128,128]{2,1,0:T(8,128)(2,1)}, bf16[6,128,128]{2,1,0:T(8,128)(2,1)}, u32[]{:S(2)}, u32[]{:S(2)}) collective-permute-start(bf16[6,128,128]{2,1,0:T(8,128)(2,1)} %get-tuple-element.143), channel_id=1, source_target_pairs={{0,16},{1,17},{2,18},{3,19},{4,20},{5,21},{6,22},{7,23},{8,24},{9,... | collective-permute-start | bytes 589832 | tf_op jit(solution)/shard_map/ppermute | solution.py:615
  (46 other events, 485.9 us)
Sparse Core Ops, SparseCore 0:
  11.5 76.9 all-gather.3
  185.9 65.2 all-gather.5

commit v4 on v3

--- a/solution.py
+++ b/solution.py
@@ -472,7 +472,9 @@
     wait_tiles(stage, sums, gsem)
 
 
-def pre_kernel(tok, gq_head, gk_head, gq_h, gk_h, gv_h, wqkv_h, far, near, mine, small, gq, gk, gv, wqkv, lsem):
+def pre_kernel(
+    row_at, tok, small, gq_head, gk_head, gq_h, gk_h, gv_h, wqkv_h, far, near, mine, totals, gq, gk, gv, wqkv, lsem
+):
     own, width = gq.shape
     window = gk.shape[0]
     side = gq_head.shape[1]
@@ -497,7 +499,13 @@
             near[...] = g.astype(near.dtype)
         hat, _ = norm_parts(tok[rows, :].astype(F32))
         total = total + jnp.sum(g * hat, axis=0, keepdims=True)
-    small[...] = jnp.broadcast_to(total, small.shape)
+    totals[...] = jnp.zeros_like(totals)
+    spots = lax.broadcasted_iota(jnp.int32, (1, width), 1)
+    placed = jnp.where(spots == row_at[0], small[1:2, :], 0.0)
+    for index, line in enumerate((total, small[0:1, :], placed)):
+        for i in range(width // side):
+            at = index * (width // side) + i
+            totals[at : at + 1, :] = line[:, i * side : (i + 1) * side]
 
 
 def input_kernel(tok, gains, ghid, mine, near, far, out):
@@ -823,18 +831,19 @@
     for which in range(1, len(plan)):
         got[1] = after(got[1], sent[-1])
         sent.append(from_got(which, 1, 2))
-    gq_head = after(gq_head, sent[-1])
     came = [swap(piece, order[0]) for piece, (_, _, order) in zip(sent, plan)]
     left = [from_got(which, 0, 1) for which in range(len(plan))]
-    far, near, mine, small_pre = pl.pallas_call(
+    gq_head = after(gq_head, sent[-1])
+    row_at = lax.axis_index("dp")
+    far, near, mine, totals = pl.pallas_call(
         pre_kernel,
         out_shape=(
             shp((own, width), BF),
             shp((own, width), BF),
             shp((own, width), F32),
-            shp((8, width), F32),
+            shp((side // 2, side), F32),
         ),
-        in_specs=[vm] * 3 + [hbm] * 4,
+        in_specs=[sm] + [vm] * 4 + [hbm] * 4,
         out_specs=tuple([vm] * 4),
         scratch_shapes=[
             VMEM((own, width), BF),
@@ -848,11 +857,7 @@
             flops=2 * (2 * window + own) * width * width, bytes_accessed=10 << 20, transcendentals=0
         ),
         name="pre_grad",
-    )(tok, gq_head, gk_head, gq, gk, gv, wqkv)
-    row_at = lax.axis_index("dp")
-    spots = jnp.arange(width, dtype=jnp.int32)
-    totals = jnp.stack([small_pre[0], small[0], jnp.where(spots == row_at, small[1], 0.0)])
-    totals = jnp.pad(totals.reshape(3 * dt, side), ((0, side // 2 - 3 * dt), (0, 0)))
+    )(row_at[None], tok, small, gq_head, gk_head, gq, gk, gv, wqkv)
     gathered = lax.all_gather(totals, axes)
     last = (sent[-1], totals)
     for step in range(1, steps):
@@ -862,7 +867,7 @@
             middle = left[which].shape[0] // 2
             piece = plus(left[which][middle:], came[which][middle:])
             rest = plus(left[which][:middle], came[which][:middle])
-            if which == 0 and step == 1:
+            if which == 1 and step == steps - 1:
                 far, near = after(far, piece), after(near, piece)
                 far = lax.ppermute(far, "seq", [(i, i - 2) for i in range(2, n_seq)])
                 near = lax.ppermute(near, "seq", [(i, i - 1) for i in range(1, n_seq)])

time: 279 us -> 280 us (level); the launches traced: 278 us -> 276 us
    ppermute x1, waiting for transfers between devices: 0.01 us -> 4.37 us  [local(): far = lax.ppermute(far, 'seq', [(i, i - 2) for i in range(2, n_seq)])]
  transfers between devices with their start and end apart: 40 -> 40, of which waited for: 19 -> 20; matrix products, arithmetic and copies ran while one was open for 13% -> 12% of each run, Pallas kernels for 4% -> 5%
where the time goes in v4:
time: 280 us; the launch traced here: 276 us
  waiting for transfers between devices  118 us (42%)
  Pallas kernels  63.5 us (23%)
  starting transfers between devices  41.5 us (15%)
  other arithmetic  31 us (11%)
  between operations  16 us (6%)
  local copies, waits for them, and re-layouts  6.68 us (2%)
    ppermute x32, waiting for transfers between devices, swap(): return lax.ppermute(x, axes, [(i, i ^ bit) for i in range(devices)])  113 us
    pallas_call x1, Pallas kernels, local(): pl.pallas_call(functools.partial(layer_kernel, tiles, sizes), out_shape=(...  41.2 us
    ppermute x32, starting transfers between devices, swap(): return lax.ppermute(x, axes, [(i, i ^ bit) for i in range(devices)])  29.4 us
    convert_element_type x13, other arithmetic, plus(): return (a.astype(F32) + b.astype(F32)).astype(BF)  25.2 us
    ppermute x2, starting transfers between devices, local(): lax.ppermute(mine_tok, 'seq', [(i, i + step) for i in range(n_seq - step)])  6.38 us
    pallas_call x1, Pallas kernels, local(): pl.pallas_call(qkv_kernel, out_shape=sums_shapes, in_specs=[sm] + [hbm] *...  6.29 us
  transfers between devices with their start and end apart: 40, of which 20 were waited for; matrix products, arithmetic and copies ran while one was open for 12% of the time, Pallas kernels for 5%

profile of v4, /device:TPU:0, one launch (start us, length us, event | category | flops | bytes accessed | tf_op | source)
XLA Modules:
  0.0 276.2 jit_solution(8420660495245354754)
XLA Ops:
  9.3 4.9 %collective-permute-start.2 = (bf16[256,768]{1,0:T(8,128)(2,1)S(1)}, bf16[256,768]{1,0:T(8,128)(2,1)S(1)}, u32[]{:S(2)}, u32[]{:S(2)}) collective-permute-start(bf16[256,768]{1,0:T(8,128)(2,1)S(1)} %bitcast.11), channel_id=1, source_target_pairs={{0,2},{1,3},{4,6},{5,7},{8,10},{9,11},{12,14},{13,15},{16,18},{17,... | collective-permute-start | bytes 1179656 | tf_op jit(solution)/shard_map/ppermute | solution.py:657
  21.7 7.6 %collective-permute-done = bf16[4,128,128]{2,1,0:T(8,128)(2,1)S(1)} collective-permute-done((bf16[4,128,128]{2,1,0:T(8,128)(2,1)S(1)}, bf16[4,128,128]{2,1,0:T(8,128)(2,1)S(1)}, u32[]{:S(2)}, u32[]{:S(2)}) %collective-permute-start) | collective-permute-done | bytes 131104 | tf_op jit(solution)/shard_map/ppermute | solution.py:623
  32.9 6.2 %collective-permute-done.1 = bf16[8,128,128]{2,1,0:T(8,128)(2,1)S(1)} collective-permute-done((bf16[8,128,128]{2,1,0:T(8,128)(2,1)S(1)}, bf16[8,128,128]{2,1,0:T(8,128)(2,1)S(1)}, u32[]{:S(2)}, u32[]{:S(2)}) %collective-permute-start.1) | collective-permute-done | bytes 262176 | tf_op jit(solution)/shard_map/ppermute | solution.py:623
  41.8 3.5 %collective-permute-done.9 = bf16[8,128,128]{2,1,0:T(8,128)(2,1)S(1)} collective-permute-done((bf16[8,128,128]{2,1,0:T(8,128)(2,1)S(1)}, bf16[8,128,128]{2,1,0:T(8,128)(2,1)S(1)}, u32[]{:S(2)}, u32[]{:S(2)}) %collective-permute-start.9) | collective-permute-done | bytes 262176 | tf_op jit(solution)/shard_map/ppermute | solution.py:623
  47.2 8.0 %collective-permute-done.4 = bf16[16,128,128]{2,1,0:T(8,128)(2,1)S(1)} collective-permute-done((bf16[16,128,128]{2,1,0:T(8,128)(2,1)S(1)}, bf16[16,128,128]{2,1,0:T(8,128)(2,1)S(1)}, u32[]{:S(2)}, u32[]{:S(2)}) %collective-permute-start.4) | collective-permute-done | bytes 524320 | tf_op jit(solution)/shard_map/ppermute | solution.py:623
  58.9 8.6 %collective-permute-done.16 = bf16[12,128,128]{2,1,0:T(8,128)(2,1)S(1)} collective-permute-done((bf16[12,128,128]{2,1,0:T(8,128)(2,1)S(1)}, bf16[12,128,128]{2,1,0:T(8,128)(2,1)S(1)}, u32[]{:S(2)}, u32[]{:S(2)}) %collective-permute-start.16) | collective-permute-done | bytes 393248 | tf_op jit(solution)/shard_map/ppermute | solution.py:623
  68.2 25.3 %collective-permute-done.17.refs_19_ = bf16[24,128,128]{2,1,0:T(8,128)(2,1)} collective-permute-done((bf16[24,128,128]{2,1,0:T(8,128)(2,1)S(1)}, bf16[24,128,128]{2,1,0:T(8,128)(2,1)}, u32[]{:S(2)}, u32[]{:S(2)}) %collective-permute-start.17) | collective-permute-done | bytes 786464 | tf_op jit(solution)/shard_map/ppermute | solution.py:623
  97.7 2.9 %collective-permute-done.19.refs_21_ = bf16[24,128,128]{2,1,0:T(8,128)(2,1)} collective-permute-done((bf16[24,128,128]{2,1,0:T(8,128)(2,1)}, bf16[24,128,128]{2,1,0:T(8,128)(2,1)}, u32[]{:S(2)}, u32[]{:S(2)}) %collective-permute-start.19) | collective-permute-done | bytes 786464 | tf_op jit(solution)/shard_map/ppermute | solution.py:623
  100.6 41.2 %layer.1 = (bf16[256,768]{1,0:T(8,128)(2,1)}, f32[256,768]{1,0:T(8,128)}, bf16[256,768]{1,0:T(8,128)(2,1)}, bf16[768,768]{1,0:T(8,128)(2,1)}, bf16[768,768]{1,0:...) custom-call(s32[448]{0:T(512)} %get-tuple-element.67.refs_0_, ...), custom_call_target="tpu_custom_call" | custom-call | tf_op jit(solution)/shard_map/layer/pallas_call | solution.py:689
  144.7 6.3 %qkv_grad.1 = (bf16[224,128,128]{2,1,0:T(8,128)(2,1)}, bf16[96,128,128]{2,1,0:T(8,128)(2,1)}, bf16[128,128,128]{2,1,0:T(8,128)(2,1)}) custom-call(s32[448]{0:T(512)} %get-tuple-element.68.refs_1_.dst, bf16[256,768]{1,0:T(8,128)(2,1)} %get-tuple-element.82.gq_h, ...), custom_call_target="tpu_custom_call", output_to_operand_aliasing={{0}: (5, {}), {1}: (6, {}), {2}: (7, {})} | custom-call | flops 2113929216 | bytes 8388608 | tf_op jit(solution)/shard_map/qkv_grad/pallas_call | solution.py:771
  151.6 4.8 %head_grad.1 = (bf16[256,128]{1,0:T(8,128)(2,1)}, bf16[768,128]{1,0:T(8,128)(2,1)}, bf16[224,128,128]{2,1,0:T(8,128)(2,1)}, bf16[96,128,128]{2,1,0:T(8,128)(2,1)}, bf16[128,128,128]{2,1,0:T(8,128)(2,1)}) custom-call(s32[448]{0:T(512)} %get-tuple-element.68.refs_1_.dst, ...), custom_call_target="tpu_custom_call", output_to_operand_aliasing={{2}: (10, {}), {3}: (11, {}), {4}: (12, {})} | custom-call | flops 1073741824 | bytes 4194304 | tf_op jit(solution)/shard_map/head_grad/pallas_call | solution.py:792
  157.7 5.5 %collective-permute-done.22 = bf16[96,128,128]{2,1,0:T(8,128)(2,1)S(1)} collective-permute-done((bf16[96,128,128]{2,1,0:T(8,128)(2,1)}, bf16[96,128,128]{2,1,0:T(8,128)(2,1)S(1)}, u32[]{:S(2)}, u32[]{:S(2)}) %collective-permute-start.22) | collective-permute-done | bytes 3145760 | tf_op jit(solution)/shard_map/ppermute | solution.py:623
  163.5 4.3 %add_convert_fusion = (bf16[48,128,128]{2,1,0:T(8,128)(2,1)S(1)}, bf16[48,128,128]{2,1,0:T(8,128)(2,1)}) fusion(bf16[96,128,128]{2,1,0:T(8,128)(2,1)S(1)} %collective-permute-done.22, bf16[224,128,128]{2,1,0:T(8,128)(2,1)} %get-tuple-element.93), kind=kLoop, calls=%fused_computation | loop fusion | flops 6291456 | bytes 9437184 | tf_op jit(solution)/shard_map/convert_element_type | solution.py:816
  170.5 4.0 %add_convert_fusion.3 = bf16[40,128,128]{2,1,0:T(8,128)(2,1)} fusion(bf16[128,128,128]{2,1,0:T(8,128)(2,1)S(1)} %collective-permute-done.23, bf16[224,128,128]{2,1,0:T(8,128)(2,1)} %get-tuple-element.93), kind=kLoop, calls=%fused_computation.3 | loop fusion | flops 2621440 | bytes 3932160 | tf_op jit(solution)/shard_map/convert_element_type | solution.py:816
  178.6 4.0 %pre_grad.1 = (bf16[256,768]{1,0:T(8,128)(2,1)}, bf16[256,768]{1,0:T(8,128)(2,1)}, f32[256,768]{1,0:T(8,128)S(1)}, f32[64,128]{1,0:T(8,128)}) custom-call(s32[1]{0:T(128)} %bitcast.6.row_at, bf16[768,768]{1,0:T(8,128)(2,1)S(1)} %copy-done.1, f32[8,768]{1,0:T(8,128)S(1)} %copy-done.17, bf16[256,128]{1,0:T(8,128)(2,1)S(1)} %copy-done.16, ...), custom_call_target="tpu_custom_call" | custom-call | flops 2113929216 | bytes 10485760 | tf_op jit(solution)/shard_map/pre_grad/pallas_call | solution.py:838
  185.7 12.3 %collective-permute-done.26 = bf16[24,128,128]{2,1,0:T(8,128)(2,1)} collective-permute-done((bf16[24,128,128]{2,1,0:T(8,128)(2,1)S(1)}, bf16[24,128,128]{2,1,0:T(8,128)(2,1)}, u32[]{:S(2)}, u32[]{:S(2)}) %collective-permute-start.26) | collective-permute-done | bytes 786464 | tf_op jit(solution)/shard_map/ppermute | solution.py:623
  202.6 3.7 %collective-permute-done.25 = bf16[40,128,128]{2,1,0:T(8,128)(2,1)} collective-permute-done((bf16[40,128,128]{2,1,0:T(8,128)(2,1)}, bf16[40,128,128]{2,1,0:T(8,128)(2,1)}, u32[]{:S(2)}, u32[]{:S(2)}) %collective-permute-start.25) | collective-permute-done | bytes 1310752 | tf_op jit(solution)/shard_map/ppermute | solution.py:623
  209.1 2.8 %add_convert_fusion.4 = (bf16[24,128,128]{2,1,0:T(8,128)(2,1)}, bf16[24,128,128]{2,1,0:T(8,128)(2,1)S(1)}) fusion(bf16[48,128,128]{2,1,0:T(8,128)(2,1)S(1)} %get-tuple-element.130, bf16[48,128,128]{2,1,0:T(8,128)(2,1)} %collective-permute-done.24), kind=kLoop, calls=%fused_computation.4 | loop fusion | flops 3145728 | bytes 4718592 | tf_op jit(solution)/shard_map/convert_element_type | solution.py:816
  213.7 6.9 %collective-permute-done.29 = bf16[12,128,128]{2,1,0:T(8,128)(2,1)} collective-permute-done((bf16[12,128,128]{2,1,0:T(8,128)(2,1)}, bf16[12,128,128]{2,1,0:T(8,128)(2,1)}, u32[]{:S(2)}, u32[]{:S(2)}) %collective-permute-start.29) | collective-permute-done | bytes 393248 | tf_op jit(solution)/shard_map/ppermute | solution.py:623
  224.4 10.8 %collective-permute-done.28 = bf16[20,128,128]{2,1,0:T(8,128)(2,1)} collective-permute-done((bf16[20,128,128]{2,1,0:T(8,128)(2,1)}, bf16[20,128,128]{2,1,0:T(8,128)(2,1)}, u32[]{:S(2)}, u32[]{:S(2)}) %collective-permute-start.28) | collective-permute-done | bytes 655392 | tf_op jit(solution)/shard_map/ppermute | solution.py:623
  236.5 2.9 %collective-permute-start.31 = (bf16[10,128,128]{2,1,0:T(8,128)(2,1)S(1)}, bf16[10,128,128]{2,1,0:T(8,128)(2,1)S(1)}, u32[]{:S(2)}, u32[]{:S(2)}) collective-permute-start(bf16[10,128,128]{2,1,0:T(8,128)(2,1)S(1)} %get-tuple-element.141), channel_id=1, source_target_pairs={{0,2},{1,3},{2,0},{3,1},{4,6},{5,7},{6,4},{7,5},{8,10},{9,11},{10,... | collective-permute-start | bytes 983048 | tf_op jit(solution)/shard_map/ppermute | solution.py:623
  241.0 5.3 %collective-permute-done.31 = bf16[10,128,128]{2,1,0:T(8,128)(2,1)S(1)} collective-permute-done((bf16[10,128,128]{2,1,0:T(8,128)(2,1)S(1)}, bf16[10,128,128]{2,1,0:T(8,128)(2,1)S(1)}, u32[]{:S(2)}, u32[]{:S(2)}) %collective-permute-start.31) | collective-permute-done | bytes 327712 | tf_op jit(solution)/shard_map/ppermute | solution.py:623
  256.0 4.4 %collective-permute-done.34.far = bf16[256,768]{1,0:T(8,128)(2,1)} collective-permute-done((bf16[256,768]{1,0:T(8,128)(2,1)}, bf16[256,768]{1,0:T(8,128)(2,1)}, u32[]{:S(2)}, u32[]{:S(2)}) %collective-permute-start.34) | collective-permute-done | bytes 393248 | tf_op jit(solution)/shard_map/ppermute | solution.py:872
  264.9 4.4 %adam.1 = (f32[14,128,128]{2,1,0:T(8,128)}, f32[14,128,128]{2,1,0:T(8,128)}, f32[14,128,128]{2,1,0:T(8,128)}) custom-call(bf16[6,128,128]{2,1,0:T(8,128)(2,1)S(1)} %get-tuple-element.121.refs_0_, bf16[6,128,128]{2,1,0:T(8,128)(2,1)} %collective-permute-done.35.refs_1_, bf16[5,128,128]{2,1,0:T(8,128)(2,1)S(1)} %get-tuple-element.146.refs_2_, ...), custom_call_target="tpu_custom_call" | custom-call | tf_op jit(solution)/shard_map/adam/pallas_call | solution.py:884
  (168 shorter events, 69.6 us)
Async XLA Ops:
  7.2 93.4 %all-gather.4.cloned.1.call-start = ((), (), s32[]{:S(2)}) async-start(), calls=%async_computation | async-start | bytes 3244032 | tf_op jit(solution)/shard_map/all_gather | solution.py:669
  9.2 243.8 %all-gather.6.cloned.1.call-start = ((), (), s32[]{:S(2)}) async-start(), calls=%async_computation.1 | async-start | bytes 1081344 | tf_op jit(solution)/shard_map/all_gather | solution.py:861
  9.3 29.9 %collective-permute-start.2 = (bf16[256,768]{1,0:T(8,128)(2,1)S(1)}, bf16[256,768]{1,0:T(8,128)(2,1)S(1)}, u32[]{:S(2)}, u32[]{:S(2)}) collective-permute-start(bf16[256,768]{1,0:T(8,128)(2,1)S(1)} %bitcast.11), channel_id=1, source_target_pairs={{0,2},{1,3},{4,6},{5,7},{8,10},{9,11},{12,14},{13,15},{16,18},{17,... | collective-permute-start | bytes 1179656 | tf_op jit(solution)/shard_map/ppermute | solution.py:657
  14.2 25.0 %collective-permute-start.3 = (bf16[256,768]{1,0:T(8,128)(2,1)S(1)}, bf16[256,768]{1,0:T(8,128)(2,1)S(1)}, u32[]{:S(2)}, u32[]{:S(2)}) collective-permute-start(bf16[256,768]{1,0:T(8,128)(2,1)S(1)} %bitcast.12), channel_id=1, source_target_pairs={{0,1},{1,2},{2,3},{4,5},{5,6},{6,7},{8,9},{9,10},{10,11},{12,13},{... | collective-permute-start | bytes 1179656 | tf_op jit(solution)/shard_map/ppermute | solution.py:657
  15.7 13.7 %collective-permute-start = (bf16[4,128,128]{2,1,0:T(8,128)(2,1)S(1)}, bf16[4,128,128]{2,1,0:T(8,128)(2,1)S(1)}, u32[]{:S(2)}, u32[]{:S(2)}) collective-permute-start(bf16[4,128,128]{2,1,0:T(8,128)(2,1)S(1)} %get-tuple-element.151), channel_id=1, source_target_pairs={{0,16},{1,17},{2,18},{3,19},{4,20},{5,21},{6,22},{7,23},{8,24},{9,... | collective-permute-start | bytes 393224 | tf_op jit(solution)/shard_map/ppermute | solution.py:623
  18.4 13.5 %collective-permute-start.8 = (bf16[4,128,128]{2,1,0:T(8,128)(2,1)S(1)}, bf16[4,128,128]{2,1,0:T(8,128)(2,1)S(1)}, u32[]{:S(2)}, u32[]{:S(2)}) collective-permute-start(bf16[4,128,128]{2,1,0:T(8,128)(2,1)S(1)} %get-tuple-element.150), channel_id=1, source_target_pairs={{0,16},{1,17},{2,18},{3,19},{4,20},{5,21},{6,22},{7,23},{8,24},{9,... | collective-permute-start | bytes 393224 | tf_op jit(solution)/shard_map/ppermute | solution.py:623
  30.7 14.7 %collective-permute-start.15 = (bf16[6,128,128]{2,1,0:T(8,128)(2,1)S(1)}, bf16[6,128,128]{2,1,0:T(8,128)(2,1)S(1)}, u32[]{:S(2)}, u32[]{:S(2)}) collective-permute-start(bf16[6,128,128]{2,1,0:T(8,128)(2,1)S(1)} %pad_maximum_fusion.8), channel_id=1, source_target_pairs={{0,2},{1,3},{2,0},{3,1},{4,6},{5,7},{6,4},{7,5},{8,10},{9,11},{10,... | collective-permute-start | bytes 589832 | tf_op jit(solution)/shard_map/ppermute | solution.py:623
  31.9 13.3 %collective-permute-start.9 = (bf16[8,128,128]{2,1,0:T(8,128)(2,1)S(1)}, bf16[8,128,128]{2,1,0:T(8,128)(2,1)S(1)}, u32[]{:S(2)}, u32[]{:S(2)}) collective-permute-start(bf16[8,128,128]{2,1,0:T(8,128)(2,1)S(1)} %pad_maximum_fusion.7), channel_id=1, source_target_pairs={{0,8},{1,9},{2,10},{3,11},{4,12},{5,13},{6,14},{7,15},{8,0},{9,1},... | collective-permute-start | bytes 786440 | tf_op jit(solution)/shard_map/ppermute | solution.py:623
  40.3 14.9 %collective-permute-start.4 = (bf16[16,128,128]{2,1,0:T(8,128)(2,1)S(1)}, bf16[16,128,128]{2,1,0:T(8,128)(2,1)S(1)}, u32[]{:S(2)}, u32[]{:S(2)}) collective-permute-start(bf16[16,128,128]{2,1,0:T(8,128)(2,1)S(1)} %pad_maximum_fusion.3), channel_id=1, source_target_pairs={{0,4},{1,5},{2,6},{3,7},{4,0},{5,1},{6,2},{7,3},{8,12},{9,13},{10,... | collective-permute-start | bytes 1572872 | tf_op jit(solution)/shard_map/ppermute | solution.py:623
  45.5 22.0 %collective-permute-start.16 = (bf16[12,128,128]{2,1,0:T(8,128)(2,1)S(1)}, bf16[12,128,128]{2,1,0:T(8,128)(2,1)S(1)}, u32[]{:S(2)}, u32[]{:S(2)}) collective-permute-start(bf16[12,128,128]{2,1,0:T(8,128)(2,1)S(1)} %pad_maximum_fusion.5), channel_id=1, source_target_pairs={{0,16},{1,17},{2,18},{3,19},{4,20},{5,21},{6,22},{7,23},{8,24},{9,... | collective-permute-start | bytes 1179656 | tf_op jit(solution)/shard_map/ppermute | solution.py:623
  55.4 38.1 %collective-permute-start.5 = (bf16[32,128,128]{2,1,0:T(8,128)(2,1)S(1)}, bf16[32,128,128]{2,1,0:T(8,128)(2,1)}, u32[]{:S(2)}, u32[]{:S(2)}) collective-permute-start(bf16[32,128,128]{2,1,0:T(8,128)(2,1)S(1)} %constant_dynamic-update-slice_fusion.refs_10_), channel_id=1, source_target_pairs={{0,2},{1,3},{2,0},{3,1},{4,6},{5,7},{6,4},{7,5},{8,10},{9,11},{10,... | collective-permute-start | bytes 3145736 | tf_op jit(solution)/shard_map/ppermute | solution.py:623
  57.6 36.3 %collective-permute-start.11 = (bf16[32,128,128]{2,1,0:T(8,128)(2,1)S(1)}, bf16[32,128,128]{2,1,0:T(8,128)(2,1)}, u32[]{:S(2)}, u32[]{:S(2)}) collective-permute-start(bf16[32,128,128]{2,1,0:T(8,128)(2,1)S(1)} %pad_maximum_fusion.1.refs_14_), channel_id=1, source_target_pairs={{0,4},{1,5},{2,6},{3,7},{4,0},{5,1},{6,2},{7,3},{8,12},{9,13},{10,... | collective-permute-start | bytes 3145736 | tf_op jit(solution)/shard_map/ppermute | solution.py:623
  67.5 25.9 %collective-permute-start.17 = (bf16[24,128,128]{2,1,0:T(8,128)(2,1)S(1)}, bf16[24,128,128]{2,1,0:T(8,128)(2,1)}, u32[]{:S(2)}, u32[]{:S(2)}) collective-permute-start(bf16[24,128,128]{2,1,0:T(8,128)(2,1)S(1)} %pad_maximum_fusion.2.refs_18_), channel_id=1, source_target_pairs={{0,8},{1,9},{2,10},{3,11},{4,12},{5,13},{6,14},{7,15},{8,0},{9,1},... | collective-permute-start | bytes 2359304 | tf_op jit(solution)/shard_map/ppermute | solution.py:623
  67.6 26.4 %collective-permute-start.18 = (bf16[24,128,128]{2,1,0:T(8,128)(2,1)S(1)}, bf16[24,128,128]{2,1,0:T(8,128)(2,1)S(1)}, u32[]{:S(2)}, u32[]{:S(2)}) collective-permute-start(bf16[24,128,128]{2,1,0:T(8,128)(2,1)S(1)} %pad_maximum_fusion.2.refs_18_), channel_id=1, source_target_pairs={{0,1},{1,0},{2,3},{3,2},{4,5},{5,4},{6,7},{7,6},{8,9},{9,8},{10,11... | collective-permute-start | bytes 2359304 | tf_op jit(solution)/shard_map/ppermute | solution.py:623
  67.7 29.3 %collective-permute-start.6 = (bf16[32,128,128]{2,1,0:T(8,128)(2,1)S(1)}, bf16[32,128,128]{2,1,0:T(8,128)(2,1)}, u32[]{:S(2)}, u32[]{:S(2)}) collective-permute-start(bf16[32,128,128]{2,1,0:T(8,128)(2,1)S(1)} %constant_dynamic-update-slice_fusion.refs_10_), channel_id=1, source_target_pairs={{0,1},{1,0},{2,3},{3,2},{4,5},{5,4},{6,7},{7,6},{8,9},{9,8},{10,11... | collective-permute-start | bytes 3145736 | tf_op jit(solution)/shard_map/ppermute | solution.py:623
  167.9 41.3 %collective-permute-start.24 = (bf16[48,128,128]{2,1,0:T(8,128)(2,1)}, bf16[48,128,128]{2,1,0:T(8,128)(2,1)}, u32[]{:S(2)}, u32[]{:S(2)}) collective-permute-start(bf16[48,128,128]{2,1,0:T(8,128)(2,1)} %get-tuple-element.131), channel_id=1, source_target_pairs={{0,2},{1,3},{2,0},{3,1},{4,6},{5,7},{6,4},{7,5},{8,10},{9,11},{10,... | collective-permute-start | bytes 4718600 | tf_op jit(solution)/shard_map/ppermute | solution.py:623
  174.6 31.7 %collective-permute-start.25 = (bf16[40,128,128]{2,1,0:T(8,128)(2,1)}, bf16[40,128,128]{2,1,0:T(8,128)(2,1)}, u32[]{:S(2)}, u32[]{:S(2)}) collective-permute-start(bf16[40,128,128]{2,1,0:T(8,128)(2,1)} %add_convert_fusion.3), channel_id=1, source_target_pairs={{0,4},{1,5},{2,6},{3,7},{4,0},{5,1},{6,2},{7,3},{8,12},{9,13},{10,... | collective-permute-start | bytes 3932168 | tf_op jit(solution)/shard_map/ppermute | solution.py:623
  178.1 19.9 %collective-permute-start.26 = (bf16[24,128,128]{2,1,0:T(8,128)(2,1)S(1)}, bf16[24,128,128]{2,1,0:T(8,128)(2,1)}, u32[]{:S(2)}, u32[]{:S(2)}) collective-permute-start(bf16[24,128,128]{2,1,0:T(8,128)(2,1)S(1)} %get-tuple-element.129), channel_id=1, source_target_pairs={{0,8},{1,9},{2,10},{3,11},{4,12},{5,13},{6,14},{7,15},{8,0},{9,1},... | collective-permute-start | bytes 2359304 | tf_op jit(solution)/shard_map/ppermute | solution.py:623
  200.3 20.2 %collective-permute-start.29 = (bf16[12,128,128]{2,1,0:T(8,128)(2,1)}, bf16[12,128,128]{2,1,0:T(8,128)(2,1)}, u32[]{:S(2)}, u32[]{:S(2)}) collective-permute-start(bf16[12,128,128]{2,1,0:T(8,128)(2,1)} %get-tuple-element.139), channel_id=1, source_target_pairs={{0,16},{1,17},{2,18},{3,19},{4,20},{5,21},{6,22},{7,23},{8,24},{9,... | collective-permute-start | bytes 1179656 | tf_op jit(solution)/shard_map/ppermute | solution.py:623
  208.9 26.4 %collective-permute-start.28 = (bf16[20,128,128]{2,1,0:T(8,128)(2,1)}, bf16[20,128,128]{2,1,0:T(8,128)(2,1)}, u32[]{:S(2)}, u32[]{:S(2)}) collective-permute-start(bf16[20,128,128]{2,1,0:T(8,128)(2,1)} %get-tuple-element.135), channel_id=1, source_target_pairs={{0,8},{1,9},{2,10},{3,11},{4,12},{5,13},{6,14},{7,15},{8,0},{9,1},... | collective-permute-start | bytes 1966088 | tf_op jit(solution)/shard_map/ppermute | solution.py:623
  211.9 27.4 %collective-permute-start.27 = (bf16[24,128,128]{2,1,0:T(8,128)(2,1)}, bf16[24,128,128]{2,1,0:T(8,128)(2,1)S(1)}, u32[]{:S(2)}, u32[]{:S(2)}) collective-permute-start(bf16[24,128,128]{2,1,0:T(8,128)(2,1)} %get-tuple-element.132), channel_id=1, source_target_pairs={{0,4},{1,5},{2,6},{3,7},{4,0},{5,1},{6,2},{7,3},{8,12},{9,13},{10,... | collective-permute-start | bytes 2359304 | tf_op jit(solution)/shard_map/ppermute | solution.py:623
  221.8 17.9 %collective-permute-start.32 = (bf16[6,128,128]{2,1,0:T(8,128)(2,1)S(1)}, bf16[6,128,128]{2,1,0:T(8,128)(2,1)S(1)}, u32[]{:S(2)}, u32[]{:S(2)}) collective-permute-start(bf16[6,128,128]{2,1,0:T(8,128)(2,1)S(1)} %get-tuple-element.145), channel_id=1, source_target_pairs={{0,2},{1,3},{2,0},{3,1},{4,6},{5,7},{6,4},{7,5},{8,10},{9,11},{10,... | collective-permute-start | bytes 589832 | tf_op jit(solution)/shard_map/ppermute | solution.py:623
  240.5 23.8 %collective-permute-start.37 = (bf16[3,128,128]{2,1,0:T(8,128)(2,1)}, bf16[3,128,128]{2,1,0:T(8,128)(2,1)}, u32[]{:S(2)}, u32[]{:S(2)}) collective-permute-start(bf16[3,128,128]{2,1,0:T(8,128)(2,1)} %get-tuple-element.153), channel_id=1, source_target_pairs={{0,4},{1,5},{2,6},{3,7},{4,0},{5,1},{6,2},{7,3},{8,12},{9,13},{10,... | collective-permute-start | bytes 294920 | tf_op jit(solution)/shard_map/ppermute | solution.py:623
  247.1 17.2 %collective-permute-start.36 = (bf16[5,128,128]{2,1,0:T(8,128)(2,1)}, bf16[5,128,128]{2,1,0:T(8,128)(2,1)}, u32[]{:S(2)}, u32[]{:S(2)}) collective-permute-start(bf16[5,128,128]{2,1,0:T(8,128)(2,1)} %get-tuple-element.147), channel_id=1, source_target_pairs={{0,16},{1,17},{2,18},{3,19},{4,20},{5,21},{6,22},{7,23},{8,24},{9,... | collective-permute-start | bytes 491528 | tf_op jit(solution)/shard_map/ppermute | solution.py:623
  (47 other events, 449.4 us)
Sparse Core Ops, SparseCore 0:
  11.5 76.9 all-gather.3
  183.6 63.8 all-gather.5

commit v5 on v4

--- a/solution.py
+++ b/solution.py
@@ -867,7 +867,7 @@
             middle = left[which].shape[0] // 2
             piece = plus(left[which][middle:], came[which][middle:])
             rest = plus(left[which][:middle], came[which][:middle])
-            if which == 1 and step == steps - 1:
+            if which == 0 and step == 1:
                 far, near = after(far, piece), after(near, piece)
                 far = lax.ppermute(far, "seq", [(i, i - 2) for i in range(2, n_seq)])
                 near = lax.ppermute(near, "seq", [(i, i - 1) for i in range(1, n_seq)])
@@ -876,7 +876,7 @@
                 rest, gathered = lax.optimization_barrier((rest, gathered))
             came[which] = swap(piece, order[step])
             left[which] = rest
-            last = piece
+            last = (piece, far, near) if which == len(plan) - 2 and step == 2 else piece
     pairs = list(zip(left, came))
     totals = jnp.sum(gathered[:, : 3 * dt], axis=0).reshape(3, width)
     correction = 1.0 - first_decay**STEP

time: 280 us -> 278 us (level); the launches traced: 276 us -> 277 us
  waiting for transfers between devices: 118 us -> 113 us
  local copies, waits for them, and re-layouts: 6.68 us -> 10.2 us
    ppermute x1, waiting for transfers between devices: 4.37 us -> 0.01 us  [local(): far = lax.ppermute(far, 'seq', [(i, i - 2) for i in range(2, n_seq)])]
    unnamed x63 -> x73, local copies, waits for them, and re-layouts: 3.64 us -> 7.14 us
  transfers between devices with their start and end apart: 40 -> 40, of which waited for: 20 -> 19; matrix products, arithmetic and copies ran while one was open for 12% -> 12% of each run, Pallas kernels for 5% -> 4%
where the time goes in v5:
time: 278 us; the launch traced here: 277 us
  waiting for transfers between devices  113 us (41%)
  Pallas kernels  62.4 us (22%)
  starting transfers between devices  43.1 us (16%)
  other arithmetic  33 us (12%)
  between operations  16 us (6%)
  local copies, waits for them, and re-layouts  10.2 us (4%)
    ppermute x32, waiting for transfers between devices, swap(): return lax.ppermute(x, axes, [(i, i ^ bit) for i in range(devices)])  112 us
    pallas_call x1, Pallas kernels, local(): pl.pallas_call(functools.partial(layer_kernel, tiles, sizes), out_shape=(...  41.3 us
    ppermute x32, starting transfers between devices, swap(): return lax.ppermute(x, axes, [(i, i ^ bit) for i in range(devices)])  31 us
    convert_element_type x13, other arithmetic, plus(): return (a.astype(F32) + b.astype(F32)).astype(BF)  27.2 us
    unnamed x73, local copies, waits for them, and re-layouts  7.14 us
    pallas_call x1, Pallas kernels, local(): pl.pallas_call(qkv_kernel, out_shape=sums_shapes, in_specs=[sm] + [hbm] *...  6.39 us
    ppermute x2, starting transfers between devices, local(): lax.ppermute(mine_tok, 'seq', [(i, i + step) for i in range(n_seq - step)])  6.38 us
  transfers between devices with their start and end apart: 40, of which 19 were waited for; matrix products, arithmetic and copies ran while one was open for 12% of the time, Pallas kernels for 4%

profile of v5, /device:TPU:0, one launch (start us, length us, event | category | flops | bytes accessed | tf_op | source)
XLA Modules:
  0.0 277.2 jit_solution(9508357386318530469)
XLA Ops:
  9.3 4.9 %collective-permute-start.2 = (bf16[256,768]{1,0:T(8,128)(2,1)S(1)}, bf16[256,768]{1,0:T(8,128)(2,1)S(1)}, u32[]{:S(2)}, u32[]{:S(2)}) collective-permute-start(bf16[256,768]{1,0:T(8,128)(2,1)S(1)} %bitcast.11), channel_id=1, source_target_pairs={{0,2},{1,3},{4,6},{5,7},{8,10},{9,11},{12,14},{13,15},{16,18},{17,... | collective-permute-start | bytes 1179656 | tf_op jit(solution)/shard_map/ppermute | solution.py:657
  21.7 7.6 %collective-permute-done = bf16[4,128,128]{2,1,0:T(8,128)(2,1)S(1)} collective-permute-done((bf16[4,128,128]{2,1,0:T(8,128)(2,1)S(1)}, bf16[4,128,128]{2,1,0:T(8,128)(2,1)S(1)}, u32[]{:S(2)}, u32[]{:S(2)}) %collective-permute-start) | collective-permute-done | bytes 131104 | tf_op jit(solution)/shard_map/ppermute | solution.py:623
  32.9 6.2 %collective-permute-done.1 = bf16[8,128,128]{2,1,0:T(8,128)(2,1)S(1)} collective-permute-done((bf16[8,128,128]{2,1,0:T(8,128)(2,1)S(1)}, bf16[8,128,128]{2,1,0:T(8,128)(2,1)S(1)}, u32[]{:S(2)}, u32[]{:S(2)}) %collective-permute-start.1) | collective-permute-done | bytes 262176 | tf_op jit(solution)/shard_map/ppermute | solution.py:623
  41.8 3.5 %collective-permute-done.9 = bf16[8,128,128]{2,1,0:T(8,128)(2,1)S(1)} collective-permute-done((bf16[8,128,128]{2,1,0:T(8,128)(2,1)S(1)}, bf16[8,128,128]{2,1,0:T(8,128)(2,1)S(1)}, u32[]{:S(2)}, u32[]{:S(2)}) %collective-permute-start.9) | collective-permute-done | bytes 262176 | tf_op jit(solution)/shard_map/ppermute | solution.py:623
  47.2 8.0 %collective-permute-done.4 = bf16[16,128,128]{2,1,0:T(8,128)(2,1)S(1)} collective-permute-done((bf16[16,128,128]{2,1,0:T(8,128)(2,1)S(1)}, bf16[16,128,128]{2,1,0:T(8,128)(2,1)S(1)}, u32[]{:S(2)}, u32[]{:S(2)}) %collective-permute-start.4) | collective-permute-done | bytes 524320 | tf_op jit(solution)/shard_map/ppermute | solution.py:623
  58.9 8.6 %collective-permute-done.16 = bf16[12,128,128]{2,1,0:T(8,128)(2,1)S(1)} collective-permute-done((bf16[12,128,128]{2,1,0:T(8,128)(2,1)S(1)}, bf16[12,128,128]{2,1,0:T(8,128)(2,1)S(1)}, u32[]{:S(2)}, u32[]{:S(2)}) %collective-permute-start.16) | collective-permute-done | bytes 393248 | tf_op jit(solution)/shard_map/ppermute | solution.py:623
  68.2 25.2 %collective-permute-done.17.refs_19_ = bf16[24,128,128]{2,1,0:T(8,128)(2,1)} collective-permute-done((bf16[24,128,128]{2,1,0:T(8,128)(2,1)S(1)}, bf16[24,128,128]{2,1,0:T(8,128)(2,1)}, u32[]{:S(2)}, u32[]{:S(2)}) %collective-permute-start.17) | collective-permute-done | bytes 786464 | tf_op jit(solution)/shard_map/ppermute | solution.py:623
  97.7 2.9 %collective-permute-done.19.refs_21_ = bf16[24,128,128]{2,1,0:T(8,128)(2,1)} collective-permute-done((bf16[24,128,128]{2,1,0:T(8,128)(2,1)}, bf16[24,128,128]{2,1,0:T(8,128)(2,1)}, u32[]{:S(2)}, u32[]{:S(2)}) %collective-permute-start.19) | collective-permute-done | bytes 786464 | tf_op jit(solution)/shard_map/ppermute | solution.py:623
  100.6 41.3 %layer.1 = (bf16[256,768]{1,0:T(8,128)(2,1)}, f32[256,768]{1,0:T(8,128)}, bf16[256,768]{1,0:T(8,128)(2,1)}, bf16[768,768]{1,0:T(8,128)(2,1)}, bf16[768,768]{1,0:...) custom-call(s32[448]{0:T(512)} %get-tuple-element.67.refs_0_, ...), custom_call_target="tpu_custom_call" | custom-call | tf_op jit(solution)/shard_map/layer/pallas_call | solution.py:689
  144.7 6.4 %qkv_grad.1 = (bf16[224,128,128]{2,1,0:T(8,128)(2,1)}, bf16[96,128,128]{2,1,0:T(8,128)(2,1)}, bf16[128,128,128]{2,1,0:T(8,128)(2,1)}) custom-call(s32[448]{0:T(512)} %get-tuple-element.68.refs_1_.dst, bf16[256,768]{1,0:T(8,128)(2,1)} %get-tuple-element.82.gq_h, ...), custom_call_target="tpu_custom_call", output_to_operand_aliasing={{0}: (5, {}), {1}: (6, {}), {2}: (7, {})} | custom-call | flops 2113929216 | bytes 8388608 | tf_op jit(solution)/shard_map/qkv_grad/pallas_call | solution.py:771
  151.8 4.8 %head_grad.1 = (bf16[256,128]{1,0:T(8,128)(2,1)}, bf16[768,128]{1,0:T(8,128)(2,1)}, bf16[224,128,128]{2,1,0:T(8,128)(2,1)}, bf16[96,128,128]{2,1,0:T(8,128)(2,1)}, bf16[128,128,128]{2,1,0:T(8,128)(2,1)}) custom-call(s32[448]{0:T(512)} %get-tuple-element.68.refs_1_.dst, ...), custom_call_target="tpu_custom_call", output_to_operand_aliasing={{2}: (10, {}), {3}: (11, {}), {4}: (12, {})} | custom-call | flops 1073741824 | bytes 4194304 | tf_op jit(solution)/shard_map/head_grad/pallas_call | solution.py:792
  157.7 5.5 %collective-permute-done.22 = bf16[96,128,128]{2,1,0:T(8,128)(2,1)S(1)} collective-permute-done((bf16[96,128,128]{2,1,0:T(8,128)(2,1)}, bf16[96,128,128]{2,1,0:T(8,128)(2,1)S(1)}, u32[]{:S(2)}, u32[]{:S(2)}) %collective-permute-start.22) | collective-permute-done | bytes 3145760 | tf_op jit(solution)/shard_map/ppermute | solution.py:623
  163.6 4.2 %add_convert_fusion = (bf16[48,128,128]{2,1,0:T(8,128)(2,1)S(1)}, bf16[48,128,128]{2,1,0:T(8,128)(2,1)}) fusion(bf16[96,128,128]{2,1,0:T(8,128)(2,1)S(1)} %collective-permute-done.22, bf16[224,128,128]{2,1,0:T(8,128)(2,1)} %get-tuple-element.93), kind=kLoop, calls=%fused_computation | loop fusion | flops 6291456 | bytes 9437184 | tf_op jit(solution)/shard_map/convert_element_type | solution.py:816
  170.6 4.0 %add_convert_fusion.3 = bf16[40,128,128]{2,1,0:T(8,128)(2,1)} fusion(bf16[128,128,128]{2,1,0:T(8,128)(2,1)S(1)} %collective-permute-done.23, bf16[224,128,128]{2,1,0:T(8,128)(2,1)} %get-tuple-element.93), kind=kLoop, calls=%fused_computation.3 | loop fusion | flops 2621440 | bytes 3932160 | tf_op jit(solution)/shard_map/convert_element_type | solution.py:816
  176.2 2.7 add_convert_fusion.6
  179.6 4.0 %pre_grad.1 = (bf16[256,768]{1,0:T(8,128)(2,1)S(1)}, bf16[256,768]{1,0:T(8,128)(2,1)S(1)}, f32[256,768]{1,0:T(8,128)S(1)}, f32[64,128]{1,0:T(8,128)}) custom-call(s32[1]{0:T(128)} %bitcast.6.row_at, bf16[768,768]{1,0:T(8,128)(2,1)S(1)} %copy-done.1, f32[8,768]{1,0:T(8,128)S(1)} %copy-done.21, bf16[256,128]{1,0:T(8,128)(2,1)S(1)} %copy-done.20, ...), custom_call_target="tpu_custom_call" | custom-call | flops 2113929216 | bytes 10485760 | tf_op jit(solution)/shard_map/pre_grad/pallas_call | solution.py:838
  186.6 12.3 %collective-permute-done.26 = bf16[24,128,128]{2,1,0:T(8,128)(2,1)} collective-permute-done((bf16[24,128,128]{2,1,0:T(8,128)(2,1)}, bf16[24,128,128]{2,1,0:T(8,128)(2,1)}, u32[]{:S(2)}, u32[]{:S(2)}) %collective-permute-start.26) | collective-permute-done | bytes 786464 | tf_op jit(solution)/shard_map/ppermute | solution.py:623
  206.3 2.8 %add_convert_fusion.8 = (bf16[20,128,128]{2,1,0:T(8,128)(2,1)}, bf16[20,128,128]{2,1,0:T(8,128)(2,1)}) fusion(bf16[40,128,128]{2,1,0:T(8,128)(2,1)S(1)} %add_convert_fusion.2, bf16[40,128,128]{2,1,0:T(8,128)(2,1)} %collective-permute-done.25), kind=kLoop, calls=%fused_computation.8 | loop fusion | flops 2621440 | bytes 3932160 | tf_op jit(solution)/shard_map/convert_element_type | solution.py:816
  209.5 2.7 add_convert_fusion.4
  216.8 4.7 %collective-permute-done.29 = bf16[12,128,128]{2,1,0:T(8,128)(2,1)} collective-permute-done((bf16[12,128,128]{2,1,0:T(8,128)(2,1)}, bf16[12,128,128]{2,1,0:T(8,128)(2,1)}, u32[]{:S(2)}, u32[]{:S(2)}) %collective-permute-start.29) | collective-permute-done | bytes 393248 | tf_op jit(solution)/shard_map/ppermute | solution.py:623
  222.9 2.7 collective-permute-start.34
  225.6 9.8 %collective-permute-done.28 = bf16[20,128,128]{2,1,0:T(8,128)(2,1)} collective-permute-done((bf16[20,128,128]{2,1,0:T(8,128)(2,1)}, bf16[20,128,128]{2,1,0:T(8,128)(2,1)}, u32[]{:S(2)}, u32[]{:S(2)}) %collective-permute-start.28) | collective-permute-done | bytes 655392 | tf_op jit(solution)/shard_map/ppermute | solution.py:623
  248.6 7.5 %collective-permute-done.32 = bf16[12,128,128]{2,1,0:T(8,128)(2,1)S(1)} collective-permute-done((bf16[12,128,128]{2,1,0:T(8,128)(2,1)S(1)}, bf16[12,128,128]{2,1,0:T(8,128)(2,1)S(1)}, u32[]{:S(2)}, u32[]{:S(2)}) %collective-permute-start.32) | collective-permute-done | bytes 393248 | tf_op jit(solution)/shard_map/ppermute | solution.py:623
  265.9 4.4 %adam.1 = (f32[14,128,128]{2,1,0:T(8,128)}, f32[14,128,128]{2,1,0:T(8,128)}, f32[14,128,128]{2,1,0:T(8,128)}) custom-call(bf16[6,128,128]{2,1,0:T(8,128)(2,1)S(1)} %get-tuple-element.121.refs_0_, bf16[6,128,128]{2,1,0:T(8,128)(2,1)} %collective-permute-done.35.refs_1_, bf16[5,128,128]{2,1,0:T(8,128)(2,1)S(1)} %get-tuple-element.146.refs_2_, ...), custom_call_target="tpu_custom_call" | custom-call | tf_op jit(solution)/shard_map/adam/pallas_call | solution.py:884
  (178 shorter events, 74.3 us)
Async XLA Ops:
  7.2 93.4 %all-gather.4.cloned.1.call-start = ((), (), s32[]{:S(2)}) async-start(), calls=%async_computation | async-start | bytes 3244032 | tf_op jit(solution)/shard_map/all_gather | solution.py:669
  9.2 247.6 %all-gather.6.cloned.1.call-start = ((), (), s32[]{:S(2)}) async-start(), calls=%async_computation.1 | async-start | bytes 1081344 | tf_op jit(solution)/shard_map/all_gather | solution.py:861
  9.3 29.9 %collective-permute-start.2 = (bf16[256,768]{1,0:T(8,128)(2,1)S(1)}, bf16[256,768]{1,0:T(8,128)(2,1)S(1)}, u32[]{:S(2)}, u32[]{:S(2)}) collective-permute-start(bf16[256,768]{1,0:T(8,128)(2,1)S(1)} %bitcast.11), channel_id=1, source_target_pairs={{0,2},{1,3},{4,6},{5,7},{8,10},{9,11},{12,14},{13,15},{16,18},{17,... | collective-permute-start | bytes 1179656 | tf_op jit(solution)/shard_map/ppermute | solution.py:657
  14.2 25.0 %collective-permute-start.3 = (bf16[256,768]{1,0:T(8,128)(2,1)S(1)}, bf16[256,768]{1,0:T(8,128)(2,1)S(1)}, u32[]{:S(2)}, u32[]{:S(2)}) collective-permute-start(bf16[256,768]{1,0:T(8,128)(2,1)S(1)} %bitcast.12), channel_id=1, source_target_pairs={{0,1},{1,2},{2,3},{4,5},{5,6},{6,7},{8,9},{9,10},{10,11},{12,13},{... | collective-permute-start | bytes 1179656 | tf_op jit(solution)/shard_map/ppermute | solution.py:657
  30.7 14.7 %collective-permute-start.15 = (bf16[6,128,128]{2,1,0:T(8,128)(2,1)S(1)}, bf16[6,128,128]{2,1,0:T(8,128)(2,1)S(1)}, u32[]{:S(2)}, u32[]{:S(2)}) collective-permute-start(bf16[6,128,128]{2,1,0:T(8,128)(2,1)S(1)} %pad_maximum_fusion.8), channel_id=1, source_target_pairs={{0,2},{1,3},{2,0},{3,1},{4,6},{5,7},{6,4},{7,5},{8,10},{9,11},{10,... | collective-permute-start | bytes 589832 | tf_op jit(solution)/shard_map/ppermute | solution.py:623
  40.3 14.9 %collective-permute-start.4 = (bf16[16,128,128]{2,1,0:T(8,128)(2,1)S(1)}, bf16[16,128,128]{2,1,0:T(8,128)(2,1)S(1)}, u32[]{:S(2)}, u32[]{:S(2)}) collective-permute-start(bf16[16,128,128]{2,1,0:T(8,128)(2,1)S(1)} %pad_maximum_fusion.3), channel_id=1, source_target_pairs={{0,4},{1,5},{2,6},{3,7},{4,0},{5,1},{6,2},{7,3},{8,12},{9,13},{10,... | collective-permute-start | bytes 1572872 | tf_op jit(solution)/shard_map/ppermute | solution.py:623
  45.5 22.0 %collective-permute-start.16 = (bf16[12,128,128]{2,1,0:T(8,128)(2,1)S(1)}, bf16[12,128,128]{2,1,0:T(8,128)(2,1)S(1)}, u32[]{:S(2)}, u32[]{:S(2)}) collective-permute-start(bf16[12,128,128]{2,1,0:T(8,128)(2,1)S(1)} %pad_maximum_fusion.5), channel_id=1, source_target_pairs={{0,16},{1,17},{2,18},{3,19},{4,20},{5,21},{6,22},{7,23},{8,24},{9,... | collective-permute-start | bytes 1179656 | tf_op jit(solution)/shard_map/ppermute | solution.py:623
  55.4 38.1 %collective-permute-start.5 = (bf16[32,128,128]{2,1,0:T(8,128)(2,1)S(1)}, bf16[32,128,128]{2,1,0:T(8,128)(2,1)}, u32[]{:S(2)}, u32[]{:S(2)}) collective-permute-start(bf16[32,128,128]{2,1,0:T(8,128)(2,1)S(1)} %constant_dynamic-update-slice_fusion.refs_10_), channel_id=1, source_target_pairs={{0,2},{1,3},{2,0},{3,1},{4,6},{5,7},{6,4},{7,5},{8,10},{9,11},{10,... | collective-permute-start | bytes 3145736 | tf_op jit(solution)/shard_map/ppermute | solution.py:623
  57.6 36.3 %collective-permute-start.11 = (bf16[32,128,128]{2,1,0:T(8,128)(2,1)S(1)}, bf16[32,128,128]{2,1,0:T(8,128)(2,1)}, u32[]{:S(2)}, u32[]{:S(2)}) collective-permute-start(bf16[32,128,128]{2,1,0:T(8,128)(2,1)S(1)} %pad_maximum_fusion.1.refs_14_), channel_id=1, source_target_pairs={{0,4},{1,5},{2,6},{3,7},{4,0},{5,1},{6,2},{7,3},{8,12},{9,13},{10,... | collective-permute-start | bytes 3145736 | tf_op jit(solution)/shard_map/ppermute | solution.py:623
  67.5 25.9 %collective-permute-start.17 = (bf16[24,128,128]{2,1,0:T(8,128)(2,1)S(1)}, bf16[24,128,128]{2,1,0:T(8,128)(2,1)}, u32[]{:S(2)}, u32[]{:S(2)}) collective-permute-start(bf16[24,128,128]{2,1,0:T(8,128)(2,1)S(1)} %pad_maximum_fusion.2.refs_18_), channel_id=1, source_target_pairs={{0,8},{1,9},{2,10},{3,11},{4,12},{5,13},{6,14},{7,15},{8,0},{9,1},... | collective-permute-start | bytes 2359304 | tf_op jit(solution)/shard_map/ppermute | solution.py:623
  67.7 26.3 %collective-permute-start.18 = (bf16[24,128,128]{2,1,0:T(8,128)(2,1)S(1)}, bf16[24,128,128]{2,1,0:T(8,128)(2,1)S(1)}, u32[]{:S(2)}, u32[]{:S(2)}) collective-permute-start(bf16[24,128,128]{2,1,0:T(8,128)(2,1)S(1)} %pad_maximum_fusion.2.refs_18_), channel_id=1, source_target_pairs={{0,1},{1,0},{2,3},{3,2},{4,5},{5,4},{6,7},{7,6},{8,9},{9,8},{10,11... | collective-permute-start | bytes 2359304 | tf_op jit(solution)/shard_map/ppermute | solution.py:623
  67.7 29.2 %collective-permute-start.6 = (bf16[32,128,128]{2,1,0:T(8,128)(2,1)S(1)}, bf16[32,128,128]{2,1,0:T(8,128)(2,1)}, u32[]{:S(2)}, u32[]{:S(2)}) collective-permute-start(bf16[32,128,128]{2,1,0:T(8,128)(2,1)S(1)} %constant_dynamic-update-slice_fusion.refs_10_), channel_id=1, source_target_pairs={{0,1},{1,0},{2,3},{3,2},{4,5},{5,4},{6,7},{7,6},{8,9},{9,8},{10,11... | collective-permute-start | bytes 3145736 | tf_op jit(solution)/shard_map/ppermute | solution.py:623
  167.8 41.7 %collective-permute-start.24 = (bf16[48,128,128]{2,1,0:T(8,128)(2,1)}, bf16[48,128,128]{2,1,0:T(8,128)(2,1)}, u32[]{:S(2)}, u32[]{:S(2)}) collective-permute-start(bf16[48,128,128]{2,1,0:T(8,128)(2,1)} %get-tuple-element.131), channel_id=1, source_target_pairs={{0,2},{1,3},{2,0},{3,1},{4,6},{5,7},{6,4},{7,5},{8,10},{9,11},{10,... | collective-permute-start | bytes 4718600 | tf_op jit(solution)/shard_map/ppermute | solution.py:623
  174.7 31.7 %collective-permute-start.25 = (bf16[40,128,128]{2,1,0:T(8,128)(2,1)}, bf16[40,128,128]{2,1,0:T(8,128)(2,1)}, u32[]{:S(2)}, u32[]{:S(2)}) collective-permute-start(bf16[40,128,128]{2,1,0:T(8,128)(2,1)} %add_convert_fusion.3), channel_id=1, source_target_pairs={{0,4},{1,5},{2,6},{3,7},{4,0},{5,1},{6,2},{7,3},{8,12},{9,13},{10,... | collective-permute-start | bytes 3932168 | tf_op jit(solution)/shard_map/ppermute | solution.py:623
  178.9 20.1 %collective-permute-start.26 = (bf16[24,128,128]{2,1,0:T(8,128)(2,1)}, bf16[24,128,128]{2,1,0:T(8,128)(2,1)}, u32[]{:S(2)}, u32[]{:S(2)}) collective-permute-start(bf16[24,128,128]{2,1,0:T(8,128)(2,1)} %get-tuple-element.129), channel_id=1, source_target_pairs={{0,8},{1,9},{2,10},{3,11},{4,12},{5,13},{6,14},{7,15},{8,0},{9,1},... | collective-permute-start | bytes 2359304 | tf_op jit(solution)/shard_map/ppermute | solution.py:623
  201.3 20.3 %collective-permute-start.29 = (bf16[12,128,128]{2,1,0:T(8,128)(2,1)}, bf16[12,128,128]{2,1,0:T(8,128)(2,1)}, u32[]{:S(2)}, u32[]{:S(2)}) collective-permute-start(bf16[12,128,128]{2,1,0:T(8,128)(2,1)} %get-tuple-element.139), channel_id=1, source_target_pairs={{0,16},{1,17},{2,18},{3,19},{4,20},{5,21},{6,22},{7,23},{8,24},{9,... | collective-permute-start | bytes 1179656 | tf_op jit(solution)/shard_map/ppermute | solution.py:623
  209.1 26.3 %collective-permute-start.28 = (bf16[20,128,128]{2,1,0:T(8,128)(2,1)}, bf16[20,128,128]{2,1,0:T(8,128)(2,1)}, u32[]{:S(2)}, u32[]{:S(2)}) collective-permute-start(bf16[20,128,128]{2,1,0:T(8,128)(2,1)} %get-tuple-element.135), channel_id=1, source_target_pairs={{0,8},{1,9},{2,10},{3,11},{4,12},{5,13},{6,14},{7,15},{8,0},{9,1},... | collective-permute-start | bytes 1966088 | tf_op jit(solution)/shard_map/ppermute | solution.py:623
  212.2 28.5 %collective-permute-start.27 = (bf16[24,128,128]{2,1,0:T(8,128)(2,1)}, bf16[24,128,128]{2,1,0:T(8,128)(2,1)}, u32[]{:S(2)}, u32[]{:S(2)}) collective-permute-start(bf16[24,128,128]{2,1,0:T(8,128)(2,1)} %get-tuple-element.132), channel_id=1, source_target_pairs={{0,4},{1,5},{2,6},{3,7},{4,0},{5,1},{6,2},{7,3},{8,12},{9,13},{10,... | collective-permute-start | bytes 2359304 | tf_op jit(solution)/shard_map/ppermute | solution.py:623
  214.0 25.3 %collective-permute-start.31 = (bf16[256,768]{1,0:T(8,128)(2,1)S(1)}, bf16[256,768]{1,0:T(8,128)(2,1)S(1)}, u32[]{:S(2)}, u32[]{:S(2)}) collective-permute-start(bf16[256,768]{1,0:T(8,128)(2,1)S(1)} %get-tuple-element.112), channel_id=1, source_target_pairs={{1,0},{2,1},{3,2},{5,4},{6,5},{7,6},{9,8},{10,9},{11,10},{13,12},{... | collective-permute-start | bytes 1179656 | tf_op jit(solution)/shard_map/ppermute | solution.py:873
  215.3 24.7 %collective-permute-start.30 = (bf16[256,768]{1,0:T(8,128)(2,1)S(1)}, bf16[256,768]{1,0:T(8,128)(2,1)S(1)}, u32[]{:S(2)}, u32[]{:S(2)}) collective-permute-start(bf16[256,768]{1,0:T(8,128)(2,1)S(1)} %get-tuple-element.110), channel_id=1, source_target_pairs={{2,0},{3,1},{6,4},{7,5},{10,8},{11,9},{14,12},{15,13},{18,16},{19,... | collective-permute-start | bytes 1179656 | tf_op jit(solution)/shard_map/ppermute | solution.py:872
  222.9 19.3 %collective-permute-start.34 = (bf16[6,128,128]{2,1,0:T(8,128)(2,1)S(1)}, bf16[6,128,128]{2,1,0:T(8,128)(2,1)S(1)}, u32[]{:S(2)}, u32[]{:S(2)}) collective-permute-start(bf16[6,128,128]{2,1,0:T(8,128)(2,1)S(1)} %get-tuple-element.145), channel_id=1, source_target_pairs={{0,2},{1,3},{2,0},{3,1},{4,6},{5,7},{6,4},{7,5},{8,10},{9,11},{10,... | collective-permute-start | bytes 589832 | tf_op jit(solution)/shard_map/ppermute | solution.py:623
  242.1 14.0 %collective-permute-start.32 = (bf16[12,128,128]{2,1,0:T(8,128)(2,1)S(1)}, bf16[12,128,128]{2,1,0:T(8,128)(2,1)S(1)}, u32[]{:S(2)}, u32[]{:S(2)}) collective-permute-start(bf16[12,128,128]{2,1,0:T(8,128)(2,1)S(1)} %get-tuple-element.136), channel_id=1, source_target_pairs={{0,8},{1,9},{2,10},{3,11},{4,12},{5,13},{6,14},{7,15},{8,0},{9,1},... | collective-permute-start | bytes 1179656 | tf_op jit(solution)/shard_map/ppermute | solution.py:623
  242.9 20.9 %collective-permute-start.37 = (bf16[3,128,128]{2,1,0:T(8,128)(2,1)}, bf16[3,128,128]{2,1,0:T(8,128)(2,1)}, u32[]{:S(2)}, u32[]{:S(2)}) collective-permute-start(bf16[3,128,128]{2,1,0:T(8,128)(2,1)} %get-tuple-element.153), channel_id=1, source_target_pairs={{0,4},{1,5},{2,6},{3,7},{4,0},{5,1},{6,2},{7,3},{8,12},{9,13},{10,... | collective-permute-start | bytes 294920 | tf_op jit(solution)/shard_map/ppermute | solution.py:623
  246.6 17.2 %collective-permute-start.36 = (bf16[5,128,128]{2,1,0:T(8,128)(2,1)}, bf16[5,128,128]{2,1,0:T(8,128)(2,1)}, u32[]{:S(2)}, u32[]{:S(2)}) collective-permute-start(bf16[5,128,128]{2,1,0:T(8,128)(2,1)} %get-tuple-element.147), channel_id=1, source_target_pairs={{0,16},{1,17},{2,18},{3,19},{4,20},{5,21},{6,22},{7,23},{8,24},{9,... | collective-permute-start | bytes 491528 | tf_op jit(solution)/shard_map/ppermute | solution.py:623
  (52 other events, 477.8 us)
Sparse Core Ops, SparseCore 0:
  11.5 76.9 all-gather.3
  184.6 64.2 all-gather.5

commit v6 on v5

--- a/solution.py
+++ b/solution.py
@@ -159,9 +159,13 @@
                 ]
 
     write(wqkv, wqkv_h)
-    for i in range(dt):
+
+    @pl.loop(0, dt)
+    def _(i):
+        rows = pl.ds(pl.multiple_of(i * side, side), side)
         for j in range(dt):
-            wout[i * side : (i + 1) * side, j * side : (j + 1) * side] = wall[src[n_qkv + i * dt + j]]
+            wout[rows, j * side : (j + 1) * side] = wall[src[n_qkv + i * dt + j]]
+
 
     @pl.loop(0, dt // 2, unroll=True)
     def _(j):
@@ -345,7 +349,7 @@
 
     gsh[...] = jnp.zeros_like(gsh)
 
-    @pl.loop(0, pairs)
+    @pl.loop(0, pairs, unroll=2)
     def _(p):
         g2 = g_s[p]
         q2 = q_s[p]

time: 278 us -> 277 us (level)
  no operation moved by 1% of the time
where the time goes in v6:
time: 277 us; the launch traced here: 276 us
  waiting for transfers between devices  112 us (40%)
  Pallas kernels  62 us (22%)
  starting transfers between devices  43.2 us (16%)
  other arithmetic  33 us (12%)
  between operations  16 us (6%)
  local copies, waits for them, and re-layouts  10.2 us (4%)
    ppermute x32, waiting for transfers between devices, swap(): return lax.ppermute(x, axes, [(i, i ^ bit) for i in range(devices)])  112 us
    pallas_call x1, Pallas kernels, local(): pl.pallas_call(functools.partial(layer_kernel, tiles, sizes), out_shape=(...  40.9 us
    ppermute x32, starting transfers between devices, swap(): return lax.ppermute(x, axes, [(i, i ^ bit) for i in range(devices)])  31.3 us
    convert_element_type x13, other arithmetic, plus(): return (a.astype(F32) + b.astype(F32)).astype(BF)  27.2 us
    unnamed x73, local copies, waits for them, and re-layouts  7.14 us
    ppermute x2, starting transfers between devices, local(): lax.ppermute(mine_tok, 'seq', [(i, i + step) for i in range(n_seq - step)])  6.38 us
    pallas_call x1, Pallas kernels, local(): pl.pallas_call(qkv_kernel, out_shape=sums_shapes, in_specs=[sm] + [hbm] *...  6.35 us
  transfers between devices with their start and end apart: 40, of which 19 were waited for; matrix products, arithmetic and copies ran while one was open for 12% of the time, Pallas kernels for 4%

profile of v6, /device:TPU:0, one launch (start us, length us, event | category | flops | bytes accessed | tf_op | source)
XLA Modules:
  0.0 276.2 jit_solution(13890228335523594290)
XLA Ops:
  9.3 4.9 %collective-permute-start.2 = (bf16[256,768]{1,0:T(8,128)(2,1)S(1)}, bf16[256,768]{1,0:T(8,128)(2,1)S(1)}, u32[]{:S(2)}, u32[]{:S(2)}) collective-permute-start(bf16[256,768]{1,0:T(8,128)(2,1)S(1)} %bitcast.11), channel_id=1, source_target_pairs={{0,2},{1,3},{4,6},{5,7},{8,10},{9,11},{12,14},{13,15},{16,18},{17,... | collective-permute-start | bytes 1179656 | tf_op jit(solution)/shard_map/ppermute | solution.py:661
  21.7 7.6 %collective-permute-done = bf16[4,128,128]{2,1,0:T(8,128)(2,1)S(1)} collective-permute-done((bf16[4,128,128]{2,1,0:T(8,128)(2,1)S(1)}, bf16[4,128,128]{2,1,0:T(8,128)(2,1)S(1)}, u32[]{:S(2)}, u32[]{:S(2)}) %collective-permute-start) | collective-permute-done | bytes 131104 | tf_op jit(solution)/shard_map/ppermute | solution.py:627
  32.9 6.2 %collective-permute-done.1 = bf16[8,128,128]{2,1,0:T(8,128)(2,1)S(1)} collective-permute-done((bf16[8,128,128]{2,1,0:T(8,128)(2,1)S(1)}, bf16[8,128,128]{2,1,0:T(8,128)(2,1)S(1)}, u32[]{:S(2)}, u32[]{:S(2)}) %collective-permute-start.1) | collective-permute-done | bytes 262176 | tf_op jit(solution)/shard_map/ppermute | solution.py:627
  41.8 3.5 %collective-permute-done.9 = bf16[8,128,128]{2,1,0:T(8,128)(2,1)S(1)} collective-permute-done((bf16[8,128,128]{2,1,0:T(8,128)(2,1)S(1)}, bf16[8,128,128]{2,1,0:T(8,128)(2,1)S(1)}, u32[]{:S(2)}, u32[]{:S(2)}) %collective-permute-start.9) | collective-permute-done | bytes 262176 | tf_op jit(solution)/shard_map/ppermute | solution.py:627
  47.2 8.0 %collective-permute-done.4 = bf16[16,128,128]{2,1,0:T(8,128)(2,1)S(1)} collective-permute-done((bf16[16,128,128]{2,1,0:T(8,128)(2,1)S(1)}, bf16[16,128,128]{2,1,0:T(8,128)(2,1)S(1)}, u32[]{:S(2)}, u32[]{:S(2)}) %collective-permute-start.4) | collective-permute-done | bytes 524320 | tf_op jit(solution)/shard_map/ppermute | solution.py:627
  58.9 8.6 %collective-permute-done.16 = bf16[12,128,128]{2,1,0:T(8,128)(2,1)S(1)} collective-permute-done((bf16[12,128,128]{2,1,0:T(8,128)(2,1)S(1)}, bf16[12,128,128]{2,1,0:T(8,128)(2,1)S(1)}, u32[]{:S(2)}, u32[]{:S(2)}) %collective-permute-start.16) | collective-permute-done | bytes 393248 | tf_op jit(solution)/shard_map/ppermute | solution.py:627
  68.2 25.2 %collective-permute-done.17.refs_19_ = bf16[24,128,128]{2,1,0:T(8,128)(2,1)} collective-permute-done((bf16[24,128,128]{2,1,0:T(8,128)(2,1)S(1)}, bf16[24,128,128]{2,1,0:T(8,128)(2,1)}, u32[]{:S(2)}, u32[]{:S(2)}) %collective-permute-start.17) | collective-permute-done | bytes 786464 | tf_op jit(solution)/shard_map/ppermute | solution.py:627
  97.7 2.9 %collective-permute-done.19.refs_21_ = bf16[24,128,128]{2,1,0:T(8,128)(2,1)} collective-permute-done((bf16[24,128,128]{2,1,0:T(8,128)(2,1)}, bf16[24,128,128]{2,1,0:T(8,128)(2,1)}, u32[]{:S(2)}, u32[]{:S(2)}) %collective-permute-start.19) | collective-permute-done | bytes 786464 | tf_op jit(solution)/shard_map/ppermute | solution.py:627
  100.6 40.9 %layer.1 = (bf16[256,768]{1,0:T(8,128)(2,1)}, f32[256,768]{1,0:T(8,128)}, bf16[256,768]{1,0:T(8,128)(2,1)}, bf16[768,768]{1,0:T(8,128)(2,1)}, bf16[768,768]{1,0:...) custom-call(s32[448]{0:T(512)} %get-tuple-element.67.refs_0_, ...), custom_call_target="tpu_custom_call" | custom-call | tf_op jit(solution)/shard_map/layer/pallas_call | solution.py:693
  144.2 6.3 %qkv_grad.1 = (bf16[224,128,128]{2,1,0:T(8,128)(2,1)}, bf16[96,128,128]{2,1,0:T(8,128)(2,1)}, bf16[128,128,128]{2,1,0:T(8,128)(2,1)}) custom-call(s32[448]{0:T(512)} %get-tuple-element.68.refs_1_.dst, bf16[256,768]{1,0:T(8,128)(2,1)} %get-tuple-element.82.gq_h, ...), custom_call_target="tpu_custom_call", output_to_operand_aliasing={{0}: (5, {}), {1}: (6, {}), {2}: (7, {})} | custom-call | flops 2113929216 | bytes 8388608 | tf_op jit(solution)/shard_map/qkv_grad/pallas_call | solution.py:775
  151.2 4.8 %head_grad.1 = (bf16[256,128]{1,0:T(8,128)(2,1)}, bf16[768,128]{1,0:T(8,128)(2,1)}, bf16[224,128,128]{2,1,0:T(8,128)(2,1)}, bf16[96,128,128]{2,1,0:T(8,128)(2,1)}, bf16[128,128,128]{2,1,0:T(8,128)(2,1)}) custom-call(s32[448]{0:T(512)} %get-tuple-element.68.refs_1_.dst, ...), custom_call_target="tpu_custom_call", output_to_operand_aliasing={{2}: (10, {}), {3}: (11, {}), {4}: (12, {})} | custom-call | flops 1073741824 | bytes 4194304 | tf_op jit(solution)/shard_map/head_grad/pallas_call | solution.py:796
  157.2 5.5 %collective-permute-done.22 = bf16[96,128,128]{2,1,0:T(8,128)(2,1)S(1)} collective-permute-done((bf16[96,128,128]{2,1,0:T(8,128)(2,1)}, bf16[96,128,128]{2,1,0:T(8,128)(2,1)S(1)}, u32[]{:S(2)}, u32[]{:S(2)}) %collective-permute-start.22) | collective-permute-done | bytes 3145760 | tf_op jit(solution)/shard_map/ppermute | solution.py:627
  163.0 4.2 %add_convert_fusion = (bf16[48,128,128]{2,1,0:T(8,128)(2,1)S(1)}, bf16[48,128,128]{2,1,0:T(8,128)(2,1)}) fusion(bf16[96,128,128]{2,1,0:T(8,128)(2,1)S(1)} %collective-permute-done.22, bf16[224,128,128]{2,1,0:T(8,128)(2,1)} %get-tuple-element.93), kind=kLoop, calls=%fused_computation | loop fusion | flops 6291456 | bytes 9437184 | tf_op jit(solution)/shard_map/convert_element_type | solution.py:820
  170.0 4.0 %add_convert_fusion.3 = bf16[40,128,128]{2,1,0:T(8,128)(2,1)} fusion(bf16[128,128,128]{2,1,0:T(8,128)(2,1)S(1)} %collective-permute-done.23, bf16[224,128,128]{2,1,0:T(8,128)(2,1)} %get-tuple-element.93), kind=kLoop, calls=%fused_computation.3 | loop fusion | flops 2621440 | bytes 3932160 | tf_op jit(solution)/shard_map/convert_element_type | solution.py:820
  175.6 2.7 add_convert_fusion.6
  179.0 4.0 %pre_grad.1 = (bf16[256,768]{1,0:T(8,128)(2,1)S(1)}, bf16[256,768]{1,0:T(8,128)(2,1)S(1)}, f32[256,768]{1,0:T(8,128)S(1)}, f32[64,128]{1,0:T(8,128)}) custom-call(s32[1]{0:T(128)} %bitcast.6.row_at, bf16[768,768]{1,0:T(8,128)(2,1)S(1)} %copy-done.1, f32[8,768]{1,0:T(8,128)S(1)} %copy-done.21, bf16[256,128]{1,0:T(8,128)(2,1)S(1)} %copy-done.20, ...), custom_call_target="tpu_custom_call" | custom-call | flops 2113929216 | bytes 10485760 | tf_op jit(solution)/shard_map/pre_grad/pallas_call | solution.py:842
  186.1 12.3 %collective-permute-done.26 = bf16[24,128,128]{2,1,0:T(8,128)(2,1)} collective-permute-done((bf16[24,128,128]{2,1,0:T(8,128)(2,1)}, bf16[24,128,128]{2,1,0:T(8,128)(2,1)}, u32[]{:S(2)}, u32[]{:S(2)}) %collective-permute-start.26) | collective-permute-done | bytes 786464 | tf_op jit(solution)/shard_map/ppermute | solution.py:627
  205.8 2.8 %add_convert_fusion.8 = (bf16[20,128,128]{2,1,0:T(8,128)(2,1)}, bf16[20,128,128]{2,1,0:T(8,128)(2,1)}) fusion(bf16[40,128,128]{2,1,0:T(8,128)(2,1)S(1)} %add_convert_fusion.2, bf16[40,128,128]{2,1,0:T(8,128)(2,1)} %collective-permute-done.25), kind=kLoop, calls=%fused_computation.8 | loop fusion | flops 2621440 | bytes 3932160 | tf_op jit(solution)/shard_map/convert_element_type | solution.py:820
  209.0 2.7 add_convert_fusion.4
  216.3 4.8 %collective-permute-done.29 = bf16[12,128,128]{2,1,0:T(8,128)(2,1)} collective-permute-done((bf16[12,128,128]{2,1,0:T(8,128)(2,1)}, bf16[12,128,128]{2,1,0:T(8,128)(2,1)}, u32[]{:S(2)}, u32[]{:S(2)}) %collective-permute-start.29) | collective-permute-done | bytes 393248 | tf_op jit(solution)/shard_map/ppermute | solution.py:627
  222.4 2.7 collective-permute-start.34
  225.1 9.8 %collective-permute-done.28 = bf16[20,128,128]{2,1,0:T(8,128)(2,1)} collective-permute-done((bf16[20,128,128]{2,1,0:T(8,128)(2,1)}, bf16[20,128,128]{2,1,0:T(8,128)(2,1)}, u32[]{:S(2)}, u32[]{:S(2)}) %collective-permute-start.28) | collective-permute-done | bytes 655392 | tf_op jit(solution)/shard_map/ppermute | solution.py:627
  248.1 7.3 %collective-permute-done.32 = bf16[12,128,128]{2,1,0:T(8,128)(2,1)S(1)} collective-permute-done((bf16[12,128,128]{2,1,0:T(8,128)(2,1)S(1)}, bf16[12,128,128]{2,1,0:T(8,128)(2,1)S(1)}, u32[]{:S(2)}, u32[]{:S(2)}) %collective-permute-start.32) | collective-permute-done | bytes 393248 | tf_op jit(solution)/shard_map/ppermute | solution.py:627
  264.9 4.4 %adam.1 = (f32[14,128,128]{2,1,0:T(8,128)}, f32[14,128,128]{2,1,0:T(8,128)}, f32[14,128,128]{2,1,0:T(8,128)}) custom-call(bf16[6,128,128]{2,1,0:T(8,128)(2,1)S(1)} %get-tuple-element.121.refs_0_, bf16[6,128,128]{2,1,0:T(8,128)(2,1)} %collective-permute-done.35.refs_1_, bf16[5,128,128]{2,1,0:T(8,128)(2,1)S(1)} %get-tuple-element.146.refs_2_, ...), custom_call_target="tpu_custom_call" | custom-call | tf_op jit(solution)/shard_map/adam/pallas_call | solution.py:888
  (178 shorter events, 73.9 us)
Async XLA Ops:
  7.2 93.4 %all-gather.4.cloned.1.call-start = ((), (), s32[]{:S(2)}) async-start(), calls=%async_computation | async-start | bytes 3244032 | tf_op jit(solution)/shard_map/all_gather | solution.py:673
  9.2 247.0 %all-gather.6.cloned.1.call-start = ((), (), s32[]{:S(2)}) async-start(), calls=%async_computation.1 | async-start | bytes 1081344 | tf_op jit(solution)/shard_map/all_gather | solution.py:865
  9.3 29.9 %collective-permute-start.2 = (bf16[256,768]{1,0:T(8,128)(2,1)S(1)}, bf16[256,768]{1,0:T(8,128)(2,1)S(1)}, u32[]{:S(2)}, u32[]{:S(2)}) collective-permute-start(bf16[256,768]{1,0:T(8,128)(2,1)S(1)} %bitcast.11), channel_id=1, source_target_pairs={{0,2},{1,3},{4,6},{5,7},{8,10},{9,11},{12,14},{13,15},{16,18},{17,... | collective-permute-start | bytes 1179656 | tf_op jit(solution)/shard_map/ppermute | solution.py:661
  14.2 25.0 %collective-permute-start.3 = (bf16[256,768]{1,0:T(8,128)(2,1)S(1)}, bf16[256,768]{1,0:T(8,128)(2,1)S(1)}, u32[]{:S(2)}, u32[]{:S(2)}) collective-permute-start(bf16[256,768]{1,0:T(8,128)(2,1)S(1)} %bitcast.12), channel_id=1, source_target_pairs={{0,1},{1,2},{2,3},{4,5},{5,6},{6,7},{8,9},{9,10},{10,11},{12,13},{... | collective-permute-start | bytes 1179656 | tf_op jit(solution)/shard_map/ppermute | solution.py:661
  30.7 14.7 %collective-permute-start.15 = (bf16[6,128,128]{2,1,0:T(8,128)(2,1)S(1)}, bf16[6,128,128]{2,1,0:T(8,128)(2,1)S(1)}, u32[]{:S(2)}, u32[]{:S(2)}) collective-permute-start(bf16[6,128,128]{2,1,0:T(8,128)(2,1)S(1)} %pad_maximum_fusion.8), channel_id=1, source_target_pairs={{0,2},{1,3},{2,0},{3,1},{4,6},{5,7},{6,4},{7,5},{8,10},{9,11},{10,... | collective-permute-start | bytes 589832 | tf_op jit(solution)/shard_map/ppermute | solution.py:627
  40.3 14.9 %collective-permute-start.4 = (bf16[16,128,128]{2,1,0:T(8,128)(2,1)S(1)}, bf16[16,128,128]{2,1,0:T(8,128)(2,1)S(1)}, u32[]{:S(2)}, u32[]{:S(2)}) collective-permute-start(bf16[16,128,128]{2,1,0:T(8,128)(2,1)S(1)} %pad_maximum_fusion.3), channel_id=1, source_target_pairs={{0,4},{1,5},{2,6},{3,7},{4,0},{5,1},{6,2},{7,3},{8,12},{9,13},{10,... | collective-permute-start | bytes 1572872 | tf_op jit(solution)/shard_map/ppermute | solution.py:627
  45.5 22.0 %collective-permute-start.16 = (bf16[12,128,128]{2,1,0:T(8,128)(2,1)S(1)}, bf16[12,128,128]{2,1,0:T(8,128)(2,1)S(1)}, u32[]{:S(2)}, u32[]{:S(2)}) collective-permute-start(bf16[12,128,128]{2,1,0:T(8,128)(2,1)S(1)} %pad_maximum_fusion.5), channel_id=1, source_target_pairs={{0,16},{1,17},{2,18},{3,19},{4,20},{5,21},{6,22},{7,23},{8,24},{9,... | collective-permute-start | bytes 1179656 | tf_op jit(solution)/shard_map/ppermute | solution.py:627
  55.4 38.1 %collective-permute-start.5 = (bf16[32,128,128]{2,1,0:T(8,128)(2,1)S(1)}, bf16[32,128,128]{2,1,0:T(8,128)(2,1)}, u32[]{:S(2)}, u32[]{:S(2)}) collective-permute-start(bf16[32,128,128]{2,1,0:T(8,128)(2,1)S(1)} %constant_dynamic-update-slice_fusion.refs_10_), channel_id=1, source_target_pairs={{0,2},{1,3},{2,0},{3,1},{4,6},{5,7},{6,4},{7,5},{8,10},{9,11},{10,... | collective-permute-start | bytes 3145736 | tf_op jit(solution)/shard_map/ppermute | solution.py:627
  57.6 36.3 %collective-permute-start.11 = (bf16[32,128,128]{2,1,0:T(8,128)(2,1)S(1)}, bf16[32,128,128]{2,1,0:T(8,128)(2,1)}, u32[]{:S(2)}, u32[]{:S(2)}) collective-permute-start(bf16[32,128,128]{2,1,0:T(8,128)(2,1)S(1)} %pad_maximum_fusion.1.refs_14_), channel_id=1, source_target_pairs={{0,4},{1,5},{2,6},{3,7},{4,0},{5,1},{6,2},{7,3},{8,12},{9,13},{10,... | collective-permute-start | bytes 3145736 | tf_op jit(solution)/shard_map/ppermute | solution.py:627
  67.5 25.9 %collective-permute-start.17 = (bf16[24,128,128]{2,1,0:T(8,128)(2,1)S(1)}, bf16[24,128,128]{2,1,0:T(8,128)(2,1)}, u32[]{:S(2)}, u32[]{:S(2)}) collective-permute-start(bf16[24,128,128]{2,1,0:T(8,128)(2,1)S(1)} %pad_maximum_fusion.2.refs_18_), channel_id=1, source_target_pairs={{0,8},{1,9},{2,10},{3,11},{4,12},{5,13},{6,14},{7,15},{8,0},{9,1},... | collective-permute-start | bytes 2359304 | tf_op jit(solution)/shard_map/ppermute | solution.py:627
  67.7 26.3 %collective-permute-start.18 = (bf16[24,128,128]{2,1,0:T(8,128)(2,1)S(1)}, bf16[24,128,128]{2,1,0:T(8,128)(2,1)S(1)}, u32[]{:S(2)}, u32[]{:S(2)}) collective-permute-start(bf16[24,128,128]{2,1,0:T(8,128)(2,1)S(1)} %pad_maximum_fusion.2.refs_18_), channel_id=1, source_target_pairs={{0,1},{1,0},{2,3},{3,2},{4,5},{5,4},{6,7},{7,6},{8,9},{9,8},{10,11... | collective-permute-start | bytes 2359304 | tf_op jit(solution)/shard_map/ppermute | solution.py:627
  67.7 29.2 %collective-permute-start.6 = (bf16[32,128,128]{2,1,0:T(8,128)(2,1)S(1)}, bf16[32,128,128]{2,1,0:T(8,128)(2,1)}, u32[]{:S(2)}, u32[]{:S(2)}) collective-permute-start(bf16[32,128,128]{2,1,0:T(8,128)(2,1)S(1)} %constant_dynamic-update-slice_fusion.refs_10_), channel_id=1, source_target_pairs={{0,1},{1,0},{2,3},{3,2},{4,5},{5,4},{6,7},{7,6},{8,9},{9,8},{10,11... | collective-permute-start | bytes 3145736 | tf_op jit(solution)/shard_map/ppermute | solution.py:627
  167.3 41.7 %collective-permute-start.24 = (bf16[48,128,128]{2,1,0:T(8,128)(2,1)}, bf16[48,128,128]{2,1,0:T(8,128)(2,1)}, u32[]{:S(2)}, u32[]{:S(2)}) collective-permute-start(bf16[48,128,128]{2,1,0:T(8,128)(2,1)} %get-tuple-element.131), channel_id=1, source_target_pairs={{0,2},{1,3},{2,0},{3,1},{4,6},{5,7},{6,4},{7,5},{8,10},{9,11},{10,... | collective-permute-start | bytes 4718600 | tf_op jit(solution)/shard_map/ppermute | solution.py:627
  174.1 31.7 %collective-permute-start.25 = (bf16[40,128,128]{2,1,0:T(8,128)(2,1)}, bf16[40,128,128]{2,1,0:T(8,128)(2,1)}, u32[]{:S(2)}, u32[]{:S(2)}) collective-permute-start(bf16[40,128,128]{2,1,0:T(8,128)(2,1)} %add_convert_fusion.3), channel_id=1, source_target_pairs={{0,4},{1,5},{2,6},{3,7},{4,0},{5,1},{6,2},{7,3},{8,12},{9,13},{10,... | collective-permute-start | bytes 3932168 | tf_op jit(solution)/shard_map/ppermute | solution.py:627
  178.3 20.1 %collective-permute-start.26 = (bf16[24,128,128]{2,1,0:T(8,128)(2,1)}, bf16[24,128,128]{2,1,0:T(8,128)(2,1)}, u32[]{:S(2)}, u32[]{:S(2)}) collective-permute-start(bf16[24,128,128]{2,1,0:T(8,128)(2,1)} %get-tuple-element.129), channel_id=1, source_target_pairs={{0,8},{1,9},{2,10},{3,11},{4,12},{5,13},{6,14},{7,15},{8,0},{9,1},... | collective-permute-start | bytes 2359304 | tf_op jit(solution)/shard_map/ppermute | solution.py:627
  200.7 20.4 %collective-permute-start.29 = (bf16[12,128,128]{2,1,0:T(8,128)(2,1)}, bf16[12,128,128]{2,1,0:T(8,128)(2,1)}, u32[]{:S(2)}, u32[]{:S(2)}) collective-permute-start(bf16[12,128,128]{2,1,0:T(8,128)(2,1)} %get-tuple-element.139), channel_id=1, source_target_pairs={{0,16},{1,17},{2,18},{3,19},{4,20},{5,21},{6,22},{7,23},{8,24},{9,... | collective-permute-start | bytes 1179656 | tf_op jit(solution)/shard_map/ppermute | solution.py:627
  208.6 26.3 %collective-permute-start.28 = (bf16[20,128,128]{2,1,0:T(8,128)(2,1)}, bf16[20,128,128]{2,1,0:T(8,128)(2,1)}, u32[]{:S(2)}, u32[]{:S(2)}) collective-permute-start(bf16[20,128,128]{2,1,0:T(8,128)(2,1)} %get-tuple-element.135), channel_id=1, source_target_pairs={{0,8},{1,9},{2,10},{3,11},{4,12},{5,13},{6,14},{7,15},{8,0},{9,1},... | collective-permute-start | bytes 1966088 | tf_op jit(solution)/shard_map/ppermute | solution.py:627
  211.7 28.4 %collective-permute-start.27 = (bf16[24,128,128]{2,1,0:T(8,128)(2,1)}, bf16[24,128,128]{2,1,0:T(8,128)(2,1)}, u32[]{:S(2)}, u32[]{:S(2)}) collective-permute-start(bf16[24,128,128]{2,1,0:T(8,128)(2,1)} %get-tuple-element.132), channel_id=1, source_target_pairs={{0,4},{1,5},{2,6},{3,7},{4,0},{5,1},{6,2},{7,3},{8,12},{9,13},{10,... | collective-permute-start | bytes 2359304 | tf_op jit(solution)/shard_map/ppermute | solution.py:627
  213.5 25.2 %collective-permute-start.31 = (bf16[256,768]{1,0:T(8,128)(2,1)S(1)}, bf16[256,768]{1,0:T(8,128)(2,1)S(1)}, u32[]{:S(2)}, u32[]{:S(2)}) collective-permute-start(bf16[256,768]{1,0:T(8,128)(2,1)S(1)} %get-tuple-element.112), channel_id=1, source_target_pairs={{1,0},{2,1},{3,2},{5,4},{6,5},{7,6},{9,8},{10,9},{11,10},{13,12},{... | collective-permute-start | bytes 1179656 | tf_op jit(solution)/shard_map/ppermute | solution.py:877
  214.8 24.6 %collective-permute-start.30 = (bf16[256,768]{1,0:T(8,128)(2,1)S(1)}, bf16[256,768]{1,0:T(8,128)(2,1)S(1)}, u32[]{:S(2)}, u32[]{:S(2)}) collective-permute-start(bf16[256,768]{1,0:T(8,128)(2,1)S(1)} %get-tuple-element.110), channel_id=1, source_target_pairs={{2,0},{3,1},{6,4},{7,5},{10,8},{11,9},{14,12},{15,13},{18,16},{19,... | collective-permute-start | bytes 1179656 | tf_op jit(solution)/shard_map/ppermute | solution.py:876
  222.4 19.1 %collective-permute-start.34 = (bf16[6,128,128]{2,1,0:T(8,128)(2,1)S(1)}, bf16[6,128,128]{2,1,0:T(8,128)(2,1)S(1)}, u32[]{:S(2)}, u32[]{:S(2)}) collective-permute-start(bf16[6,128,128]{2,1,0:T(8,128)(2,1)S(1)} %get-tuple-element.145), channel_id=1, source_target_pairs={{0,2},{1,3},{2,0},{3,1},{4,6},{5,7},{6,4},{7,5},{8,10},{9,11},{10,... | collective-permute-start | bytes 589832 | tf_op jit(solution)/shard_map/ppermute | solution.py:627
  241.5 14.0 %collective-permute-start.32 = (bf16[12,128,128]{2,1,0:T(8,128)(2,1)S(1)}, bf16[12,128,128]{2,1,0:T(8,128)(2,1)S(1)}, u32[]{:S(2)}, u32[]{:S(2)}) collective-permute-start(bf16[12,128,128]{2,1,0:T(8,128)(2,1)S(1)} %get-tuple-element.136), channel_id=1, source_target_pairs={{0,8},{1,9},{2,10},{3,11},{4,12},{5,13},{6,14},{7,15},{8,0},{9,1},... | collective-permute-start | bytes 1179656 | tf_op jit(solution)/shard_map/ppermute | solution.py:627
  242.3 20.9 %collective-permute-start.37 = (bf16[3,128,128]{2,1,0:T(8,128)(2,1)}, bf16[3,128,128]{2,1,0:T(8,128)(2,1)}, u32[]{:S(2)}, u32[]{:S(2)}) collective-permute-start(bf16[3,128,128]{2,1,0:T(8,128)(2,1)} %get-tuple-element.153), channel_id=1, source_target_pairs={{0,4},{1,5},{2,6},{3,7},{4,0},{5,1},{6,2},{7,3},{8,12},{9,13},{10,... | collective-permute-start | bytes 294920 | tf_op jit(solution)/shard_map/ppermute | solution.py:627
  245.9 17.3 %collective-permute-start.36 = (bf16[5,128,128]{2,1,0:T(8,128)(2,1)}, bf16[5,128,128]{2,1,0:T(8,128)(2,1)}, u32[]{:S(2)}, u32[]{:S(2)}) collective-permute-start(bf16[5,128,128]{2,1,0:T(8,128)(2,1)} %get-tuple-element.147), channel_id=1, source_target_pairs={{0,16},{1,17},{2,18},{3,19},{4,20},{5,21},{6,22},{7,23},{8,24},{9,... | collective-permute-start | bytes 491528 | tf_op jit(solution)/shard_map/ppermute | solution.py:627
  (52 other events, 475.3 us)
Sparse Core Ops, SparseCore 0:
  11.5 76.9 all-gather.3
  184.1 64.2 all-gather.5
